TPU v7x, 32 devices: a whole 2x2x4 slice. The times are simulated.
32 devices in a mesh: dp: 8 (over y, x, core), tensor: 4 (over z).
Axes of the slice: x: 2, y: 2, z: 4, core: 2. Of those that a mesh axis runs over, the one named last changes fastest.
Arguments:
- tokens: bfloat16 [16384, 768], P(('dp', 'tensor')), may hold values from -6 to 6
- page_lengths: int32 [32], P('dp'), may hold values from 64 to 512, as said below
- w_query: bfloat16 [768, 768], P(None, 'tensor'), may hold values from -0.21875 to 0.21875
- b_query: bfloat16 [768], P('tensor'), may hold values from -1.796875 to 1.796875
- w_key: bfloat16 [768, 768], P(None, 'tensor'), may hold values from -0.21875 to 0.21875
- w_value: bfloat16 [768, 768], P(None, 'tensor'), may hold values from -0.21875 to 0.21875
- b_value: bfloat16 [768], P('tensor'), may hold values from -1.796875 to 1.796875
- w_out: bfloat16 [768, 768], P('tensor'), may hold values from -3.5 to 3.5
- b_out: bfloat16 [768], replicated, may hold values from -1.796875 to 1.796875
- ln1_gain: bfloat16 [768], replicated, may hold values from 0.099609375 to 1.8984375
- ln1_bias: bfloat16 [768], replicated, may hold values from -1.796875 to 1.796875
- w_up: bfloat16 [768, 3072], P(None, 'tensor'), may hold values from -0.21875 to 0.21875
- b_up: bfloat16 [3072], P('tensor'), may hold values from -3 to 3
- w_down: bfloat16 [3072, 768], P('tensor'), may hold values from -0.109375 to 0.109375
- b_down: bfloat16 [768], replicated, may hold values from -1.796875 to 1.796875
- ln2_gain: bfloat16 [768], replicated, may hold values from 0.099609375 to 1.8984375
- ln2_bias: bfloat16 [768], replicated, may hold values from -1.796875 to 1.796875
- cotangent: bfloat16 [16384, 768], P(('dp', 'tensor')), may hold values from -6 to 6
Outputs:
- output: bfloat16 [16384, 768], P(('dp', 'tensor'))
- grad_tokens: bfloat16 [16384, 768], P(('dp', 'tensor'))
- grad_w_query: float32 [768, 768], P(None, 'tensor')
- grad_b_query: float32 [768], P('tensor')
- grad_w_key: float32 [768, 768], P(None, 'tensor')
- grad_w_value: float32 [768, 768], P(None, 'tensor')
- grad_b_value: float32 [768], P('tensor')
- grad_w_out: float32 [768, 768], P('tensor')
- grad_b_out: float32 [768], replicated
- grad_ln1_gain: float32 [768], replicated
- grad_ln1_bias: float32 [768], replicated
- grad_w_up: float32 [768, 3072], P(None, 'tensor')
- grad_b_up: float32 [3072], P('tensor')
- grad_w_down: float32 [3072, 768], P('tensor')
- grad_b_down: float32 [768], replicated
- grad_ln2_gain: float32 [768], replicated
- grad_ln2_bias: float32 [768], replicated
Inputs may be any that keep to these rules, and one draw needn't show every extreme that they name: `page_lengths`: the number of real tokens of page p; the keys of a page at positions from its length on are padding.
All inputs are finite; a program needn't handle non-finite values.
Results may differ from a plain program's by a relative error of at most 0.023.
Values may be sent and summed in bfloat16 or wider, within the bound.
No kernel may reach another device: no remote copies, remote signals or barrier semaphores. Data moves between devices by JAX's collectives and lax.ppermute only.
A program may use at most 128 MiB of HBM per device.

v0:
```python
from functools import partial

import jax
import jax.numpy as jnp
from jax import lax
from jax.experimental import pallas as pl
from jax.experimental.pallas import tpu as pltpu
from jax.sharding import PartitionSpec as P

HD = 64
SEQ = 512
GROUP = 8
LOG2E = 1.4426950408889634
TAIL_P = 0.39
TAIL = (
    0.23532521908406087,
    0.09138841455460205,
    0.6495593986198918,
    -0.6354002786931026,
    0.8866643698688825,
    -0.22753712513305413,
)

epsilon = 1e-12
masked_score = -1000000000.0
low = jnp.bfloat16
wide = jnp.float32
PEAK = 1.1e15
LIMIT = 12


def mm(left, right, left_dim, right_dim):
    return lax.dot_general(
        left, right, (((left_dim,), (right_dim,)), ((), ())), preferred_element_type=wide
    )


def vmem():
    return pl.BlockSpec(memory_space=pltpu.VMEM)


def smem():
    return pl.BlockSpec(memory_space=pltpu.SMEM)


def hbm():
    return pl.BlockSpec(memory_space=pl.ANY)


def cost(microseconds):
    return pl.CostEstimate(
        flops=int(microseconds * 1e-6 * PEAK), bytes_accessed=1 << 20, transcendentals=0
    )


def params(mebibytes=LIMIT):
    return pltpu.CompilerParams(vmem_limit_bytes=mebibytes << 20)


def shaped(shape, dtype):
    return jax.ShapeDtypeStruct(shape, dtype)


def masked_pad(length, seq):
    row = lax.broadcasted_iota(jnp.int32, (16, seq), 0)
    key = lax.broadcasted_iota(jnp.int32, (16, seq), 1)
    bias = jnp.where((row == 0) & (key >= length), masked_score, 0.0).astype(low)
    ones = jnp.where(row == 0, 1.0, 0.0).astype(low)
    return bias, ones


def as_column(row, ones):
    first = lax.broadcasted_iota(jnp.int32, (16, row.shape[1]), 0) == 0
    return mm(jnp.where(first, row, 0.0).astype(low), ones, 0, 0)


def group_forward(tokens, weights, bias, length, qkv_ref, ctx_ref, lse_ref):
    local = weights[0].shape[0]
    seq = tokens.shape[0]
    scale = HD**-0.5 * LOG2E
    key_pad, ones = masked_pad(length, seq)
    query = (mm(weights[0], tokens, 1, 1) + as_column(bias[:, :local], ones)).astype(low)
    key = mm(weights[1], tokens, 1, 1).astype(low)
    value = mm(weights[2], tokens, 1, 1) + as_column(bias[:, local : 2 * local], ones)
    value = value.astype(low)
    qkv_ref[:local] = query
    qkv_ref[local : 2 * local] = key
    qkv_ref[2 * local :] = value
    for h in range(local // HD):
        part = slice(h * HD, (h + 1) * HD)
        scores = mm(
            jnp.concatenate([key[part], key_pad], 0), jnp.concatenate([query[part], ones], 0), 0, 0
        )
        top = jnp.max(scores, axis=0, keepdims=True)
        probs = jnp.exp2((scores - top) * scale)
        total = jnp.sum(probs, axis=0, keepdims=True)
        context = mm(value[part], probs.astype(low), 1, 0)
        ctx_ref[part] = (context * (1.0 / total)).astype(low)
        lse_ref[h : h + 1] = top * scale + jnp.log2(total)


def gelu_parts(x):
    t = 1.0 / (1.0 + (TAIL_P * 0.5**0.5) * jnp.abs(x))
    poly = TAIL[-1]
    for factor in TAIL[-2::-1]:
        poly = poly * t + factor
    bell = jnp.exp2(x * x * (-0.5 * LOG2E))
    half = 0.5 * poly * t * bell
    cdf = jnp.where(x >= 0, 1.0 - half, half)
    return x * cdf, cdf + x * bell * (0.5 / jnp.pi) ** 0.5


def norm_parts(values):
    centred = values - jnp.mean(values, axis=1, keepdims=True)
    inverse = lax.rsqrt(jnp.mean(centred * centred, axis=1, keepdims=True) + epsilon)
    return centred * inverse, inverse


def norm_back(scaled, normal, inverse):
    return inverse * (
        scaled
        - jnp.mean(scaled, axis=1, keepdims=True)
        - normal * jnp.mean(scaled * normal, axis=1, keepdims=True)
    )


def assemble(info, refs, target, own=None):
    if own is not None:
        target[0] = own[...]
    skip = 1 if own is None else 0
    for s in range(2):
        first, second, third = refs[3 * s : 3 * s + 3]
        holder = info[1] ^ s
        order = (1 + holder, 2 - holder, 3)
        views = (first, second, third.at[0], third.at[1])
        for view, move in zip(views, (0,) + order):
            rows = view.shape[1]
            start = pl.multiple_of((holder * 4 + (info[2] ^ move)) * rows, rows)
            for entry, k in enumerate(order):
                target[k - skip, pl.ds(start, rows), :] = view[entry]


def place_pieces(info, scratch, keep_ref, send_ref, entry):
    rows = scratch.shape[0] // GROUP
    for s, target in enumerate((keep_ref, send_ref)):
        half = info[1] ^ s
        for q in range(4):
            move = info[2] ^ q
            x_bit, y_bit = move & 1, move >> 1
            a = jnp.where(half == 0, x_bit, y_bit)
            start = pl.multiple_of((half * 4 + q) * rows, rows)
            target[a, x_bit + y_bit - a, entry] = scratch[pl.ds(start, rows), :]


def attn_own_kernel(info, tokens, w_query, w_key, w_value, bias, qkv, ctx, lse):
    weights = (w_query[...], w_key[...], w_value[...])
    group_forward(tokens[...], weights, bias[0], info[0], qkv.at[0], ctx.at[0], lse.at[0])


def attn_own(info, tokens, weights, bias):
    local, seq = weights[0].shape[0], tokens.shape[0]
    return pl.pallas_call(
        attn_own_kernel,
        in_specs=[smem()] + [vmem()] * 5,
        out_specs=[vmem()] * 3,
        out_shape=[
            shaped((1, 3 * local, seq), low),
            shaped((1, local, seq), low),
            shaped((1, 8, seq), wide),
        ],
        compiler_params=params(),
        cost_estimate=cost(4),
        name="attn_own",
    )(info, tokens, *weights, bias)


def attn_rest_kernel(info, tokens, bias, *refs):
    qkv_out, whole, ctx, lse, out_w, weights, qkv, sems = refs[6:]
    others, local = ctx.shape[:2]
    assemble(info, refs[:6], weights)
    sent = [pltpu.make_async_copy(weights, whole, sems.at[others])]
    sent[0].start()
    out_w[...] = weights[:, 3 * local :]

    def group(k, _):
        joint = tuple(weights[k, i * local : (i + 1) * local] for i in range(3))
        group_forward(
            tokens[...], joint, bias[k + 1], info[0], qkv.at[k], ctx.at[k], lse.at[k]
        )
        pltpu.make_async_copy(qkv.at[k], qkv_out.at[k], sems.at[k]).start()
        return 0

    lax.fori_loop(0, others, group, 0)
    sent += [pltpu.make_async_copy(qkv.at[k], qkv_out.at[k], sems.at[k]) for k in range(others)]
    for copy in sent:
        copy.wait()


def attn_rest(info, tokens, bias, pieces):
    others, rows, cols = pieces[0].shape
    size, seq = rows * GROUP, tokens.shape[0]
    local = size // 4
    joint, whole = (others, 3 * local, seq), (others, size, cols)
    return pl.pallas_call(
        attn_rest_kernel,
        in_specs=[smem()] + [vmem()] * 8,
        out_specs=[pl.BlockSpec(memory_space=pltpu.HBM)] * 2 + [vmem()] * 3,
        out_shape=[
            shaped(joint, low),
            shaped(whole, low),
            shaped((others, local, seq), low),
            shaped((others, 8, seq), wide),
            shaped((others, local, cols), low),
        ],
        scratch_shapes=[
            pltpu.VMEM(whole, low),
            pltpu.VMEM(joint, low),
            pltpu.SemaphoreType.DMA((others + 1,)),
        ],
        compiler_params=params(),
        cost_estimate=cost(8),
        name="attn_rest",
    )(info, tokens, bias, *pieces)


def ffn_in_kernel(tokens, ctx_own, ctx_rest, vec, out_own, out_rest, skip, normed_ref, hat_ref, inv_ref):
    others = ctx_rest.shape[0]
    rows = vec[...]
    b_out, gain_one, bias_one, b_down = (rows[i : i + 1] for i in range(4))
    attended = mm(ctx_own[0], out_own[...], 0, 0)
    for k in range(others):
        attended = attended + mm(ctx_rest[k], out_rest[k], 0, 0)
    hat, inv = norm_parts(tokens[...].astype(wide) + attended + b_out)
    hat_ref[...] = hat
    inv_ref[...] = jnp.broadcast_to(inv, inv_ref.shape)
    normed = hat * gain_one + bias_one
    normed_ref[...] = normed.astype(low)
    skip[...] = normed + b_down


def ffn_in(tokens, ctx_own, ctx_rest, vec, out_own, out_rest):
    seq, width = tokens.shape
    others, local = ctx_rest.shape[:2]
    return pl.pallas_call(
        ffn_in_kernel,
        in_specs=[vmem()] * 6,
        out_specs=[vmem()] * 4,
        out_shape=[
            shaped((seq, width), wide),
            shaped((seq, width), low),
            shaped((seq, width), wide),
            shaped((seq, 128), wide),
        ],
        compiler_params=params(),
        cost_estimate=cost(5),
        name="ffn_in",
    )(tokens, ctx_own, ctx_rest, vec, out_own, out_rest)


def ffn_up_kernel(info, normed, bias, up_own, *refs):
    _, act, slope, up, mark = refs[6:]
    size = up.shape[2]
    first = bias.shape[2] - size
    mark[...] = jnp.zeros(mark.shape, wide)
    assemble(info, refs[:6], up, up_own)

    def forward(k, _):
        preact = mm(normed[...], up[k], 1, 0) + bias[k][:, first:].astype(wide)
        value, derivative = gelu_parts(preact)
        act[k] = value.astype(low)
        slope[k] = derivative.astype(low)
        return 0

    lax.fori_loop(0, act.shape[0], forward, 0)


def ffn_up(info, normed, bias, up_own, pieces, mark):
    seq, width = normed.shape
    others, size = pieces[0].shape[0], up_own.shape[1]
    return pl.pallas_call(
        ffn_up_kernel,
        in_specs=[smem()] + [vmem()] * (3 + 6) + [hbm()],
        out_specs=[vmem()] * 4,
        out_shape=[
            shaped((others + 1, seq, size), low),
            shaped((others + 1, seq, size), low),
            shaped((others + 1, width, size), low),
            shaped((8, 128), wide),
        ],
        compiler_params=params(),
        cost_estimate=cost(11),
        name="ffn_up",
    )(info, normed, bias, up_own, *pieces, mark)


def ffn_down_kernel(info, skip, vec, cot, act, down_own, *refs):
    _, out, grad_ref, branch_ref, small, keep, send, down, scratch = refs[6:]
    parts = act.shape[0]
    assemble(info, refs[:6], down, down_own)
    grad_ref[...] = skip[...]

    def branch(k, _):
        grad_ref[...] += mm(act[k], down[k], 1, 0)
        return 0

    lax.fori_loop(0, parts, branch, 0)
    total = grad_ref[...]
    gain_two, bias_two = vec[4:5], vec[5:6]
    hat_two, inv_two = norm_parts(total)
    out[...] = (hat_two * gain_two + bias_two).astype(low)
    grad = cot[...].astype(wide)
    grad_branch = norm_back(grad * gain_two, hat_two, inv_two)
    grad_ref[...] = grad_branch
    branch_low = grad_branch.astype(low)
    branch_ref[...] = branch_low
    small[...] = jnp.zeros(small.shape, wide)
    small[3:4] = jnp.sum(grad_branch, axis=0, keepdims=True)
    small[4:5] = jnp.sum(grad * hat_two, axis=0, keepdims=True)
    small[5:6] = jnp.sum(grad, axis=0, keepdims=True)

    def weight(k, _):
        scratch[...] = mm(act[k], branch_ref[...], 0, 0).astype(low)
        place_pieces(info, scratch, keep, send, k)
        return 0

    lax.fori_loop(0, parts, weight, 0)


def halves_shape(entries, rows, cols):
    return (2, 2, entries, rows // GROUP, cols)


def ffn_down(info, act, skip, vec, cot, down_own, pieces, mark):
    parts, seq, size = act.shape
    width = skip.shape[1]
    half = halves_shape(parts, size, width)
    return pl.pallas_call(
        ffn_down_kernel,
        in_specs=[smem()] + [vmem()] * (5 + 6) + [hbm()],
        out_specs=[vmem()] * 7,
        out_shape=[
            shaped((seq, width), low),
            shaped((seq, width), wide),
            shaped((seq, width), low),
            shaped((16, width), wide),
            shaped(half, low),
            shaped(half, low),
            shaped((parts, size, width), low),
        ],
        scratch_shapes=[pltpu.VMEM((size, width), low)],
        compiler_params=params(),
        cost_estimate=cost(12),
        name="ffn_down",
    )(info, skip, vec, cot, act, down_own, *pieces, mark)


def ffn_back_kernel(
    info, branch_low, grad_branch, normed_low, hat_ref, inv_ref, vec, small_in, slope, up, down,
    grad_ref, residual_ref, small, keep, send, turned, total, scratch,
):
    parts = slope.shape[0]
    index = lax.broadcasted_iota(jnp.int32, small.shape, 0)
    small[...] = small_in[...]
    total[...] = grad_branch[...]
    turned[...] = normed_low[...].T

    def backward(k, _):
        grad_pre = mm(branch_low[...], down[k], 1, 1) * slope[k].astype(wide)
        grad_pre = grad_pre.astype(low)
        sums = jnp.sum(grad_pre.astype(wide), axis=0, keepdims=True)
        small[...] = jnp.where(index == 6 + (info[3] ^ k), sums, small[...])
        scratch[...] = mm(turned[...], grad_pre, 1, 0).astype(low)
        place_pieces(info, scratch, keep, send, k)
        total[...] += mm(grad_pre, up[k], 1, 1)
        return 0

    lax.fori_loop(0, parts, backward, 0)
    grad_normed = total[...]
    hat = hat_ref[...]
    grad_residual = norm_back(grad_normed * vec[1:2], hat, inv_ref[:, :1])
    grad_ref[...] = grad_residual
    residual_ref[...] = grad_residual.astype(low)
    small[0:1] = jnp.sum(grad_residual, axis=0, keepdims=True)
    small[1:2] = jnp.sum(grad_normed * hat, axis=0, keepdims=True)
    small[2:3] = jnp.sum(grad_normed, axis=0, keepdims=True)


def ffn_back(info, branch_low, grad_branch, slope, normed_low, hat, inv, vec, small, up, down):
    _, width, size = up.shape
    parts, seq = slope.shape[:2]
    half = halves_shape(parts, width, size)
    return pl.pallas_call(
        ffn_back_kernel,
        in_specs=[smem()] + [vmem()] * 10,
        out_specs=[vmem()] * 5,
        out_shape=[
            shaped((seq, width), wide),
            shaped((seq, width), low),
            shaped((16, width), wide),
            shaped(half, low),
            shaped(half, low),
        ],
        scratch_shapes=[
            pltpu.VMEM((width, seq), low),
            pltpu.VMEM((seq, width), wide),
            pltpu.VMEM((width, size), low),
        ],
        compiler_params=params(),
        cost_estimate=cost(11),
        name="ffn_back",
    )(info, branch_low, grad_branch, normed_low, hat, inv, vec, small, slope, up, down)


def attn_back_kernel(first, info, tokens, residual_low, small_in, *refs):
    groups = (refs[:4], refs[4:8])
    small, joint, keep, send, scratch = refs[8:]
    local = groups[0][2].shape[1]
    seq, width = tokens.shape
    scale = HD**-0.5
    index = lax.broadcasted_iota(jnp.int32, small.shape, 0)
    small[...] = small_in[...]
    key_pad, query_pad = masked_pad(info[0], seq)
    ones = jnp.ones((8, seq), low)
    for i, (out_w, qkv_ref, ctx_ref, lse_ref) in enumerate(groups):
        k = first + i
        out_rows = out_w[...] if k == 0 else out_w[k - 1]
        qkv, ctx, lse = (ref.at[max(k - 1, 0)] for ref in (qkv_ref, ctx_ref, lse_ref))
        grad_ctx = mm(out_rows, residual_low[...], 1, 1).astype(low)
        for h in range(local // HD):
            lo, hi = h * HD, (h + 1) * HD
            query = qkv[lo:hi]
            key = qkv[local + lo : local + hi]
            value = qkv[2 * local + lo : 2 * local + hi]
            grad_head = grad_ctx[lo:hi]
            scores = mm(
                jnp.concatenate([key, key_pad], 0), jnp.concatenate([query, query_pad], 0), 0, 0
            )
            probs = jnp.exp2(scores * (scale * LOG2E) - lse[h : h + 1])
            grad_probs = mm(value, grad_head, 0, 0)
            product = probs * grad_probs
            grad_scores = (product - probs * jnp.sum(product, axis=0, keepdims=True)).astype(low)
            joint[i, lo:hi] = (mm(key, grad_scores, 1, 0) * scale).astype(low)
            joint[i, local + lo : local + hi] = (mm(query, grad_scores, 1, 1) * scale).astype(low)
            joint[i, 2 * local + lo : 2 * local + hi] = mm(
                grad_head, probs.astype(low), 1, 1
            ).astype(low)
        grads = joint[i]
        sums = mm(ones, grads, 1, 1)[:1]
        gap = jnp.zeros((1, 256 - local), wide)
        rest = jnp.zeros((1, width - 512), wide)
        sums = jnp.concatenate([sums[:, :local], gap, sums[:, 2 * local :], gap, rest], 1)
        small[...] = jnp.where(index == 10 + (info[3] ^ (first + i)), sums, small[...])
        scratch[: 3 * local] = mm(grads, tokens[...], 1, 0).astype(low)
        scratch[3 * local :] = mm(ctx[...], residual_low[...], 1, 0).astype(low)
        place_pieces(info, scratch, keep, send, i)


def attn_back(first, info, tokens, residual_low, small, out_own, own, out_rest, rest):
    seq, width = tokens.shape
    local = out_own.shape[0]
    arrays = []
    for k in (first, first + 1):
        arrays += (out_own,) + tuple(own) if k == 0 else (out_rest,) + tuple(rest)
    half = halves_shape(2, 4 * local, width)
    return pl.pallas_call(
        partial(attn_back_kernel, first),
        in_specs=[smem()] + [vmem()] * 11,
        out_specs=[vmem()] * 4,
        out_shape=[
            shaped((16, width), wide),
            shaped((2, 3 * local, seq), low),
            shaped(half, low),
            shaped(half, low),
        ],
        scratch_shapes=[pltpu.VMEM((4 * local, width), low)],
        compiler_params=params(),
        cost_estimate=cost(9),
        name="attn_back",
    )(info, tokens, residual_low, small, *arrays)


def grad_tokens_kernel(grad, joint_a, joint_b, w_query, w_key, w_value, rest_w, out):
    local, rows = w_query.shape[0], joint_a.shape[1]
    total = grad[...]
    for i, weights in enumerate((w_query, w_key, w_value)):
        total = total + mm(joint_a[0, i * local : (i + 1) * local], weights[...], 0, 0)
    for k in range(1, 4):
        joint = joint_a[k] if k < 2 else joint_b[k - 2]
        total = total + mm(joint, rest_w[k - 1, :rows], 0, 0)
    out[...] = total.astype(low)


def grad_tokens_of(grad, joint_a, joint_b, weights, rest_w):
    return pl.pallas_call(
        grad_tokens_kernel,
        in_specs=[vmem()] * 7,
        out_specs=vmem(),
        out_shape=shaped(grad.shape, low),
        compiler_params=params(),
        cost_estimate=cost(4),
        name="grad_tokens",
    )(grad, joint_a, joint_b, *weights, rest_w)


def finish_ffn_kernel(info, held, held_mates, corner, corner_mate, down, up):
    rows = corner.shape[1]
    for s, (pieces, last) in enumerate(((held, corner), (held_mates, corner_mate))):
        holder = info[1] ^ s
        for move in range(4):
            source = last if move == 3 else pieces.at[move]
            start = pl.multiple_of((holder * 4 + (info[2] ^ move)) * rows, rows)
            down[pl.ds(start, rows), :] = source[0].astype(wide)
            up[pl.ds(start, rows), :] = source[1].astype(wide)


def finish_ffn(info, *pieces):
    _, rows, cols = pieces[-1].shape
    return pl.pallas_call(
        finish_ffn_kernel,
        in_specs=[smem()] + [vmem()] * 4,
        out_specs=[vmem()] * 2,
        out_shape=[shaped((GROUP * rows, cols), wide)] * 2,
        compiler_params=params(),
        cost_estimate=cost(3),
        name="finish_ffn",
    )(info, *pieces)


def finish_attn_kernel(info, *refs):
    query, key, value, out, whole = refs[8:]
    for s in range(2):
        holder = info[1] ^ s
        for move in range(4):
            view = refs[4 * s + move]
            rows = view.shape[0]
            start = pl.multiple_of((holder * 4 + (info[2] ^ move)) * rows, rows)
            whole[pl.ds(start, rows), :] = view[...].astype(wide)
    local = whole.shape[0] // 4
    query[...] = whole[:local]
    key[...] = whole[local : 2 * local]
    value[...] = whole[2 * local : 3 * local]
    out[...] = whole[3 * local :]


def finish_attn(info, pieces):
    rows, cols = pieces[0].shape
    size = GROUP * rows
    local = size // 4
    return pl.pallas_call(
        finish_attn_kernel,
        in_specs=[smem()] + [vmem()] * 8,
        out_specs=[vmem()] * 4,
        out_shape=[shaped((local, cols), wide)] * 4,
        scratch_shapes=[pltpu.VMEM((size, cols), wide)],
        compiler_params=params(),
        cost_estimate=cost(2),
        name="finish_attn",
    )(info, *pieces)


class Links:
    def __init__(self, dp_size, parts):
        self.dp_size, self.parts = dp_size, parts

    def move(self, array, partner):
        pairs = []
        for d in range(self.dp_size):
            for t in range(self.parts):
                to_d, to_t = partner(d, t)
                pairs.append((d * self.parts + t, to_d * self.parts + to_t))
        return lax.ppermute(array, ("dp", "tensor"), pairs)

    def bit(self, array, bit):
        return self.move(array, lambda d, t: (d ^ bit, t))

    def core(self, array):
        return self.bit(array, 1)

    def plane(self, array, step):
        return self.move(array, lambda d, t: (d ^ (2 if (d & 1) == step else 4), t))

    def everywhere(self, array, bits):
        return [self.bit(array, bit) for bit in bits]

    def across(self, array, k):
        return self.move(array, lambda d, t: (d, t ^ k))

    def line(self, array, step):
        return self.move(array, lambda d, t: (d, t ^ (1 if (d & 1) == step else 2)))


def add(left, right):
    return (left.astype(wide) + right.astype(wide)).astype(low)


def after(*values):
    return lax.optimization_barrier(values)


def per_device(
    dp_size,
    parts,
    tokens,
    page_lengths,
    w_query,
    b_query,
    w_key,
    w_value,
    b_value,
    w_out,
    b_out,
    ln1_gain,
    ln1_bias,
    w_up,
    b_up,
    w_down,
    b_down,
    ln2_gain,
    ln2_bias,
    cotangent,
):
    links = Links(dp_size, parts)
    me = lax.axis_index("tensor")
    place = lax.axis_index("dp") % GROUP
    core, quarter = place & 1, place >> 1
    is_odd = core == 1
    width = tokens.shape[1]
    local = w_query.shape[1]
    rows = width // GROUP
    length = lax.dynamic_slice_in_dim(page_lengths, me, 1, 0)
    info = jnp.concatenate([length, jnp.stack([core, quarter, me]).astype(jnp.int32)])
    attn_w = (w_query.T, w_key.T, w_value.T, w_out)
    piece = core * 4 + quarter

    def cut(array, index):
        return lax.dynamic_slice_in_dim(array, index * rows, rows, 0)

    a0 = lax.select_n(piece >> 1, *(cut(array, piece & 1) for array in attn_w))
    bias_own = jnp.concatenate([b_query, b_value, b_up])
    bias_rows = jnp.pad(bias_own, (0, 8 * width - bias_own.size)).reshape(8, width)
    a0, piece_d = after(a0, piece)
    d0 = cut(w_down, piece_d)
    u0 = jnp.concatenate([cut(w_up, piece), bias_rows], axis=0)
    vec = jnp.stack([b_out, ln1_gain, ln1_bias, b_down, ln2_gain, ln2_bias, b_down, b_down])
    vec = vec.astype(wide)
    a1, d1 = links.line(a0, 0), links.line(d0, 0)
    a1, d1, u0, vec, tokens_in = after(a1, d1, u0, vec, tokens)
    a2 = links.line(jnp.stack([a0, a1]), 1)
    u1 = links.line(u0, 0)
    own = list(attn_own(info, tokens_in, attn_w[:3], bias_own.astype(wide)[None, None]))
    a2, u1, own[2] = after(a2, u1, own[2])
    a3 = jnp.concatenate([a1[None], a2])
    a4 = links.plane(a3, 0)
    u2 = links.line(jnp.stack([u0, u1]), 1)
    a4, u2, d1 = after(a4, u2, d1)
    u3 = jnp.concatenate([u1[None], u2])
    bias_rest = u3[:, rows:].reshape(parts - 1, 8 * width)[:, : bias_own.size]
    near, far = bias_rest[0], bias_rest[1]
    bias = jnp.stack(
        [bias_own, jnp.where(is_odd, far, near), jnp.where(is_odd, near, far), bias_rest[2]]
    )
    bias = bias.astype(wide)[:, None]
    u3 = u3[:, :rows]
    a5 = links.plane(jnp.stack([a3, a4]), 1)
    u4 = links.plane(u3, 0)
    d2 = links.line(jnp.stack([d0, d1]), 1)
    a5, u4, d2, bias = after(a5, u4, d2, bias)
    d3 = jnp.concatenate([d1[None], d2])
    pieces_a = [a3, a4, a5] + [links.core(array) for array in (a3, a4, a5)]
    u5 = links.plane(jnp.stack([u3, u4]), 1)
    d4 = links.plane(d3, 0)
    qkv, attn_rest_w, ctx, lse, out_rest = attn_rest(info, tokens, bias, pieces_a)
    skip, normed_low, hat, inv = ffn_in(tokens, own[1], ctx, vec, w_out, out_rest)
    u5, d4, lse, inv = after(u5, d4, lse, inv)
    pieces_u = [u3, u4, u5] + [links.core(array) for array in (u3, u4, u5)]
    d5 = links.plane(jnp.stack([d3, d4]), 1)
    act, slope, up, mark = ffn_up(info, normed_low, bias, w_up, pieces_u, inv)
    d5, mark = after(d5, mark)
    pieces_d = [d3, d4, d5] + [links.core(array) for array in (d3, d4, d5)]
    output, grad_branch, branch_low, small, keep_d, send_d, down = ffn_down(
        info, act, skip, vec, cotangent, w_down, pieces_d, mark
    )
    rest = (qkv, ctx, lse)

    def plane_a(keep, got):
        return links.plane(add(keep[1], got[1]), 0), add(keep[0], got[0])

    def plane_b(kept, got):
        return links.plane(add(kept[1], got[1]), 1), add(kept[0], got[0])

    def line_a(both):
        both = both.reshape(-1, 2, parts // 2, rows, width)
        sent = jnp.where(is_odd, both[:, :, 1], both[:, 1])
        return links.line(sent, 1), jnp.where(is_odd, both[:, :, 0], both[:, 0])

    def line_b(kept, got):
        both = add(kept, got)
        return links.line(both[:, 1], 0), both[:, 0]

    def settle(kept, got):
        total = kept.astype(wide) + got.astype(wide)
        bit = GROUP
        while bit < dp_size:
            total = total + links.bit(total, bit)
            bit *= 2
        return total.astype(low)

    def mates(held):
        return held + [links.core(array) for array in held]

    got_d = links.core(send_d)
    got_d, small = after(got_d, small)
    near_d, kept_d = plane_a(keep_d, got_d)
    grad_residual, residual_low, small, keep_u, send_u = ffn_back(
        info, branch_low, grad_branch, slope, normed_low, hat, inv, vec, small, up, down
    )
    near_d, send_u, small = after(near_d, send_u, small)
    got_u = links.core(send_u)
    far_d, kept_d = plane_b(kept_d, near_d)
    small, joint_a, keep_a, send_a = attn_back(
        0, info, tokens, residual_low, small, w_out, own, out_rest, rest
    )
    got_u, far_d, send_a, small = after(got_u, far_d, send_a, small)
    near_u, kept_u = plane_a(keep_u, got_u)
    got_a = links.core(send_a)
    line_d, kept_d = line_a(add(kept_d, far_d))
    small, joint_b, keep_b, send_b = attn_back(
        2, info, tokens, residual_low, small, w_out, own, out_rest, rest
    )
    near_u, got_a, line_d, send_b, small, grad_residual = after(
        near_u, got_a, line_d, send_b, small, grad_residual
    )
    got_b = links.core(send_b)
    far_u, kept_u = plane_b(kept_u, near_u)
    last_d, kept_d = line_b(kept_d, line_d)
    grad_tokens = grad_tokens_of(grad_residual, joint_a, joint_b, attn_w[:3], attn_rest_w)
    small_got = links.core(small)
    got_b, far_u, last_d, grad_tokens, small_got = after(got_b, far_u, last_d, grad_tokens, small_got)
    small = small + small_got
    size = parts * 2 * rows

    def joined(share, small):
        return jnp.concatenate([share.reshape(-1, width), small.astype(low)], axis=0)

    keep_ab, got_ab = jnp.stack([keep_a, keep_b], axis=2), jnp.stack([got_a, got_b], axis=2)
    near_a = links.plane(joined(add(keep_ab[1], got_ab[1]), small), 0)
    kept_a = add(keep_ab[0], got_ab[0])
    line_u, kept_u = line_a(add(kept_u, far_u))
    near_a, line_u = after(near_a, line_u)
    small = small + near_a[size:].astype(wide)
    near_a = near_a[:size].reshape(kept_a.shape)
    far_a = links.plane(joined(add(kept_a[1], near_a[1]), small), 1)
    kept_a = add(kept_a[0], near_a[0])
    last_u, kept_u = line_b(kept_u, line_u)
    far_a, last_u = after(far_a, last_u)
    size = parts * rows
    small = small + far_a[size:].astype(wide)
    share = add(kept_a, far_a[:size].reshape(kept_a.shape)).reshape(parts, rows, width)
    across = [links.across(joined(share[k], small), k) for k in range(parts - 1, 0, -1)]
    sum_f = jnp.stack([settle(kept_d, last_d)[0], settle(kept_u, last_u)[0]])
    f_x, f_y = links.everywhere(sum_f, (2, 4))
    across, f_x, f_y = after(across, f_x, f_y)
    sum_a = share[0].astype(wide)
    for array in across:
        sum_a = sum_a + array[:rows].astype(wide)
        small = small + array[rows:].astype(wide)
    bit = GROUP
    while bit < dp_size:
        sum_a = sum_a + links.bit(sum_a, bit)
        small = small + links.bit(small, bit)
        bit *= 2
    sum_a = sum_a.astype(low)
    around = links.everywhere(sum_a, (2, 4, 6))
    f_xy = links.plane(jnp.where(is_odd, f_x, f_y), 0)
    held = jnp.stack([sum_f, f_x, f_y])
    held_mates = links.core(held)
    pair = lax.dynamic_index_in_dim(small, 10 + me, 0, keepdims=False)
    grad_b_up = lax.dynamic_index_in_dim(small, 6 + me, 0, keepdims=False)
    around, small, pair, grad_b_up, f_xy, held_mates = after(
        around, small, pair, grad_b_up, f_xy, held_mates
    )
    grad_w_down, grad_w_up = finish_ffn(info, held, held_mates, f_xy, links.core(f_xy))
    grad_w_query, grad_w_key, grad_w_value, grad_w_out = finish_attn(info, mates([sum_a] + around))
    grad_w_query, grad_w_key, grad_w_value = grad_w_query.T, grad_w_key.T, grad_w_value.T
    return (
        output,
        grad_tokens,
        grad_w_query,
        pair[:local],
        grad_w_key,
        grad_w_value,
        pair[256 : 256 + local],
        grad_w_out,
        small[0],
        small[1],
        small[2],
        grad_w_up,
        grad_b_up,
        grad_w_down,
        small[3],
        small[4],
        small[5],
    )


def solution(mesh):
    columns, rows, both = P(None, "tensor"), P("tensor", None), P(("dp", "tensor"), None)
    share = P("tensor")
    return jax.shard_map(
        partial(per_device, mesh.shape["dp"], mesh.shape["tensor"]),
        mesh=mesh,
        in_specs=(
            both,
            P("dp"),
            columns,
            share,
            columns,
            columns,
            share,
            rows,
            P(),
            P(),
            P(),
            columns,
            share,
            rows,
            P(),
            P(),
            P(),
            both,
        ),
        out_specs=(
            both,
            both,
            columns,
            share,
            columns,
            columns,
            share,
            rows,
            P(),
            P(),
            P(),
            columns,
            share,
            rows,
            P(),
            P(),
            P(),
        ),
        check_vma=False,
    )
```

profile of v0, /device:TPU:0, one launch (start us, length us, event | category | flops | bytes accessed | tf_op | source)
XLA Modules:
  0.0 227.8 jit_solution(3899940096945952097)
XLA Ops:
  0.8 1.3 fusion.27
  2.2 0.9 constant_dynamic-slice_fusion.1
  3.1 3.1 %collective-permute-start.1 = (bf16[96,768]{1,0:T(8,128)(2,1)S(1)}, bf16[96,768]{1,0:T(8,128)(2,1)S(1)}, u32[]{:S(2)}, u32[]{:S(2)}) collective-permute-start(bf16[96,768]{1,0:T(8,128)(2,1)S(1)} %constant_dynamic-slice_fusion.1), channel_id=1, source_target_pairs={{0,1},{1,0},{2,3},{3,2},{4,6},{5,7},{6,4},{7,5},{8,9},{9,8},{10,11... | collective-permute-start | bytes 442376 | tf_op jit(solution)/shard_map/ppermute | solution.py:571
  6.3 0.9 constant_dynamic-slice_fusion
  7.8 0.7 pad_add_fusion.info
  9.0 1.5 collective-permute-done.1
  10.5 3.5 %collective-permute-done = bf16[96,768]{1,0:T(8,128)(2,1)S(1)} collective-permute-done((bf16[96,768]{1,0:T(8,128)(2,1)S(1)}, bf16[96,768]{1,0:T(8,128)(2,1)S(1)}, u32[]{:S(2)}, u32[]{:S(2)}) %collective-permute-start) | collective-permute-done | bytes 147488 | tf_op jit(solution)/shard_map/ppermute | solution.py:571
  14.0 2.0 collective-permute-start.2
  16.1 2.6 %collective-permute-start.3 = (bf16[104,768]{1,0:T(8,128)(2,1)S(1)}, bf16[104,768]{1,0:T(8,128)(2,1)S(1)}, u32[]{:S(2)}, u32[]{:S(2)}) collective-permute-start(bf16[104,768]{1,0:T(8,128)(2,1)S(1)} %pad_maximum_fusion.17), channel_id=1, source_target_pairs={{0,1},{1,0},{2,3},{3,2},{4,6},{5,7},{6,4},{7,5},{8,9},{9,8},{10,11... | collective-permute-start | bytes 479240 | tf_op jit(solution)/shard_map/ppermute | solution.py:571
  18.7 3.0 %attn_own.1 = (bf16[1,576,512]{2,1,0:T(8,128)(2,1)S(1)}, bf16[1,192,512]{2,1,0:T(8,128)(2,1)S(1)}, f32[1,8,512]{2,1,0:T(8,128)S(1)}) custom-call(s32[4]{0:T(128)S(1)} %pad_add_fusion.info, bf16[512,768]{1,0:T(8,128)(2,1)S(1)} %copy-done.7, bf16[192,768]{1,0:T(8,128)(2,1)S(1)} %bitcast.167, bf16[192,768]{1,0:T(8,128)(2,1)S(1)} %bitcast.169, ...), custom_call_target="tpu_custom_call" | custom-call | flops 4400000000 | bytes 1048576 | tf_op jit(solution)/shard_map/attn_own/pallas_call | solution.py:162
  21.7 0.8 copy-done.9
  22.5 2.6 %collective-permute-done.3 = bf16[104,768]{1,0:T(8,128)(2,1)S(1)} collective-permute-done((bf16[104,768]{1,0:T(8,128)(2,1)S(1)}, bf16[104,768]{1,0:T(8,128)(2,1)S(1)}, u32[]{:S(2)}, u32[]{:S(2)}) %collective-permute-start.3) | collective-permute-done | bytes 159776 | tf_op jit(solution)/shard_map/ppermute | solution.py:571
  25.0 3.3 %collective-permute-done.2 = bf16[2,96,768]{2,1,0:T(8,128)(2,1)S(1)} collective-permute-done((bf16[2,96,768]{2,1,0:T(8,128)(2,1)S(1)}, bf16[2,96,768]{2,1,0:T(8,128)(2,1)S(1)}, u32[]{:S(2)}, u32[]{:S(2)}) %collective-permute-start.2) | collective-permute-done | bytes 294944 | tf_op jit(solution)/shard_map/ppermute | solution.py:571
  28.4 0.8 fusion.35
  29.2 1.7 collective-permute-start.4
  30.9 0.8 pad_maximum_fusion.10
  32.1 10.9 %collective-permute-done.5 = bf16[2,104,768]{2,1,0:T(8,128)(2,1)S(1)} collective-permute-done((bf16[2,104,768]{2,1,0:T(8,128)(2,1)}, bf16[2,104,768]{2,1,0:T(8,128)(2,1)S(1)}, u32[]{:S(2)}, u32[]{:S(2)}) %collective-permute-start.5) | collective-permute-done | bytes 319520 | tf_op jit(solution)/shard_map/ppermute | solution.py:571
  43.0 0.7 fusion.28
  43.9 1.3 collective-permute-start.6
  45.2 0.9 collective-permute-start.7
  46.3 10.0 %collective-permute-done.8 = bf16[2,96,768]{2,1,0:T(8,128)(2,1)S(1)} collective-permute-done((bf16[2,96,768]{2,1,0:T(8,128)(2,1)S(1)}, bf16[2,96,768]{2,1,0:T(8,128)(2,1)S(1)}, u32[]{:S(2)}, u32[]{:S(2)}) %collective-permute-start.8) | collective-permute-done | bytes 294944 | tf_op jit(solution)/shard_map/ppermute | solution.py:571
  57.6 1.3 collective-permute-start.12
  59.0 0.9 collective-permute-start.13
  60.7 9.2 %attn_rest.1 = (bf16[3,576,512]{2,1,0:T(8,128)(2,1)S(1)}, bf16[3,768,768]{2,1,0:T(8,128)(2,1)S(1)}, bf16[3,192,512]{2,1,0:T(8,128)(2,1)S(1)}, f32[3,8,512]{2,1,0:T(8,128)S(1)}, bf16[3,192,768]{2,1,0:T(8,128)(2,1)S(1)}) custom-call(s32[4]{0:T(128)S(1)} %pad_add_fusion.info, bf16[512,768]{1,0:T(8,128)(2,1)S(1)} %copy-done.8, ...), custom_call_target="tpu_custom_call" | custom-call | flops 8800000000 | bytes 1048576 | tf_op jit(solution)/shard_map/attn_rest/pallas_call | solution.py:204
  69.9 1.6 ffn_in.1
  72.2 3.1 %collective-permute-done.12.refs_2_ = bf16[2,3,96,768]{3,2,1,0:T(8,128)(2,1)S(1)} collective-permute-done((bf16[2,3,96,768]{3,2,1,0:T(8,128)(2,1)S(1)}, bf16[2,3,96,768]{3,2,1,0:T(8,128)(2,1)S(1)}, u32[]{:S(2)}, u32[]{:S(2)}) %collective-permute-start.12) | collective-permute-done | bytes 884768 | tf_op jit(solution)/shard_map/ppermute | solution.py:571
  75.9 1.5 collective-permute-start.17
  77.4 0.9 collective-permute-done.14.refs_3_
  79.0 8.7 %ffn_up.1 = (bf16[4,512,768]{2,1,0:T(8,128)(2,1)S(1)}, bf16[4,512,768]{2,1,0:T(8,128)(2,1)S(1)}, bf16[4,768,768]{2,1,0:T(8,128)(2,1)S(1)}, f32[8,128]{1,0:T(8,128)S(1)}) custom-call(s32[4]{0:T(128)S(1)} %pad_add_fusion.info, bf16[512,768]{1,0:T(8,128)(2,1)S(1)} %get-tuple-element.138.normed.normed_low, f32[4,1,1152]{2,1,0:T(1,128)S(1)} %maximum_convert_fusion.bias, ...), custom_call_target="tpu_custom_call" | custom-call | flops 12099999744 | bytes 1048576 | tf_op jit(solution)/shard_map/ffn_up/pallas_call | solution.py:280
  87.6 1.3 collective-permute-done.17.refs_2_
  89.5 2.5 %collective-permute-done.18.refs_3_ = bf16[3,96,768]{2,1,0:T(8,128)(2,1)S(1)} collective-permute-done((bf16[3,96,768]{2,1,0:T(8,128)(2,1)S(1)}, bf16[3,96,768]{2,1,0:T(8,128)(2,1)S(1)}, u32[]{:S(2)}, u32[]{:S(2)}) %collective-permute-start.18) | collective-permute-done | bytes 442400 | tf_op jit(solution)/shard_map/ppermute | solution.py:571
  92.7 9.9 %ffn_down.1 = (bf16[512,768]{1,0:T(8,128)(2,1)}, f32[512,768]{1,0:T(8,128)S(1)}, bf16[512,768]{1,0:T(8,128)(2,1)S(1)}, f32[16,768]{1,0:T(8,128)S(1)}, bf16[2,2,4...) custom-call(s32[4]{0:T(128)S(1)} %pad_add_fusion.info, ...), custom_call_target="tpu_custom_call" | custom-call | flops 13200000000 | bytes 1048576 | tf_op jit(solution)/shard_map/ffn_down/pallas_call | solution.py:337
  102.7 4.4 %collective-permute-done.21 = bf16[2,2,4,96,768]{4,3,2,1,0:T(8,128)(2,1)S(1)} collective-permute-done((bf16[2,2,4,96,768]{4,3,2,1,0:T(8,128)(2,1)S(1)}, bf16[2,2,4,96,768]{4,3,2,1,0:T(8,128)(2,1)S(1)}, u32[]{:S(2)}, u32[]{:S(2)}) %collective-permute-start.21) | collective-permute-done | bytes 2359328 | tf_op jit(solution)/shard_map/ppermute | solution.py:571
  107.1 0.7 add_convert_fusion.4
  108.5 10.5 %ffn_back.1 = (f32[512,768]{1,0:T(8,128)S(1)}, bf16[512,768]{1,0:T(8,128)(2,1)S(1)}, f32[16,768]{1,0:T(8,128)S(1)}, bf16[2,2,4,96,768]{4,3,2,1,0:T(8,128)(2,1)S(1)}, bf16[2,2,4,96,768]{4,3,2,1,0:T(8,128)(2,1)S(1)}) custom-call(s32[4]{0:T(128)S(1)} %pad_add_fusion.info, bf16[512,768]{1,0:T(8,128)(2,1)S(1)} %get-tuple-element.151.branch_low, ...), custom_call_target="tpu_custom_call" | custom-call | flops 12099999744 | bytes 1048576 | tf_op jit(solution)/shard_map/ffn_back/pallas_call | solution.py:392
  119.0 5.1 %collective-permute-done.22 = bf16[2,4,96,768]{3,2,1,0:T(8,128)(2,1)S(1)} collective-permute-done((bf16[2,4,96,768]{3,2,1,0:T(8,128)(2,1)S(1)}, bf16[2,4,96,768]{3,2,1,0:T(8,128)(2,1)S(1)}, u32[]{:S(2)}, u32[]{:S(2)}) %collective-permute-start.22) | collective-permute-done | bytes 1179680 | tf_op jit(solution)/shard_map/ppermute | solution.py:571
  124.2 1.5 collective-permute-start.24
  125.7 7.9 %attn_back.2 = (f32[16,768]{1,0:T(8,128)S(1)}, bf16[2,576,512]{2,1,0:T(8,128)(2,1)S(1)}, bf16[2,2,2,96,768]{4,3,2,1,0:T(8,128)(2,1)S(1)}, bf16[2,2,2,96,768]{4,3,2,1,0:T(8,128)(2,1)S(1)}) custom-call(s32[4]{0:T(128)S(1)} %pad_add_fusion.info, bf16[512,768]{1,0:T(8,128)(2,1)S(1)} %copy-done.8, bf16[512,768]{1,0:T(8,128)(2,1)S(1)} %get-tuple-element.167.residual_low, ...), custom_call_target="tpu_custom_call" | custom-call | flops 9900000256 | bytes 1048576 | tf_op jit(solution)/shard_map/attn_back/pallas_call | solution.py:465
  134.2 0.7 add_convert_fusion.2
  136.2 8.2 %attn_back.3 = (f32[16,768]{1,0:T(8,128)S(1)}, bf16[2,576,512]{2,1,0:T(8,128)(2,1)S(1)}, bf16[2,2,2,96,768]{4,3,2,1,0:T(8,128)(2,1)S(1)}, bf16[2,2,2,96,768]{4,3,2,1,0:T(8,128)(2,1)S(1)}) custom-call(s32[4]{0:T(128)S(1)} %pad_add_fusion.info, bf16[512,768]{1,0:T(8,128)(2,1)S(1)} %copy-done.8, bf16[512,768]{1,0:T(8,128)(2,1)S(1)} %get-tuple-element.167.residual_low, ...), custom_call_target="tpu_custom_call" | custom-call | flops 9900000256 | bytes 1048576 | tf_op jit(solution)/shard_map/attn_back/pallas_call | solution.py:465
  144.4 2.3 %collective-permute-done.27 = bf16[1,2,96,768]{3,2,1,0:T(8,128)(2,1)S(1)} collective-permute-done((bf16[1,2,96,768]{3,2,1,0:T(8,128)(2,1)S(1)}, bf16[1,2,96,768]{3,2,1,0:T(8,128)(2,1)S(1)}, u32[]{:S(2)}, u32[]{:S(2)}) %collective-permute-start.27) | collective-permute-done | bytes 294944 | tf_op jit(solution)/shard_map/ppermute | solution.py:571
  146.7 4.4 %collective-permute-done.25 = bf16[2,4,96,768]{3,2,1,0:T(8,128)(2,1)S(1)} collective-permute-done((bf16[2,4,96,768]{3,2,1,0:T(8,128)(2,1)S(1)}, bf16[2,4,96,768]{3,2,1,0:T(8,128)(2,1)S(1)}, u32[]{:S(2)}, u32[]{:S(2)}) %collective-permute-start.25) | collective-permute-done | bytes 1179680 | tf_op jit(solution)/shard_map/ppermute | solution.py:571
  151.3 1.5 collective-permute-start.29
  153.1 3.6 %grad_tokens.1 = bf16[512,768]{1,0:T(8,128)(2,1)} custom-call(f32[512,768]{1,0:T(8,128)S(1)} %get-tuple-element.185.grad, bf16[2,576,512]{2,1,0:T(8,128)(2,1)S(1)} %get-tuple-element.186.joint_a, bf16[2,576,512]{2,1,0:T(8,128)(2,1)S(1)} %get-tuple-element.187.joint_b, bf16[192,768]{1,0:T(8,128)(2,1)S(1)} %bitcast.168, bf16[192,768]{1,0:T(8,128)(2,1)S(1)} %bitcast.170, ...), custom_call_target="tpu_custom_call" | custom-call | flops 4400000000 | bytes 1048576 | tf_op jit(solution)/shard_map/grad_tokens/pallas_call | solution.py:494
  156.7 2.9 %collective-permute-done.30 = bf16[1,96,768]{2,1,0:T(8,128)(2,1)S(1)} collective-permute-done((bf16[1,96,768]{2,1,0:T(8,128)(2,1)S(1)}, bf16[1,96,768]{2,1,0:T(8,128)(2,1)S(1)}, u32[]{:S(2)}, u32[]{:S(2)}) %collective-permute-start.30) | collective-permute-done | bytes 147488 | tf_op jit(solution)/shard_map/ppermute | solution.py:571
  159.7 1.6 collective-permute-done.29
  163.5 10.4 %collective-permute-done.33 = bf16[1,2,96,768]{3,2,1,0:T(8,128)(2,1)S(1)} collective-permute-done((bf16[1,2,96,768]{3,2,1,0:T(8,128)(2,1)S(1)}, bf16[1,2,96,768]{3,2,1,0:T(8,128)(2,1)S(1)}, u32[]{:S(2)}, u32[]{:S(2)}) %collective-permute-start.33) | collective-permute-done | bytes 294944 | tf_op jit(solution)/shard_map/ppermute | solution.py:571
  173.9 4.8 %collective-permute-done.32 = bf16[784,768]{1,0:T(8,128)(2,1)S(1)} collective-permute-done((bf16[784,768]{1,0:T(8,128)(2,1)S(1)}, bf16[784,768]{1,0:T(8,128)(2,1)S(1)}, u32[]{:S(2)}, u32[]{:S(2)}) %collective-permute-start.32) | collective-permute-done | bytes 1204256 | tf_op jit(solution)/shard_map/ppermute | solution.py:571
  178.9 1.5 collective-permute-start.34
  180.7 5.8 %collective-permute-done.35 = bf16[1,96,768]{2,1,0:T(8,128)(2,1)S(1)} collective-permute-done((bf16[1,96,768]{2,1,0:T(8,128)(2,1)S(1)}, bf16[1,96,768]{2,1,0:T(8,128)(2,1)S(1)}, u32[]{:S(2)}, u32[]{:S(2)}) %collective-permute-start.35) | collective-permute-done | bytes 147488 | tf_op jit(solution)/shard_map/ppermute | solution.py:571
  186.4 2.7 %collective-permute-done.34 = bf16[400,768]{1,0:T(8,128)(2,1)S(1)} collective-permute-done((bf16[400,768]{1,0:T(8,128)(2,1)S(1)}, bf16[400,768]{1,0:T(8,128)(2,1)S(1)}, u32[]{:S(2)}, u32[]{:S(2)}) %collective-permute-start.34) | collective-permute-done | bytes 614432 | tf_op jit(solution)/shard_map/ppermute | solution.py:571
  189.9 1.7 collective-permute-start.40
  192.0 2.3 collective-permute-start.36
  194.3 2.2 collective-permute-start.38
  196.5 4.7 %collective-permute-done.36 = bf16[112,768]{1,0:T(8,128)(2,1)S(1)} collective-permute-done((bf16[112,768]{1,0:T(8,128)(2,1)S(1)}, bf16[112,768]{1,0:T(8,128)(2,1)S(1)}, u32[]{:S(2)}, u32[]{:S(2)}) %collective-permute-start.36) | collective-permute-done | bytes 172064 | tf_op jit(solution)/shard_map/ppermute | solution.py:571
  201.2 5.6 %collective-permute-done.37 = bf16[112,768]{1,0:T(8,128)(2,1)S(1)} collective-permute-done((bf16[112,768]{1,0:T(8,128)(2,1)S(1)}, bf16[112,768]{1,0:T(8,128)(2,1)S(1)}, u32[]{:S(2)}, u32[]{:S(2)}) %collective-permute-start.37) | collective-permute-done | bytes 172064 | tf_op jit(solution)/shard_map/ppermute | solution.py:571
  207.0 1.3 collective-permute-start.44
  208.4 0.9 collective-permute-start.41
  209.6 2.3 %collective-permute-start.43 = (bf16[96,768]{1,0:T(8,128)(2,1)S(1)}, bf16[96,768]{1,0:T(8,128)(2,1)S(1)}, u32[]{:S(2)}, u32[]{:S(2)}) collective-permute-start(bf16[96,768]{1,0:T(8,128)(2,1)S(1)} %fusion.26.refs_0_), channel_id=1, source_target_pairs={{0,24},{1,25},{2,26},{3,27},{4,28},{5,29},{6,30},{7,31},{8,16},{9,... | collective-permute-start | bytes 442376 | tf_op jit(solution)/shard_map/ppermute | solution.py:571
  211.9 0.8 convert_add_fusion.12
  213.3 5.0 %collective-permute-done.41.refs_1_ = bf16[96,768]{1,0:T(8,128)(2,1)S(1)} collective-permute-done((bf16[96,768]{1,0:T(8,128)(2,1)S(1)}, bf16[96,768]{1,0:T(8,128)(2,1)S(1)}, u32[]{:S(2)}, u32[]{:S(2)}) %collective-permute-start.41) | collective-permute-done | bytes 147488 | tf_op jit(solution)/shard_map/ppermute | solution.py:571
  218.3 1.6 collective-permute-done.43.refs_3_
  222.2 2.1 finish_attn.1
  224.3 3.0 %finish_ffn.1 = (f32[768,768]{1,0:T(8,128)}, f32[768,768]{1,0:T(8,128)}) custom-call(s32[4]{0:T(128)S(1)} %pad_add_fusion.info, bf16[3,2,96,768]{3,2,1,0:T(8,128)(2,1)S(1)} %pad_maximum_fusion.6.held, bf16[3,2,96,768]{3,2,1,0:T(8,128)(2,1)S(1)} %collective-permute-done.45.held_mates, bf16[2,96,768]{2,1,0:T(8,128)(2,1)S(1)} %collective-permute-done.44.corner, ...), custom_call_target="tpu_custom_call" | custom-call | flops 3300000000 | bytes 1048576 | tf_op jit(solution)/shard_map/finish_ffn/pallas_call | solution.py:518
  (182 shorter events, 17.6 us)
Async XLA Ops:
  0.7 8.0 %copy-start.25 = (bf16[768]{0:T(1024)(128)(2,1)S(1)}, bf16[768]{0:T(1024)(128)(2,1)}, u32[]{:S(2)}) copy-start(bf16[768]{0:T(1024)(128)(2,1)} %param.33) | copy-start | bytes 4612
  0.8 8.1 %copy-start.26 = (bf16[768]{0:T(1024)(128)(2,1)S(1)}, bf16[768]{0:T(1024)(128)(2,1)}, u32[]{:S(2)}) copy-start(bf16[768]{0:T(1024)(128)(2,1)} %param.34) | copy-start | bytes 4612
  0.8 17.9 %copy-start.2 = (bf16[768,192]{0,1:T(8,128)(2,1)S(1)}, bf16[768,192]{0,1:T(8,128)(2,1)}, u32[]{:S(2)}) copy-start(bf16[768,192]{0,1:T(8,128)(2,1)} %param.20) | copy-start | bytes 884740
  0.8 17.9 %copy-start.3 = (bf16[768,192]{0,1:T(8,128)(2,1)S(1)}, bf16[768,192]{0,1:T(8,128)(2,1)}, u32[]{:S(2)}) copy-start(bf16[768,192]{0,1:T(8,128)(2,1)} %param.22) | copy-start | bytes 884740
  0.8 17.8 %copy-start.4 = (bf16[768,192]{0,1:T(8,128)(2,1)S(1)}, bf16[768,192]{0,1:T(8,128)(2,1)}, u32[]{:S(2)}) copy-start(bf16[768,192]{0,1:T(8,128)(2,1)} %param.23) | copy-start | bytes 884740
  0.8 17.8 %copy-start.7 = (bf16[512,768]{1,0:T(8,128)(2,1)S(1)}, bf16[512,768]{1,0:T(8,128)(2,1)}, u32[]{:S(2)}) copy-start(bf16[512,768]{1,0:T(8,128)(2,1)} %tokens.8) | copy-start | bytes 2359300
  3.1 7.4 %collective-permute-start.1 = (bf16[96,768]{1,0:T(8,128)(2,1)S(1)}, bf16[96,768]{1,0:T(8,128)(2,1)S(1)}, u32[]{:S(2)}, u32[]{:S(2)}) collective-permute-start(bf16[96,768]{1,0:T(8,128)(2,1)S(1)} %constant_dynamic-slice_fusion.1), channel_id=1, source_target_pairs={{0,1},{1,0},{2,3},{3,2},{4,6},{5,7},{6,4},{7,5},{8,9},{9,8},{10,11... | collective-permute-start | bytes 442376 | tf_op jit(solution)/shard_map/ppermute | solution.py:571
  6.2 7.8 %collective-permute-start = (bf16[96,768]{1,0:T(8,128)(2,1)S(1)}, bf16[96,768]{1,0:T(8,128)(2,1)S(1)}, u32[]{:S(2)}, u32[]{:S(2)}) collective-permute-start(bf16[96,768]{1,0:T(8,128)(2,1)S(1)} %fusion.27), channel_id=1, source_target_pairs={{0,1},{1,0},{2,3},{3,2},{4,6},{5,7},{6,4},{7,5},{8,9},{9,8},{10,11... | collective-permute-start | bytes 442376 | tf_op jit(solution)/shard_map/ppermute | solution.py:571
  10.5 8.1 %copy-start.18 = (bf16[96,768]{1,0:T(8,128)(2,1)}, bf16[96,768]{1,0:T(8,128)(2,1)S(1)}, u32[]{:S(2)}) copy-start(bf16[96,768]{1,0:T(8,128)(2,1)S(1)} %collective-permute-done.1) | copy-start | bytes 442372
  14.0 14.3 %collective-permute-start.2 = (bf16[2,96,768]{2,1,0:T(8,128)(2,1)S(1)}, bf16[2,96,768]{2,1,0:T(8,128)(2,1)S(1)}, u32[]{:S(2)}, u32[]{:S(2)}) collective-permute-start(bf16[2,96,768]{2,1,0:T(8,128)(2,1)S(1)} %pad_maximum_fusion.11), channel_id=1, source_target_pairs={{0,2},{1,3},{2,0},{3,1},{4,5},{5,4},{6,7},{7,6},{8,10},{9,11},{10,... | collective-permute-start | bytes 884744 | tf_op jit(solution)/shard_map/ppermute | solution.py:571
  16.1 8.9 %collective-permute-start.3 = (bf16[104,768]{1,0:T(8,128)(2,1)S(1)}, bf16[104,768]{1,0:T(8,128)(2,1)S(1)}, u32[]{:S(2)}, u32[]{:S(2)}) collective-permute-start(bf16[104,768]{1,0:T(8,128)(2,1)S(1)} %pad_maximum_fusion.17), channel_id=1, source_target_pairs={{0,1},{1,0},{2,3},{3,2},{4,6},{5,7},{6,4},{7,5},{8,9},{9,8},{10,11... | collective-permute-start | bytes 479240 | tf_op jit(solution)/shard_map/ppermute | solution.py:571
  22.5 9.6 %copy-start = (bf16[768,768]{1,0:T(8,128)(2,1)S(1)}, bf16[768,768]{1,0:T(8,128)(2,1)}, u32[]{:S(2)}) copy-start(bf16[768,768]{1,0:T(8,128)(2,1)} %down_own.1) | copy-start | bytes 3538948
  29.2 13.8 %collective-permute-start.4 = (bf16[3,96,768]{2,1,0:T(8,128)(2,1)S(1)}, bf16[3,96,768]{2,1,0:T(8,128)(2,1)S(1)}, u32[]{:S(2)}, u32[]{:S(2)}) collective-permute-start(bf16[3,96,768]{2,1,0:T(8,128)(2,1)S(1)} %get-tuple-element.245.refs_0_), channel_id=1, source_target_pairs={{0,8},{1,9},{2,10},{3,11},{4,20},{5,21},{6,22},{7,23},{8,0},{9,1},... | collective-permute-start | bytes 1327112 | tf_op jit(solution)/shard_map/ppermute | solution.py:571
  31.7 11.4 %collective-permute-start.5 = (bf16[2,104,768]{2,1,0:T(8,128)(2,1)}, bf16[2,104,768]{2,1,0:T(8,128)(2,1)S(1)}, u32[]{:S(2)}, u32[]{:S(2)}) collective-permute-start(bf16[2,104,768]{2,1,0:T(8,128)(2,1)} %pad_maximum_fusion.10), channel_id=1, source_target_pairs={{0,2},{1,3},{2,0},{3,1},{4,5},{5,4},{6,7},{7,6},{8,10},{9,11},{10,... | collective-permute-start | bytes 958472 | tf_op jit(solution)/shard_map/ppermute | solution.py:571
  32.1 11.7 %copy-start.15 = (bf16[1,3,96,768]{3,2,1,0:T(8,128)(2,1)S(1)}, bf16[1,3,96,768]{3,2,1,0:T(8,128)(2,1)}, u32[]{:S(2)}) copy-start(bf16[1,3,96,768]{3,2,1,0:T(8,128)(2,1)} %get-tuple-element.244) | copy-start | bytes 1327108
  32.1 13.1 %copy-start.14 = (bf16[104,768]{1,0:T(8,128)(2,1)S(1)}, bf16[104,768]{1,0:T(8,128)(2,1)}, u32[]{:S(2)}) copy-start(bf16[104,768]{1,0:T(8,128)(2,1)} %copy-done.13) | copy-start | bytes 479236
  43.9 13.1 %collective-permute-start.6 = (bf16[2,3,96,768]{3,2,1,0:T(8,128)(2,1)S(1)}, bf16[2,3,96,768]{3,2,1,0:T(8,128)(2,1)S(1)}, u32[]{:S(2)}, u32[]{:S(2)}) collective-permute-start(bf16[2,3,96,768]{3,2,1,0:T(8,128)(2,1)S(1)} %pad_maximum_fusion.3), channel_id=1, source_target_pairs={{0,16},{1,17},{2,18},{3,19},{4,12},{5,13},{6,14},{7,15},{8,24},{9,... | collective-permute-start | bytes 2654216 | tf_op jit(solution)/shard_map/ppermute | solution.py:571
  45.2 11.1 %collective-permute-start.7 = (bf16[3,96,768]{2,1,0:T(8,128)(2,1)S(1)}, bf16[3,96,768]{2,1,0:T(8,128)(2,1)S(1)}, u32[]{:S(2)}, u32[]{:S(2)}) collective-permute-start(bf16[3,96,768]{2,1,0:T(8,128)(2,1)S(1)} %fusion.17.refs_0_), channel_id=1, source_target_pairs={{0,8},{1,9},{2,10},{3,11},{4,20},{5,21},{6,22},{7,23},{8,0},{9,1},... | collective-permute-start | bytes 1327112 | tf_op jit(solution)/shard_map/ppermute | solution.py:571
  46.1 10.1 %collective-permute-start.8 = (bf16[2,96,768]{2,1,0:T(8,128)(2,1)S(1)}, bf16[2,96,768]{2,1,0:T(8,128)(2,1)S(1)}, u32[]{:S(2)}, u32[]{:S(2)}) collective-permute-start(bf16[2,96,768]{2,1,0:T(8,128)(2,1)S(1)} %pad_maximum_fusion.12), channel_id=1, source_target_pairs={{0,2},{1,3},{2,0},{3,1},{4,5},{5,4},{6,7},{7,6},{8,10},{9,11},{10,... | collective-permute-start | bytes 884744 | tf_op jit(solution)/shard_map/ppermute | solution.py:571
  57.0 3.7 %collective-permute-start.11 = (bf16[2,3,96,768]{3,2,1,0:T(8,128)(2,1)S(1)}, bf16[2,3,96,768]{3,2,1,0:T(8,128)(2,1)S(1)}, u32[]{:S(2)}, u32[]{:S(2)}) collective-permute-start(bf16[2,3,96,768]{3,2,1,0:T(8,128)(2,1)S(1)} %collective-permute-done.6.refs_2_), channel_id=1, source_target_pairs={{0,4},{1,5},{2,6},{3,7},{4,0},{5,1},{6,2},{7,3},{8,12},{9,13},{10,... | collective-permute-start | bytes 2654216 | tf_op jit(solution)/shard_map/ppermute | solution.py:571
  57.0 3.1 %collective-permute-start.9 = (bf16[3,96,768]{2,1,0:T(8,128)(2,1)S(1)}, bf16[3,96,768]{2,1,0:T(8,128)(2,1)S(1)}, u32[]{:S(2)}, u32[]{:S(2)}) collective-permute-start(bf16[3,96,768]{2,1,0:T(8,128)(2,1)S(1)} %get-tuple-element.245.refs_0_), channel_id=1, source_target_pairs={{0,4},{1,5},{2,6},{3,7},{4,0},{5,1},{6,2},{7,3},{8,12},{9,13},{10,... | collective-permute-start | bytes 1327112 | tf_op jit(solution)/shard_map/ppermute | solution.py:571
  57.5 3.2 %collective-permute-start.10 = (bf16[3,96,768]{2,1,0:T(8,128)(2,1)S(1)}, bf16[3,96,768]{2,1,0:T(8,128)(2,1)S(1)}, u32[]{:S(2)}, u32[]{:S(2)}) collective-permute-start(bf16[3,96,768]{2,1,0:T(8,128)(2,1)S(1)} %collective-permute-done.4.refs_1_), channel_id=1, source_target_pairs={{0,4},{1,5},{2,6},{3,7},{4,0},{5,1},{6,2},{7,3},{8,12},{9,13},{10,... | collective-permute-start | bytes 1327112 | tf_op jit(solution)/shard_map/ppermute | solution.py:571
  57.6 17.6 %collective-permute-start.12 = (bf16[2,3,96,768]{3,2,1,0:T(8,128)(2,1)S(1)}, bf16[2,3,96,768]{3,2,1,0:T(8,128)(2,1)S(1)}, u32[]{:S(2)}, u32[]{:S(2)}) collective-permute-start(bf16[2,3,96,768]{3,2,1,0:T(8,128)(2,1)S(1)} %pad_maximum_fusion.4), channel_id=1, source_target_pairs={{0,16},{1,17},{2,18},{3,19},{4,12},{5,13},{6,14},{7,15},{8,24},{9,... | collective-permute-start | bytes 2654216 | tf_op jit(solution)/shard_map/ppermute | solution.py:571
  59.0 10.9 %copy-start.1 = (bf16[192,768]{1,0:T(8,128)(2,1)S(1)}, bf16[192,768]{1,0:T(8,128)(2,1)}, u32[]{:S(2)}) copy-start(bf16[192,768]{1,0:T(8,128)(2,1)} %refs_0_.1) | copy-start | bytes 884740
  59.0 13.2 %collective-permute-start.13 = (bf16[3,96,768]{2,1,0:T(8,128)(2,1)S(1)}, bf16[3,96,768]{2,1,0:T(8,128)(2,1)S(1)}, u32[]{:S(2)}, u32[]{:S(2)}) collective-permute-start(bf16[3,96,768]{2,1,0:T(8,128)(2,1)S(1)} %get-tuple-element.243.refs_0_), channel_id=1, source_target_pairs={{0,8},{1,9},{2,10},{3,11},{4,20},{5,21},{6,22},{7,23},{8,0},{9,1},... | collective-permute-start | bytes 1327112 | tf_op jit(solution)/shard_map/ppermute | solution.py:571
  75.3 3.7 %collective-permute-start.16 = (bf16[2,3,96,768]{3,2,1,0:T(8,128)(2,1)S(1)}, bf16[2,3,96,768]{3,2,1,0:T(8,128)(2,1)S(1)}, u32[]{:S(2)}, u32[]{:S(2)}) collective-permute-start(bf16[2,3,96,768]{3,2,1,0:T(8,128)(2,1)S(1)} %collective-permute-done.12.refs_2_), channel_id=1, source_target_pairs={{0,4},{1,5},{2,6},{3,7},{4,0},{5,1},{6,2},{7,3},{8,12},{9,13},{10,... | collective-permute-start | bytes 2654216 | tf_op jit(solution)/shard_map/ppermute | solution.py:571
  75.3 3.1 %collective-permute-start.14 = (bf16[3,96,768]{2,1,0:T(8,128)(2,1)S(1)}, bf16[3,96,768]{2,1,0:T(8,128)(2,1)S(1)}, u32[]{:S(2)}, u32[]{:S(2)}) collective-permute-start(bf16[3,96,768]{2,1,0:T(8,128)(2,1)S(1)} %fusion.17.refs_0_), channel_id=1, source_target_pairs={{0,4},{1,5},{2,6},{3,7},{4,0},{5,1},{6,2},{7,3},{8,12},{9,13},{10,... | collective-permute-start | bytes 1327112 | tf_op jit(solution)/shard_map/ppermute | solution.py:571
  75.8 3.2 %collective-permute-start.15 = (bf16[3,96,768]{2,1,0:T(8,128)(2,1)S(1)}, bf16[3,96,768]{2,1,0:T(8,128)(2,1)S(1)}, u32[]{:S(2)}, u32[]{:S(2)}) collective-permute-start(bf16[3,96,768]{2,1,0:T(8,128)(2,1)S(1)} %collective-permute-done.7.refs_1_), channel_id=1, source_target_pairs={{0,4},{1,5},{2,6},{3,7},{4,0},{5,1},{6,2},{7,3},{8,12},{9,13},{10,... | collective-permute-start | bytes 1327112 | tf_op jit(solution)/shard_map/ppermute | solution.py:571
  75.9 13.1 %collective-permute-start.17 = (bf16[2,3,96,768]{3,2,1,0:T(8,128)(2,1)S(1)}, bf16[2,3,96,768]{3,2,1,0:T(8,128)(2,1)S(1)}, u32[]{:S(2)}, u32[]{:S(2)}) collective-permute-start(bf16[2,3,96,768]{3,2,1,0:T(8,128)(2,1)S(1)} %pad_maximum_fusion.5), channel_id=1, source_target_pairs={{0,16},{1,17},{2,18},{3,19},{4,12},{5,13},{6,14},{7,15},{8,24},{9,... | collective-permute-start | bytes 2654216 | tf_op jit(solution)/shard_map/ppermute | solution.py:571
  79.0 13.7 %copy-start.6 = (bf16[512,768]{1,0:T(8,128)(2,1)S(1)}, bf16[512,768]{1,0:T(8,128)(2,1)}, u32[]{:S(2)}) copy-start(bf16[512,768]{1,0:T(8,128)(2,1)} %cot.1) | copy-start | bytes 2359300
  89.0 3.7 %collective-permute-start.20 = (bf16[2,3,96,768]{3,2,1,0:T(8,128)(2,1)S(1)}, bf16[2,3,96,768]{3,2,1,0:T(8,128)(2,1)S(1)}, u32[]{:S(2)}, u32[]{:S(2)}) collective-permute-start(bf16[2,3,96,768]{3,2,1,0:T(8,128)(2,1)S(1)} %collective-permute-done.17.refs_2_), channel_id=1, source_target_pairs={{0,4},{1,5},{2,6},{3,7},{4,0},{5,1},{6,2},{7,3},{8,12},{9,13},{10,... | collective-permute-start | bytes 2654216 | tf_op jit(solution)/shard_map/ppermute | solution.py:571
  89.0 3.1 %collective-permute-start.18 = (bf16[3,96,768]{2,1,0:T(8,128)(2,1)S(1)}, bf16[3,96,768]{2,1,0:T(8,128)(2,1)S(1)}, u32[]{:S(2)}, u32[]{:S(2)}) collective-permute-start(bf16[3,96,768]{2,1,0:T(8,128)(2,1)S(1)} %get-tuple-element.243.refs_0_), channel_id=1, source_target_pairs={{0,4},{1,5},{2,6},{3,7},{4,0},{5,1},{6,2},{7,3},{8,12},{9,13},{10,... | collective-permute-start | bytes 1327112 | tf_op jit(solution)/shard_map/ppermute | solution.py:571
  89.5 3.2 %collective-permute-start.19 = (bf16[3,96,768]{2,1,0:T(8,128)(2,1)S(1)}, bf16[3,96,768]{2,1,0:T(8,128)(2,1)S(1)}, u32[]{:S(2)}, u32[]{:S(2)}) collective-permute-start(bf16[3,96,768]{2,1,0:T(8,128)(2,1)S(1)} %collective-permute-done.13.refs_1_), channel_id=1, source_target_pairs={{0,4},{1,5},{2,6},{3,7},{4,0},{5,1},{6,2},{7,3},{8,12},{9,13},{10,... | collective-permute-start | bytes 1327112 | tf_op jit(solution)/shard_map/ppermute | solution.py:571
  102.5 4.5 %collective-permute-start.21 = (bf16[2,2,4,96,768]{4,3,2,1,0:T(8,128)(2,1)S(1)}, bf16[2,2,4,96,768]{4,3,2,1,0:T(8,128)(2,1)S(1)}, u32[]{:S(2)}, u32[]{:S(2)}) collective-permute-start(bf16[2,2,4,96,768]{4,3,2,1,0:T(8,128)(2,1)S(1)} %get-tuple-element.154), channel_id=1, source_target_pairs={{0,4},{1,5},{2,6},{3,7},{4,0},{5,1},{6,2},{7,3},{8,12},{9,13},{10,... | collective-permute-start | bytes 7077896 | tf_op jit(solution)/shard_map/ppermute | solution.py:571
  107.8 16.3 %collective-permute-start.22 = (bf16[2,4,96,768]{3,2,1,0:T(8,128)(2,1)S(1)}, bf16[2,4,96,768]{3,2,1,0:T(8,128)(2,1)S(1)}, u32[]{:S(2)}, u32[]{:S(2)}) collective-permute-start(bf16[2,4,96,768]{3,2,1,0:T(8,128)(2,1)S(1)} %get-tuple-element.236), channel_id=1, source_target_pairs={{0,8},{1,9},{2,10},{3,11},{4,20},{5,21},{6,22},{7,23},{8,0},{9,1},... | collective-permute-start | bytes 3538952 | tf_op jit(solution)/shard_map/ppermute | solution.py:571
  124.1 10.1 %collective-permute-start.23 = (bf16[2,2,4,96,768]{4,3,2,1,0:T(8,128)(2,1)S(1)}, bf16[2,2,4,96,768]{4,3,2,1,0:T(8,128)(2,1)S(1)}, u32[]{:S(2)}, u32[]{:S(2)}) collective-permute-start(bf16[2,2,4,96,768]{4,3,2,1,0:T(8,128)(2,1)S(1)} %get-tuple-element.165), channel_id=1, source_target_pairs={{0,4},{1,5},{2,6},{3,7},{4,0},{5,1},{6,2},{7,3},{8,12},{9,13},{10,... | collective-permute-start | bytes 7077896 | tf_op jit(solution)/shard_map/ppermute | solution.py:571
  124.2 9.9 %collective-permute-start.24 = (bf16[4,96,768]{2,1,0:T(8,128)(2,1)S(1)}, bf16[4,96,768]{2,1,0:T(8,128)(2,1)S(1)}, u32[]{:S(2)}, u32[]{:S(2)}) collective-permute-start(bf16[4,96,768]{2,1,0:T(8,128)(2,1)S(1)} %fusion.13), channel_id=1, source_target_pairs={{0,16},{1,17},{2,18},{3,19},{4,12},{5,13},{6,14},{7,15},{8,24},{9,... | collective-permute-start | bytes 1769480 | tf_op jit(solution)/shard_map/ppermute | solution.py:571
  134.9 16.3 %collective-permute-start.25 = (bf16[2,4,96,768]{3,2,1,0:T(8,128)(2,1)S(1)}, bf16[2,4,96,768]{3,2,1,0:T(8,128)(2,1)S(1)}, u32[]{:S(2)}, u32[]{:S(2)}) collective-permute-start(bf16[2,4,96,768]{3,2,1,0:T(8,128)(2,1)S(1)} %get-tuple-element.234), channel_id=1, source_target_pairs={{0,8},{1,9},{2,10},{3,11},{4,20},{5,21},{6,22},{7,23},{8,0},{9,1},... | collective-permute-start | bytes 3538952 | tf_op jit(solution)/shard_map/ppermute | solution.py:571
  135.6 15.6 %collective-permute-start.26 = (bf16[2,2,2,96,768]{4,3,2,1,0:T(8,128)(2,1)S(1)}, bf16[2,2,2,96,768]{4,3,2,1,0:T(8,128)(2,1)S(1)}, u32[]{:S(2)}, u32[]{:S(2)}) collective-permute-start(bf16[2,2,2,96,768]{4,3,2,1,0:T(8,128)(2,1)S(1)} %get-tuple-element.176), channel_id=1, source_target_pairs={{0,4},{1,5},{2,6},{3,7},{4,0},{5,1},{6,2},{7,3},{8,12},{9,13},{10,... | collective-permute-start | bytes 3538952 | tf_op jit(solution)/shard_map/ppermute | solution.py:571
  136.1 10.7 %collective-permute-start.27 = (bf16[1,2,96,768]{3,2,1,0:T(8,128)(2,1)S(1)}, bf16[1,2,96,768]{3,2,1,0:T(8,128)(2,1)S(1)}, u32[]{:S(2)}, u32[]{:S(2)}) collective-permute-start(bf16[1,2,96,768]{3,2,1,0:T(8,128)(2,1)S(1)} %fusion.21), channel_id=1, source_target_pairs={{0,2},{1,3},{2,0},{3,1},{4,5},{5,4},{6,7},{7,6},{8,10},{9,11},{10,... | collective-permute-start | bytes 884744 | tf_op jit(solution)/shard_map/ppermute | solution.py:571
  151.2 10.1 %collective-permute-start.28 = (bf16[2,2,2,96,768]{4,3,2,1,0:T(8,128)(2,1)S(1)}, bf16[2,2,2,96,768]{4,3,2,1,0:T(8,128)(2,1)S(1)}, u32[]{:S(2)}, u32[]{:S(2)}) collective-permute-start(bf16[2,2,2,96,768]{4,3,2,1,0:T(8,128)(2,1)S(1)} %get-tuple-element.182), channel_id=1, source_target_pairs={{0,4},{1,5},{2,6},{3,7},{4,0},{5,1},{6,2},{7,3},{8,12},{9,13},{10,... | collective-permute-start | bytes 3538952 | tf_op jit(solution)/shard_map/ppermute | solution.py:571
  151.3 9.9 %collective-permute-start.29 = (bf16[4,96,768]{2,1,0:T(8,128)(2,1)S(1)}, bf16[4,96,768]{2,1,0:T(8,128)(2,1)S(1)}, u32[]{:S(2)}, u32[]{:S(2)}) collective-permute-start(bf16[4,96,768]{2,1,0:T(8,128)(2,1)S(1)} %fusion.15), channel_id=1, source_target_pairs={{0,16},{1,17},{2,18},{3,19},{4,12},{5,13},{6,14},{7,15},{8,24},{9,... | collective-permute-start | bytes 1769480 | tf_op jit(solution)/shard_map/ppermute | solution.py:571
  153.0 6.7 %collective-permute-start.30 = (bf16[1,96,768]{2,1,0:T(8,128)(2,1)S(1)}, bf16[1,96,768]{2,1,0:T(8,128)(2,1)S(1)}, u32[]{:S(2)}, u32[]{:S(2)}) collective-permute-start(bf16[1,96,768]{2,1,0:T(8,128)(2,1)S(1)} %slice_bitcast_fusion.19), channel_id=1, source_target_pairs={{0,1},{1,0},{2,3},{3,2},{4,6},{5,7},{6,4},{7,5},{8,9},{9,8},{10,11... | collective-permute-start | bytes 442376 | tf_op jit(solution)/shard_map/ppermute | solution.py:571
  153.1 3.7 %collective-permute-start.31 = (f32[16,768]{1,0:T(8,128)S(1)}, f32[16,768]{1,0:T(8,128)S(1)}, u32[]{:S(2)}, u32[]{:S(2)}) collective-permute-start(f32[16,768]{1,0:T(8,128)S(1)} %get-tuple-element.189), channel_id=1, source_target_pairs={{0,4},{1,5},{2,6},{3,7},{4,0},{5,1},{6,2},{7,3},{8,12},{9,13},{10,... | collective-permute-start | bytes 147464 | tf_op jit(solution)/shard_map/ppermute | solution.py:571
  162.1 16.5 %collective-permute-start.32 = (bf16[784,768]{1,0:T(8,128)(2,1)S(1)}, bf16[784,768]{1,0:T(8,128)(2,1)S(1)}, u32[]{:S(2)}, u32[]{:S(2)}) collective-permute-start(bf16[784,768]{1,0:T(8,128)(2,1)S(1)} %pad_maximum_fusion), channel_id=1, source_target_pairs={{0,8},{1,9},{2,10},{3,11},{4,20},{5,21},{6,22},{7,23},{8,0},{9,1},... | collective-permute-start | bytes 3612680 | tf_op jit(solution)/shard_map/ppermute | solution.py:571
  163.0 10.8 %collective-permute-start.33 = (bf16[1,2,96,768]{3,2,1,0:T(8,128)(2,1)S(1)}, bf16[1,2,96,768]{3,2,1,0:T(8,128)(2,1)S(1)}, u32[]{:S(2)}, u32[]{:S(2)}) collective-permute-start(bf16[1,2,96,768]{3,2,1,0:T(8,128)(2,1)S(1)} %fusion.19), channel_id=1, source_target_pairs={{0,2},{1,3},{2,0},{3,1},{4,5},{5,4},{6,7},{7,6},{8,10},{9,11},{10,... | collective-permute-start | bytes 884744 | tf_op jit(solution)/shard_map/ppermute | solution.py:571
  178.7 13.0 %copy-start.16 = (bf16[784,768]{1,0:T(8,128)(2,1)}, bf16[784,768]{1,0:T(8,128)(2,1)S(1)}, u32[]{:S(2)}) copy-start(bf16[784,768]{1,0:T(8,128)(2,1)S(1)} %collective-permute-done.32) | copy-start | bytes 3612676
  178.9 10.2 %collective-permute-start.34 = (bf16[400,768]{1,0:T(8,128)(2,1)S(1)}, bf16[400,768]{1,0:T(8,128)(2,1)S(1)}, u32[]{:S(2)}, u32[]{:S(2)}) collective-permute-start(bf16[400,768]{1,0:T(8,128)(2,1)S(1)} %pad_maximum_fusion.7), channel_id=1, source_target_pairs={{0,16},{1,17},{2,18},{3,19},{4,12},{5,13},{6,14},{7,15},{8,24},{9,... | collective-permute-start | bytes 1843208 | tf_op jit(solution)/shard_map/ppermute | solution.py:571
  180.6 5.9 %collective-permute-start.35 = (bf16[1,96,768]{2,1,0:T(8,128)(2,1)S(1)}, bf16[1,96,768]{2,1,0:T(8,128)(2,1)S(1)}, u32[]{:S(2)}, u32[]{:S(2)}) collective-permute-start(bf16[1,96,768]{2,1,0:T(8,128)(2,1)S(1)} %slice_bitcast_fusion.18), channel_id=1, source_target_pairs={{0,1},{1,0},{2,3},{3,2},{4,6},{5,7},{6,4},{7,5},{8,9},{9,8},{10,11... | collective-permute-start | bytes 442376 | tf_op jit(solution)/shard_map/ppermute | solution.py:571
  189.3 17.5 %collective-permute-start.39 = (bf16[2,96,768]{2,1,0:T(8,128)(2,1)S(1)}, bf16[2,96,768]{2,1,0:T(8,128)(2,1)S(1)}, u32[]{:S(2)}, u32[]{:S(2)}) collective-permute-start(bf16[2,96,768]{2,1,0:T(8,128)(2,1)S(1)} %get-tuple-element.247), channel_id=1, source_target_pairs={{0,8},{1,9},{2,10},{3,11},{4,12},{5,13},{6,14},{7,15},{8,0},{9,1},... | collective-permute-start | bytes 884744 | tf_op jit(solution)/shard_map/ppermute | solution.py:571
  189.9 16.8 %collective-permute-start.40 = (bf16[2,96,768]{2,1,0:T(8,128)(2,1)S(1)}, bf16[2,96,768]{2,1,0:T(8,128)(2,1)S(1)}, u32[]{:S(2)}, u32[]{:S(2)}) collective-permute-start(bf16[2,96,768]{2,1,0:T(8,128)(2,1)S(1)} %get-tuple-element.247), channel_id=1, source_target_pairs={{0,16},{1,17},{2,18},{3,19},{4,20},{5,21},{6,22},{7,23},{8,24},{9,... | collective-permute-start | bytes 884744 | tf_op jit(solution)/shard_map/ppermute | solution.py:571
  192.0 9.2 %collective-permute-start.36 = (bf16[112,768]{1,0:T(8,128)(2,1)S(1)}, bf16[112,768]{1,0:T(8,128)(2,1)S(1)}, u32[]{:S(2)}, u32[]{:S(2)}) collective-permute-start(bf16[112,768]{1,0:T(8,128)(2,1)S(1)} %get-tuple-element.253), channel_id=1, source_target_pairs={{0,3},{1,2},{2,1},{3,0},{4,7},{5,6},{6,5},{7,4},{8,11},{9,10},{10,... | collective-permute-start | bytes 516104 | tf_op jit(solution)/shard_map/ppermute | solution.py:571
  194.3 12.5 %collective-permute-start.37 = (bf16[112,768]{1,0:T(8,128)(2,1)S(1)}, bf16[112,768]{1,0:T(8,128)(2,1)S(1)}, u32[]{:S(2)}, u32[]{:S(2)}) collective-permute-start(bf16[112,768]{1,0:T(8,128)(2,1)S(1)} %get-tuple-element.252), channel_id=1, source_target_pairs={{0,2},{1,3},{2,0},{3,1},{4,6},{5,7},{6,4},{7,5},{8,10},{9,11},{10,... | collective-permute-start | bytes 516104 | tf_op jit(solution)/shard_map/ppermute | solution.py:571
  194.3 12.5 %collective-permute-start.38 = (bf16[112,768]{1,0:T(8,128)(2,1)S(1)}, bf16[112,768]{1,0:T(8,128)(2,1)S(1)}, u32[]{:S(2)}, u32[]{:S(2)}) collective-permute-start(bf16[112,768]{1,0:T(8,128)(2,1)S(1)} %get-tuple-element.251), channel_id=1, source_target_pairs={{0,1},{1,0},{2,3},{3,2},{4,5},{5,4},{6,7},{7,6},{8,9},{9,8},{10,11... | collective-permute-start | bytes 516104 | tf_op jit(solution)/shard_map/ppermute | solution.py:571
  206.9 13.0 %collective-permute-start.45 = (bf16[3,2,96,768]{3,2,1,0:T(8,128)(2,1)S(1)}, bf16[3,2,96,768]{3,2,1,0:T(8,128)(2,1)S(1)}, u32[]{:S(2)}, u32[]{:S(2)}) collective-permute-start(bf16[3,2,96,768]{3,2,1,0:T(8,128)(2,1)S(1)} %pad_maximum_fusion.6.held), channel_id=1, source_target_pairs={{0,4},{1,5},{2,6},{3,7},{4,0},{5,1},{6,2},{7,3},{8,12},{9,13},{10,... | collective-permute-start | bytes 2654216 | tf_op jit(solution)/shard_map/ppermute | solution.py:571
  207.0 12.9 %collective-permute-start.44 = (bf16[2,96,768]{2,1,0:T(8,128)(2,1)S(1)}, bf16[2,96,768]{2,1,0:T(8,128)(2,1)S(1)}, u32[]{:S(2)}, u32[]{:S(2)}) collective-permute-start(bf16[2,96,768]{2,1,0:T(8,128)(2,1)S(1)} %broadcast_select_fusion), channel_id=1, source_target_pairs={{0,8},{1,9},{2,10},{3,11},{4,20},{5,21},{6,22},{7,23},{8,0},{9,1},... | collective-permute-start | bytes 884744 | tf_op jit(solution)/shard_map/ppermute | solution.py:571
  208.4 9.9 %collective-permute-start.41 = (bf16[96,768]{1,0:T(8,128)(2,1)S(1)}, bf16[96,768]{1,0:T(8,128)(2,1)S(1)}, u32[]{:S(2)}, u32[]{:S(2)}) collective-permute-start(bf16[96,768]{1,0:T(8,128)(2,1)S(1)} %fusion.26.refs_0_), channel_id=1, source_target_pairs={{0,8},{1,9},{2,10},{3,11},{4,12},{5,13},{6,14},{7,15},{8,0},{9,1},... | collective-permute-start | bytes 442376 | tf_op jit(solution)/shard_map/ppermute | solution.py:571
  209.2 9.0 %collective-permute-start.42 = (bf16[96,768]{1,0:T(8,128)(2,1)S(1)}, bf16[96,768]{1,0:T(8,128)(2,1)S(1)}, u32[]{:S(2)}, u32[]{:S(2)}) collective-permute-start(bf16[96,768]{1,0:T(8,128)(2,1)S(1)} %fusion.26.refs_0_), channel_id=1, source_target_pairs={{0,16},{1,17},{2,18},{3,19},{4,20},{5,21},{6,22},{7,23},{8,24},{9,... | collective-permute-start | bytes 442376 | tf_op jit(solution)/shard_map/ppermute | solution.py:571
  209.6 10.3 %collective-permute-start.43 = (bf16[96,768]{1,0:T(8,128)(2,1)S(1)}, bf16[96,768]{1,0:T(8,128)(2,1)S(1)}, u32[]{:S(2)}, u32[]{:S(2)}) collective-permute-start(bf16[96,768]{1,0:T(8,128)(2,1)S(1)} %fusion.26.refs_0_), channel_id=1, source_target_pairs={{0,24},{1,25},{2,26},{3,27},{4,28},{5,29},{6,30},{7,31},{8,16},{9,... | collective-permute-start | bytes 442376 | tf_op jit(solution)/shard_map/ppermute | solution.py:571
  218.3 3.9 %collective-permute-start.46 = (bf16[96,768]{1,0:T(8,128)(2,1)S(1)}, bf16[96,768]{1,0:T(8,128)(2,1)S(1)}, u32[]{:S(2)}, u32[]{:S(2)}) collective-permute-start(bf16[96,768]{1,0:T(8,128)(2,1)S(1)} %fusion.26.refs_0_), channel_id=1, source_target_pairs={{0,4},{1,5},{2,6},{3,7},{4,0},{5,1},{6,2},{7,3},{8,12},{9,13},{10,... | collective-permute-start | bytes 442376 | tf_op jit(solution)/shard_map/ppermute | solution.py:571
  219.9 4.4 %collective-permute-start.50 = (bf16[2,96,768]{2,1,0:T(8,128)(2,1)S(1)}, bf16[2,96,768]{2,1,0:T(8,128)(2,1)S(1)}, u32[]{:S(2)}, u32[]{:S(2)}) collective-permute-start(bf16[2,96,768]{2,1,0:T(8,128)(2,1)S(1)} %collective-permute-done.44.corner), channel_id=1, source_target_pairs={{0,4},{1,5},{2,6},{3,7},{4,0},{5,1},{6,2},{7,3},{8,12},{9,13},{10,... | collective-permute-start | bytes 884744 | tf_op jit(solution)/shard_map/ppermute | solution.py:571
  219.9 2.2 collective-permute-start.47
  220.4 1.7 collective-permute-start.48
  220.5 1.7 collective-permute-start.49
  (17 other events, 99.4 us)
where the time goes:
time: 232 us; the launch traced here: 228 us
  waiting for transfers between devices  105 us (45%)
  Pallas kernels  67.7 us (29%)
  starting transfers between devices  37.8 us (16%)
  other arithmetic  9.65 us (4%)
  local copies, waits for them, and re-layouts  5.87 us (3%)
    ppermute x51, waiting for transfers between devices, move(): return lax.ppermute(array, ('dp', 'tensor'), pairs)  105 us
    ppermute x51, starting transfers between devices, move(): return lax.ppermute(array, ('dp', 'tensor'), pairs)  37.8 us
    pallas_call x2, Pallas kernels, attn_back(): pl.pallas_call(partial(attn_back_kernel, first), in_specs=[smem()] + [vme...  16.1 us
    pallas_call x1, Pallas kernels, ffn_back(): pl.pallas_call(ffn_back_kernel, in_specs=[smem()] + [vmem()] * 10, out_sp...  10.5 us
    pallas_call x1, Pallas kernels, ffn_down(): pl.pallas_call(ffn_down_kernel, in_specs=[smem()] + [vmem()] * (5 + 6) +...  9.85 us
    pallas_call x1, Pallas kernels, attn_rest(): pl.pallas_call(attn_rest_kernel, in_specs=[smem()] + [vmem()] * 8, out_sp...  9.22 us
    pallas_call x1, Pallas kernels, ffn_up(): pl.pallas_call(ffn_up_kernel, in_specs=[smem()] + [vmem()] * (3 + 6) + [h...  8.66 us
  transfers between devices with their start and end apart: 51, of which 31 were waited for; matrix products, arithmetic and copies ran while one was open for 3% of the time, Pallas kernels for 24%

commit v1 on v0

--- a/solution.py
+++ b/solution.py
@@ -502,28 +502,62 @@
     )(grad, joint_a, joint_b, *weights, rest_w)
 
 
-def finish_ffn_kernel(info, held, held_mates, corner, corner_mate, down, up):
-    rows = corner.shape[1]
-    for s, (pieces, last) in enumerate(((held, corner), (held_mates, corner_mate))):
+def finish_ffn_kernel(info, held, held_mates, down, up, mark):
+    rows = held.shape[2]
+    mark[...] = jnp.zeros(mark.shape, wide)
+    for s, pieces in enumerate((held, held_mates)):
         holder = info[1] ^ s
-        for move in range(4):
-            source = last if move == 3 else pieces.at[move]
+        for move in range(3):
             start = pl.multiple_of((holder * 4 + (info[2] ^ move)) * rows, rows)
-            down[pl.ds(start, rows), :] = source[0].astype(wide)
-            up[pl.ds(start, rows), :] = source[1].astype(wide)
-
-
-def finish_ffn(info, *pieces):
-    _, rows, cols = pieces[-1].shape
+            down[pl.ds(start, rows), :] = pieces[move, 0].astype(wide)
+            up[pl.ds(start, rows), :] = pieces[move, 1].astype(wide)
+        start = pl.multiple_of((holder * 4 + (info[2] ^ 3)) * rows, rows)
+        down[pl.ds(start, rows), :] = jnp.zeros((rows, down.shape[1]), wide)
+        up[pl.ds(start, rows), :] = jnp.zeros((rows, up.shape[1]), wide)
+
+
+def finish_ffn(info, held, mates):
+    _, _, rows, cols = held.shape
     return pl.pallas_call(
         finish_ffn_kernel,
-        in_specs=[smem()] + [vmem()] * 4,
-        out_specs=[vmem()] * 2,
-        out_shape=[shaped((GROUP * rows, cols), wide)] * 2,
+        in_specs=[smem()] + [vmem()] * 2,
+        out_specs=[vmem()] * 3,
+        out_shape=[shaped((GROUP * rows, cols), wide)] * 2 + [shaped((8, 128), wide)],
         compiler_params=params(),
         cost_estimate=cost(3),
         name="finish_ffn",
-    )(info, *pieces)
+    )(info, held, mates)
+
+
+def finish_ffn_corner_kernel(info, corner, corner_mate, mark, down_in, up_in, down, up, ready, sems):
+    rows = corner.shape[1]
+    copies = []
+    for s, pieces in enumerate((corner, corner_mate)):
+        holder = info[1] ^ s
+        start = pl.multiple_of((holder * 4 + (info[2] ^ 3)) * rows, rows)
+        for i, target in enumerate((down, up)):
+            ready[s, i] = pieces[i].astype(wide)
+            copies.append(
+                pltpu.make_async_copy(ready.at[s, i], target.at[pl.ds(start, rows), :], sems.at[s, i])
+            )
+            copies[-1].start()
+    for copy in copies:
+        copy.wait()
+
+
+def finish_ffn_corner(info, corner, corner_mate, mark, down, up):
+    _, rows, cols = corner.shape
+    return pl.pallas_call(
+        finish_ffn_corner_kernel,
+        in_specs=[smem()] + [vmem()] * 2 + [hbm()] * 3,
+        out_specs=[hbm()] * 2,
+        out_shape=[shaped(down.shape, wide)] * 2,
+        scratch_shapes=[pltpu.VMEM((2, 2, rows, cols), wide), pltpu.SemaphoreType.DMA((2, 2))],
+        input_output_aliases={4: 0, 5: 1},
+        compiler_params=params(),
+        cost_estimate=cost(1),
+        name="finish_ffn_corner",
+    )(info, corner, corner_mate, mark, down, up)
 
 
 def finish_attn_kernel(info, *refs):
@@ -644,15 +678,15 @@
     vec = jnp.stack([b_out, ln1_gain, ln1_bias, b_down, ln2_gain, ln2_bias, b_down, b_down])
     vec = vec.astype(wide)
     a1, d1 = links.line(a0, 0), links.line(d0, 0)
-    a1, d1, u0, vec, tokens_in = after(a1, d1, u0, vec, tokens)
+    a1, u0, vec, tokens_in = after(a1, u0, vec, tokens)
     a2 = links.line(jnp.stack([a0, a1]), 1)
     u1 = links.line(u0, 0)
     own = list(attn_own(info, tokens_in, attn_w[:3], bias_own.astype(wide)[None, None]))
-    a2, u1, own[2] = after(a2, u1, own[2])
+    a2, u1, d1, own[2] = after(a2, u1, d1, own[2])
     a3 = jnp.concatenate([a1[None], a2])
     a4 = links.plane(a3, 0)
     u2 = links.line(jnp.stack([u0, u1]), 1)
-    a4, u2, d1 = after(a4, u2, d1)
+    a4, d1 = after(a4, d1)
     u3 = jnp.concatenate([u1[None], u2])
     bias_rest = u3[:, rows:].reshape(parts - 1, 8 * width)[:, : bias_own.size]
     near, far = bias_rest[0], bias_rest[1]
@@ -773,13 +807,11 @@
     around = links.everywhere(sum_a, (2, 4, 6))
     f_xy = links.plane(jnp.where(is_odd, f_x, f_y), 0)
     held = jnp.stack([sum_f, f_x, f_y])
-    held_mates = links.core(held)
+    *early, mark = finish_ffn(info, held, links.core(held))
     pair = lax.dynamic_index_in_dim(small, 10 + me, 0, keepdims=False)
     grad_b_up = lax.dynamic_index_in_dim(small, 6 + me, 0, keepdims=False)
-    around, small, pair, grad_b_up, f_xy, held_mates = after(
-        around, small, pair, grad_b_up, f_xy, held_mates
-    )
-    grad_w_down, grad_w_up = finish_ffn(info, held, held_mates, f_xy, links.core(f_xy))
+    around, small, pair, grad_b_up, mark = after(around, small, pair, grad_b_up, mark)
+    grad_w_down, grad_w_up = finish_ffn_corner(info, f_xy, links.core(f_xy), mark, *early)
     grad_w_query, grad_w_key, grad_w_value, grad_w_out = finish_attn(info, mates([sum_a] + around))
     grad_w_query, grad_w_key, grad_w_value = grad_w_query.T, grad_w_key.T, grad_w_value.T
     return (

time: 232 us -> 226 us (0.974)
  waiting for transfers between devices: 105 us -> 95.3 us
  starting transfers between devices: 37.8 us -> 40.3 us
    ppermute x51, waiting for transfers between devices: 105 us -> 95.3 us  [move(): return lax.ppermute(array, ('dp', 'tensor'), pairs)]
    ppermute x51, starting transfers between devices: 37.8 us -> 40.3 us  [move(): return lax.ppermute(array, ('dp', 'tensor'), pairs)]
  transfers between devices with their start and end apart: 51 -> 51, of which waited for: 31 -> 30; matrix products, arithmetic and copies ran while one was open for 3% -> 4% of each run, Pallas kernels for 24% -> 26%
where the time goes in v1:
time: 226 us; the launch traced here: 222 us
  waiting for transfers between devices  95.3 us (42%)
  Pallas kernels  69.3 us (31%)
  starting transfers between devices  40.3 us (18%)
  other arithmetic  9.65 us (4%)
  local copies, waits for them, and re-layouts  5.87 us (3%)
    ppermute x51, waiting for transfers between devices, move(): return lax.ppermute(array, ('dp', 'tensor'), pairs)  95.3 us
    ppermute x51, starting transfers between devices, move(): return lax.ppermute(array, ('dp', 'tensor'), pairs)  40.3 us
    pallas_call x2, Pallas kernels, attn_back(): pl.pallas_call(partial(attn_back_kernel, first), in_specs=[smem()] + [vme...  16.1 us
    pallas_call x1, Pallas kernels, ffn_back(): pl.pallas_call(ffn_back_kernel, in_specs=[smem()] + [vmem()] * 10, out_sp...  10.5 us
    pallas_call x1, Pallas kernels, ffn_down(): pl.pallas_call(ffn_down_kernel, in_specs=[smem()] + [vmem()] * (5 + 6) +...  9.86 us
    pallas_call x1, Pallas kernels, attn_rest(): pl.pallas_call(attn_rest_kernel, in_specs=[smem()] + [vmem()] * 8, out_sp...  9.22 us
    pallas_call x1, Pallas kernels, ffn_up(): pl.pallas_call(ffn_up_kernel, in_specs=[smem()] + [vmem()] * (3 + 6) + [h...  8.66 us
  transfers between devices with their start and end apart: 51, of which 30 were waited for; matrix products, arithmetic and copies ran while one was open for 4% of the time, Pallas kernels for 26%

profile of v1, /device:TPU:0, one launch (start us, length us, event | category | flops | bytes accessed | tf_op | source)
XLA Modules:
  0.0 222.3 jit_solution(14492388688794572465)
XLA Ops:
  0.8 1.3 fusion.27
  2.2 3.1 %collective-permute-start = (bf16[96,768]{1,0:T(8,128)(2,1)S(1)}, bf16[96,768]{1,0:T(8,128)(2,1)S(1)}, u32[]{:S(2)}, u32[]{:S(2)}) collective-permute-start(bf16[96,768]{1,0:T(8,128)(2,1)S(1)} %fusion.27), channel_id=1, source_target_pairs={{0,1},{1,0},{2,3},{3,2},{4,6},{5,7},{6,4},{7,5},{8,9},{9,8},{10,11... | collective-permute-start | bytes 442376 | tf_op jit(solution)/shard_map/ppermute | solution.py:605
  5.2 0.9 constant_dynamic-slice_fusion
  6.3 0.9 constant_dynamic-slice_fusion.1
  7.8 0.7 pad_add_fusion.info
  9.6 2.5 %collective-permute-start.1 = (bf16[2,96,768]{2,1,0:T(8,128)(2,1)S(1)}, bf16[2,96,768]{2,1,0:T(8,128)(2,1)S(1)}, u32[]{:S(2)}, u32[]{:S(2)}) collective-permute-start(bf16[2,96,768]{2,1,0:T(8,128)(2,1)S(1)} %pad_maximum_fusion.11), channel_id=1, source_target_pairs={{0,2},{1,3},{2,0},{3,1},{4,5},{5,4},{6,7},{7,6},{8,10},{9,11},{10,... | collective-permute-start | bytes 884744 | tf_op jit(solution)/shard_map/ppermute | solution.py:605
  12.1 2.5 %collective-permute-start.2 = (bf16[104,768]{1,0:T(8,128)(2,1)S(1)}, bf16[104,768]{1,0:T(8,128)(2,1)S(1)}, u32[]{:S(2)}, u32[]{:S(2)}) collective-permute-start(bf16[104,768]{1,0:T(8,128)(2,1)S(1)} %pad_maximum_fusion.17), channel_id=1, source_target_pairs={{0,1},{1,0},{2,3},{3,2},{4,6},{5,7},{6,4},{7,5},{8,9},{9,8},{10,11... | collective-permute-start | bytes 479240 | tf_op jit(solution)/shard_map/ppermute | solution.py:605
  14.7 3.0 %attn_own.1 = (bf16[1,576,512]{2,1,0:T(8,128)(2,1)S(1)}, bf16[1,192,512]{2,1,0:T(8,128)(2,1)S(1)}, f32[1,8,512]{2,1,0:T(8,128)S(1)}) custom-call(s32[4]{0:T(128)S(1)} %pad_add_fusion.info, bf16[512,768]{1,0:T(8,128)(2,1)S(1)} %copy-done.7, bf16[192,768]{1,0:T(8,128)(2,1)S(1)} %bitcast.167, bf16[192,768]{1,0:T(8,128)(2,1)S(1)} %bitcast.169, ...), custom_call_target="tpu_custom_call" | custom-call | flops 4400000000 | bytes 1048576 | tf_op jit(solution)/shard_map/attn_own/pallas_call | solution.py:162
  17.7 0.8 copy-done.9
  18.5 3.8 %collective-permute-done.2 = bf16[104,768]{1,0:T(8,128)(2,1)S(1)} collective-permute-done((bf16[104,768]{1,0:T(8,128)(2,1)S(1)}, bf16[104,768]{1,0:T(8,128)(2,1)S(1)}, u32[]{:S(2)}, u32[]{:S(2)}) %collective-permute-start.2) | collective-permute-done | bytes 159776 | tf_op jit(solution)/shard_map/ppermute | solution.py:605
  22.3 1.6 collective-permute-done.1
  23.9 0.8 fusion.35
  24.7 1.9 collective-permute-start.4
  26.6 0.8 pad_maximum_fusion.10
  28.1 10.9 %collective-permute-done.6 = bf16[2,104,768]{2,1,0:T(8,128)(2,1)S(1)} collective-permute-done((bf16[2,104,768]{2,1,0:T(8,128)(2,1)}, bf16[2,104,768]{2,1,0:T(8,128)(2,1)S(1)}, u32[]{:S(2)}, u32[]{:S(2)}) %collective-permute-start.6) | collective-permute-done | bytes 319520 | tf_op jit(solution)/shard_map/ppermute | solution.py:605
  39.8 1.6 collective-permute-start.5
  42.2 9.9 %collective-permute-done.8 = bf16[2,96,768]{2,1,0:T(8,128)(2,1)S(1)} collective-permute-done((bf16[2,96,768]{2,1,0:T(8,128)(2,1)S(1)}, bf16[2,96,768]{2,1,0:T(8,128)(2,1)S(1)}, u32[]{:S(2)}, u32[]{:S(2)}) %collective-permute-start.8) | collective-permute-done | bytes 294944 | tf_op jit(solution)/shard_map/ppermute | solution.py:605
  52.1 1.3 collective-permute-done.5.refs_2_
  54.1 1.0 collective-permute-start.12
  55.8 0.7 collective-permute-done.9.refs_3_
  57.2 9.2 %attn_rest.1 = (bf16[3,576,512]{2,1,0:T(8,128)(2,1)S(1)}, bf16[3,768,768]{2,1,0:T(8,128)(2,1)S(1)}, bf16[3,192,512]{2,1,0:T(8,128)(2,1)S(1)}, f32[3,8,512]{2,1,0:T(8,128)S(1)}, bf16[3,192,768]{2,1,0:T(8,128)(2,1)S(1)}) custom-call(s32[4]{0:T(128)S(1)} %pad_add_fusion.info, bf16[512,768]{1,0:T(8,128)(2,1)S(1)} %copy-done.8, ...), custom_call_target="tpu_custom_call" | custom-call | flops 8800000000 | bytes 1048576 | tf_op jit(solution)/shard_map/attn_rest/pallas_call | solution.py:204
  66.4 1.6 ffn_in.1
  68.4 3.3 %collective-permute-done.12.refs_2_ = bf16[2,3,96,768]{3,2,1,0:T(8,128)(2,1)S(1)} collective-permute-done((bf16[2,3,96,768]{3,2,1,0:T(8,128)(2,1)S(1)}, bf16[2,3,96,768]{3,2,1,0:T(8,128)(2,1)S(1)}, u32[]{:S(2)}, u32[]{:S(2)}) %collective-permute-start.12) | collective-permute-done | bytes 884768 | tf_op jit(solution)/shard_map/ppermute | solution.py:605
  72.3 1.2 collective-permute-start.17
  73.5 1.2 collective-permute-done.14.refs_3_
  75.4 8.7 %ffn_up.1 = (bf16[4,512,768]{2,1,0:T(8,128)(2,1)S(1)}, bf16[4,512,768]{2,1,0:T(8,128)(2,1)S(1)}, bf16[4,768,768]{2,1,0:T(8,128)(2,1)S(1)}, f32[8,128]{1,0:T(8,128)S(1)}) custom-call(s32[4]{0:T(128)S(1)} %pad_add_fusion.info, bf16[512,768]{1,0:T(8,128)(2,1)S(1)} %get-tuple-element.138.normed.normed_low, f32[4,1,1152]{2,1,0:T(1,128)S(1)} %maximum_convert_fusion.bias, ...), custom_call_target="tpu_custom_call" | custom-call | flops 12099999744 | bytes 1048576 | tf_op jit(solution)/shard_map/ffn_up/pallas_call | solution.py:280
  84.0 1.3 collective-permute-done.17.refs_2_
  85.9 2.5 %collective-permute-done.18.refs_3_ = bf16[3,96,768]{2,1,0:T(8,128)(2,1)S(1)} collective-permute-done((bf16[3,96,768]{2,1,0:T(8,128)(2,1)S(1)}, bf16[3,96,768]{2,1,0:T(8,128)(2,1)S(1)}, u32[]{:S(2)}, u32[]{:S(2)}) %collective-permute-start.18) | collective-permute-done | bytes 442400 | tf_op jit(solution)/shard_map/ppermute | solution.py:605
  89.1 9.9 %ffn_down.1 = (bf16[512,768]{1,0:T(8,128)(2,1)}, f32[512,768]{1,0:T(8,128)S(1)}, bf16[512,768]{1,0:T(8,128)(2,1)S(1)}, f32[16,768]{1,0:T(8,128)S(1)}, bf16[2,2,4...) custom-call(s32[4]{0:T(128)S(1)} %pad_add_fusion.info, ...), custom_call_target="tpu_custom_call" | custom-call | flops 13200000000 | bytes 1048576 | tf_op jit(solution)/shard_map/ffn_down/pallas_call | solution.py:337
  99.1 4.4 %collective-permute-done.21 = bf16[2,2,4,96,768]{4,3,2,1,0:T(8,128)(2,1)S(1)} collective-permute-done((bf16[2,2,4,96,768]{4,3,2,1,0:T(8,128)(2,1)S(1)}, bf16[2,2,4,96,768]{4,3,2,1,0:T(8,128)(2,1)S(1)}, u32[]{:S(2)}, u32[]{:S(2)}) %collective-permute-start.21) | collective-permute-done | bytes 2359328 | tf_op jit(solution)/shard_map/ppermute | solution.py:605
  103.5 0.7 add_convert_fusion.4
  104.9 10.5 %ffn_back.1 = (f32[512,768]{1,0:T(8,128)S(1)}, bf16[512,768]{1,0:T(8,128)(2,1)S(1)}, f32[16,768]{1,0:T(8,128)S(1)}, bf16[2,2,4,96,768]{4,3,2,1,0:T(8,128)(2,1)S(1)}, bf16[2,2,4,96,768]{4,3,2,1,0:T(8,128)(2,1)S(1)}) custom-call(s32[4]{0:T(128)S(1)} %pad_add_fusion.info, bf16[512,768]{1,0:T(8,128)(2,1)S(1)} %get-tuple-element.151.branch_low, ...), custom_call_target="tpu_custom_call" | custom-call | flops 12099999744 | bytes 1048576 | tf_op jit(solution)/shard_map/ffn_back/pallas_call | solution.py:392
  115.4 5.1 %collective-permute-done.22 = bf16[2,4,96,768]{3,2,1,0:T(8,128)(2,1)S(1)} collective-permute-done((bf16[2,4,96,768]{3,2,1,0:T(8,128)(2,1)S(1)}, bf16[2,4,96,768]{3,2,1,0:T(8,128)(2,1)S(1)}, u32[]{:S(2)}, u32[]{:S(2)}) %collective-permute-start.22) | collective-permute-done | bytes 1179680 | tf_op jit(solution)/shard_map/ppermute | solution.py:605
  120.6 1.2 collective-permute-start.24
  121.8 7.9 %attn_back.2 = (f32[16,768]{1,0:T(8,128)S(1)}, bf16[2,576,512]{2,1,0:T(8,128)(2,1)S(1)}, bf16[2,2,2,96,768]{4,3,2,1,0:T(8,128)(2,1)S(1)}, bf16[2,2,2,96,768]{4,3,2,1,0:T(8,128)(2,1)S(1)}) custom-call(s32[4]{0:T(128)S(1)} %pad_add_fusion.info, bf16[512,768]{1,0:T(8,128)(2,1)S(1)} %copy-done.8, bf16[512,768]{1,0:T(8,128)(2,1)S(1)} %get-tuple-element.167.residual_low, ...), custom_call_target="tpu_custom_call" | custom-call | flops 9900000256 | bytes 1048576 | tf_op jit(solution)/shard_map/attn_back/pallas_call | solution.py:465
  129.8 0.8 collective-permute-done.24
  130.6 0.7 add_convert_fusion.2
  132.2 1.8 collective-permute-start.27
  134.0 8.2 %attn_back.3 = (f32[16,768]{1,0:T(8,128)S(1)}, bf16[2,576,512]{2,1,0:T(8,128)(2,1)S(1)}, bf16[2,2,2,96,768]{4,3,2,1,0:T(8,128)(2,1)S(1)}, bf16[2,2,2,96,768]{4,3,2,1,0:T(8,128)(2,1)S(1)}) custom-call(s32[4]{0:T(128)S(1)} %pad_add_fusion.info, bf16[512,768]{1,0:T(8,128)(2,1)S(1)} %copy-done.8, bf16[512,768]{1,0:T(8,128)(2,1)S(1)} %get-tuple-element.167.residual_low, ...), custom_call_target="tpu_custom_call" | custom-call | flops 9900000256 | bytes 1048576 | tf_op jit(solution)/shard_map/attn_back/pallas_call | solution.py:465
  142.7 4.9 %collective-permute-done.25 = bf16[2,4,96,768]{3,2,1,0:T(8,128)(2,1)S(1)} collective-permute-done((bf16[2,4,96,768]{3,2,1,0:T(8,128)(2,1)S(1)}, bf16[2,4,96,768]{3,2,1,0:T(8,128)(2,1)S(1)}, u32[]{:S(2)}, u32[]{:S(2)}) %collective-permute-start.25) | collective-permute-done | bytes 1179680 | tf_op jit(solution)/shard_map/ppermute | solution.py:605
  147.7 1.2 collective-permute-start.29
  149.1 1.1 collective-permute-start.31
  150.2 3.6 %grad_tokens.1 = bf16[512,768]{1,0:T(8,128)(2,1)} custom-call(f32[512,768]{1,0:T(8,128)S(1)} %get-tuple-element.185.grad, bf16[2,576,512]{2,1,0:T(8,128)(2,1)S(1)} %get-tuple-element.186.joint_a, bf16[2,576,512]{2,1,0:T(8,128)(2,1)S(1)} %get-tuple-element.187.joint_b, bf16[192,768]{1,0:T(8,128)(2,1)S(1)} %bitcast.168, bf16[192,768]{1,0:T(8,128)(2,1)S(1)} %bitcast.170, ...), custom_call_target="tpu_custom_call" | custom-call | flops 4400000000 | bytes 1048576 | tf_op jit(solution)/shard_map/grad_tokens/pallas_call | solution.py:494
  153.8 2.0 collective-permute-done.30
  155.8 1.9 collective-permute-done.29
  159.4 1.8 collective-permute-start.33
  161.3 8.8 %collective-permute-done.33 = bf16[1,2,96,768]{3,2,1,0:T(8,128)(2,1)S(1)} collective-permute-done((bf16[1,2,96,768]{3,2,1,0:T(8,128)(2,1)S(1)}, bf16[1,2,96,768]{3,2,1,0:T(8,128)(2,1)S(1)}, u32[]{:S(2)}, u32[]{:S(2)}) %collective-permute-start.33) | collective-permute-done | bytes 294944 | tf_op jit(solution)/shard_map/ppermute | solution.py:605
  170.1 5.0 %collective-permute-done.32 = bf16[784,768]{1,0:T(8,128)(2,1)S(1)} collective-permute-done((bf16[784,768]{1,0:T(8,128)(2,1)S(1)}, bf16[784,768]{1,0:T(8,128)(2,1)S(1)}, u32[]{:S(2)}, u32[]{:S(2)}) %collective-permute-start.32) | collective-permute-done | bytes 1204256 | tf_op jit(solution)/shard_map/ppermute | solution.py:605
  175.3 1.2 collective-permute-start.34
  176.8 5.6 %collective-permute-done.35 = bf16[1,96,768]{2,1,0:T(8,128)(2,1)S(1)} collective-permute-done((bf16[1,96,768]{2,1,0:T(8,128)(2,1)S(1)}, bf16[1,96,768]{2,1,0:T(8,128)(2,1)S(1)}, u32[]{:S(2)}, u32[]{:S(2)}) %collective-permute-start.35) | collective-permute-done | bytes 147488 | tf_op jit(solution)/shard_map/ppermute | solution.py:605
  182.4 3.1 %collective-permute-done.34 = bf16[400,768]{1,0:T(8,128)(2,1)S(1)} collective-permute-done((bf16[400,768]{1,0:T(8,128)(2,1)S(1)}, bf16[400,768]{1,0:T(8,128)(2,1)S(1)}, u32[]{:S(2)}, u32[]{:S(2)}) %collective-permute-start.34) | collective-permute-done | bytes 614432 | tf_op jit(solution)/shard_map/ppermute | solution.py:605
  186.3 1.2 collective-permute-start.40
  187.9 2.2 %collective-permute-start.36 = (bf16[112,768]{1,0:T(8,128)(2,1)S(1)}, bf16[112,768]{1,0:T(8,128)(2,1)S(1)}, u32[]{:S(2)}, u32[]{:S(2)}) collective-permute-start(bf16[112,768]{1,0:T(8,128)(2,1)S(1)} %get-tuple-element.255), channel_id=1, source_target_pairs={{0,3},{1,2},{2,1},{3,0},{4,7},{5,6},{6,5},{7,4},{8,11},{9,10},{10,... | collective-permute-start | bytes 516104 | tf_op jit(solution)/shard_map/ppermute | solution.py:605
  190.1 2.2 collective-permute-start.38
  192.4 4.7 %collective-permute-done.36 = bf16[112,768]{1,0:T(8,128)(2,1)S(1)} collective-permute-done((bf16[112,768]{1,0:T(8,128)(2,1)S(1)}, bf16[112,768]{1,0:T(8,128)(2,1)S(1)}, u32[]{:S(2)}, u32[]{:S(2)}) %collective-permute-start.36) | collective-permute-done | bytes 172064 | tf_op jit(solution)/shard_map/ppermute | solution.py:605
  197.1 5.6 %collective-permute-done.37 = bf16[112,768]{1,0:T(8,128)(2,1)S(1)} collective-permute-done((bf16[112,768]{1,0:T(8,128)(2,1)S(1)}, bf16[112,768]{1,0:T(8,128)(2,1)S(1)}, u32[]{:S(2)}, u32[]{:S(2)}) %collective-permute-start.37) | collective-permute-done | bytes 172064 | tf_op jit(solution)/shard_map/ppermute | solution.py:605
  202.9 1.5 collective-permute-start.49
  205.1 0.9 collective-permute-start.42
  206.0 2.0 collective-permute-start.43
  208.0 0.8 convert_add_fusion.12
  209.4 3.2 %collective-permute-done.49.corner = bf16[2,96,768]{2,1,0:T(8,128)(2,1)S(1)} collective-permute-done((bf16[2,96,768]{2,1,0:T(8,128)(2,1)S(1)}, bf16[2,96,768]{2,1,0:T(8,128)(2,1)S(1)}, u32[]{:S(2)}, u32[]{:S(2)}) %collective-permute-start.49) | collective-permute-done | bytes 294944 | tf_op jit(solution)/shard_map/ppermute | solution.py:605
  213.1 3.0 %finish_ffn.1 = (f32[768,768]{1,0:T(8,128)}, f32[768,768]{1,0:T(8,128)}, f32[8,128]{1,0:T(8,128)S(1)}) custom-call(s32[4]{0:T(128)S(1)} %pad_add_fusion.info, bf16[3,2,96,768]{3,2,1,0:T(8,128)(2,1)S(1)} %pad_maximum_fusion.6.held, bf16[3,2,96,768]{3,2,1,0:T(8,128)(2,1)S(1)} %collective-permute-done.44.held_mates), custom_call_target="tpu_custom_call" | custom-call | flops 3300000000 | bytes 1048576 | tf_op jit(solution)/shard_map/finish_ffn/pallas_call | solution.py:521
  217.4 1.6 finish_ffn_corner.1
  219.7 2.1 finish_attn.1
  (183 shorter events, 18.8 us)
Async XLA Ops:
  0.7 8.0 %copy-start.24 = (bf16[768]{0:T(1024)(128)(2,1)S(1)}, bf16[768]{0:T(1024)(128)(2,1)}, u32[]{:S(2)}) copy-start(bf16[768]{0:T(1024)(128)(2,1)} %param.32) | copy-start | bytes 4612
  0.7 8.0 %copy-start.25 = (bf16[768]{0:T(1024)(128)(2,1)S(1)}, bf16[768]{0:T(1024)(128)(2,1)}, u32[]{:S(2)}) copy-start(bf16[768]{0:T(1024)(128)(2,1)} %param.33) | copy-start | bytes 4612
  0.8 8.1 %copy-start.26 = (bf16[768]{0:T(1024)(128)(2,1)S(1)}, bf16[768]{0:T(1024)(128)(2,1)}, u32[]{:S(2)}) copy-start(bf16[768]{0:T(1024)(128)(2,1)} %param.34) | copy-start | bytes 4612
  0.8 13.9 %copy-start.2 = (bf16[768,192]{0,1:T(8,128)(2,1)S(1)}, bf16[768,192]{0,1:T(8,128)(2,1)}, u32[]{:S(2)}) copy-start(bf16[768,192]{0,1:T(8,128)(2,1)} %param.20) | copy-start | bytes 884740
  0.8 13.9 %copy-start.3 = (bf16[768,192]{0,1:T(8,128)(2,1)S(1)}, bf16[768,192]{0,1:T(8,128)(2,1)}, u32[]{:S(2)}) copy-start(bf16[768,192]{0,1:T(8,128)(2,1)} %param.22) | copy-start | bytes 884740
  0.8 13.9 %copy-start.4 = (bf16[768,192]{0,1:T(8,128)(2,1)S(1)}, bf16[768,192]{0,1:T(8,128)(2,1)}, u32[]{:S(2)}) copy-start(bf16[768,192]{0,1:T(8,128)(2,1)} %param.23) | copy-start | bytes 884740
  0.8 13.8 %copy-start.7 = (bf16[512,768]{1,0:T(8,128)(2,1)S(1)}, bf16[512,768]{1,0:T(8,128)(2,1)}, u32[]{:S(2)}) copy-start(bf16[512,768]{1,0:T(8,128)(2,1)} %tokens.8) | copy-start | bytes 2359300
  2.2 7.4 %collective-permute-start = (bf16[96,768]{1,0:T(8,128)(2,1)S(1)}, bf16[96,768]{1,0:T(8,128)(2,1)S(1)}, u32[]{:S(2)}, u32[]{:S(2)}) collective-permute-start(bf16[96,768]{1,0:T(8,128)(2,1)S(1)} %fusion.27), channel_id=1, source_target_pairs={{0,1},{1,0},{2,3},{3,2},{4,6},{5,7},{6,4},{7,5},{8,9},{9,8},{10,11... | collective-permute-start | bytes 442376 | tf_op jit(solution)/shard_map/ppermute | solution.py:605
  6.2 12.3 %collective-permute-start.3 = (bf16[96,768]{1,0:T(8,128)(2,1)S(1)}, bf16[96,768]{1,0:T(8,128)(2,1)S(1)}, u32[]{:S(2)}, u32[]{:S(2)}) collective-permute-start(bf16[96,768]{1,0:T(8,128)(2,1)S(1)} %constant_dynamic-slice_fusion), channel_id=1, source_target_pairs={{0,1},{1,0},{2,3},{3,2},{4,6},{5,7},{6,4},{7,5},{8,9},{9,8},{10,11... | collective-permute-start | bytes 442376 | tf_op jit(solution)/shard_map/ppermute | solution.py:605
  9.6 14.3 %collective-permute-start.1 = (bf16[2,96,768]{2,1,0:T(8,128)(2,1)S(1)}, bf16[2,96,768]{2,1,0:T(8,128)(2,1)S(1)}, u32[]{:S(2)}, u32[]{:S(2)}) collective-permute-start(bf16[2,96,768]{2,1,0:T(8,128)(2,1)S(1)} %pad_maximum_fusion.11), channel_id=1, source_target_pairs={{0,2},{1,3},{2,0},{3,1},{4,5},{5,4},{6,7},{7,6},{8,10},{9,11},{10,... | collective-permute-start | bytes 884744 | tf_op jit(solution)/shard_map/ppermute | solution.py:605
  12.1 10.2 %collective-permute-start.2 = (bf16[104,768]{1,0:T(8,128)(2,1)S(1)}, bf16[104,768]{1,0:T(8,128)(2,1)S(1)}, u32[]{:S(2)}, u32[]{:S(2)}) collective-permute-start(bf16[104,768]{1,0:T(8,128)(2,1)S(1)} %pad_maximum_fusion.17), channel_id=1, source_target_pairs={{0,1},{1,0},{2,3},{3,2},{4,6},{5,7},{6,4},{7,5},{8,9},{9,8},{10,11... | collective-permute-start | bytes 479240 | tf_op jit(solution)/shard_map/ppermute | solution.py:605
  18.5 9.5 %copy-start = (bf16[768,768]{1,0:T(8,128)(2,1)S(1)}, bf16[768,768]{1,0:T(8,128)(2,1)}, u32[]{:S(2)}) copy-start(bf16[768,768]{1,0:T(8,128)(2,1)} %down_own.1) | copy-start | bytes 3538948
  24.7 14.9 %collective-permute-start.4 = (bf16[3,96,768]{2,1,0:T(8,128)(2,1)S(1)}, bf16[3,96,768]{2,1,0:T(8,128)(2,1)S(1)}, u32[]{:S(2)}, u32[]{:S(2)}) collective-permute-start(bf16[3,96,768]{2,1,0:T(8,128)(2,1)S(1)} %get-tuple-element.247.refs_0_), channel_id=1, source_target_pairs={{0,8},{1,9},{2,10},{3,11},{4,20},{5,21},{6,22},{7,23},{8,0},{9,1},... | collective-permute-start | bytes 1327112 | tf_op jit(solution)/shard_map/ppermute | solution.py:605
  27.4 11.5 %collective-permute-start.6 = (bf16[2,104,768]{2,1,0:T(8,128)(2,1)}, bf16[2,104,768]{2,1,0:T(8,128)(2,1)S(1)}, u32[]{:S(2)}, u32[]{:S(2)}) collective-permute-start(bf16[2,104,768]{2,1,0:T(8,128)(2,1)} %pad_maximum_fusion.10), channel_id=1, source_target_pairs={{0,2},{1,3},{2,0},{3,1},{4,5},{5,4},{6,7},{7,6},{8,10},{9,11},{10,... | collective-permute-start | bytes 958472 | tf_op jit(solution)/shard_map/ppermute | solution.py:605
  28.0 11.7 %copy-start.15 = (bf16[1,3,96,768]{3,2,1,0:T(8,128)(2,1)S(1)}, bf16[1,3,96,768]{3,2,1,0:T(8,128)(2,1)}, u32[]{:S(2)}) copy-start(bf16[1,3,96,768]{3,2,1,0:T(8,128)(2,1)} %get-tuple-element.246) | copy-start | bytes 1327108
  28.0 13.3 %copy-start.14 = (bf16[104,768]{1,0:T(8,128)(2,1)S(1)}, bf16[104,768]{1,0:T(8,128)(2,1)}, u32[]{:S(2)}) copy-start(bf16[104,768]{1,0:T(8,128)(2,1)} %copy-done.13) | copy-start | bytes 479236
  39.8 13.7 %collective-permute-start.5 = (bf16[2,3,96,768]{3,2,1,0:T(8,128)(2,1)S(1)}, bf16[2,3,96,768]{3,2,1,0:T(8,128)(2,1)S(1)}, u32[]{:S(2)}, u32[]{:S(2)}) collective-permute-start(bf16[2,3,96,768]{3,2,1,0:T(8,128)(2,1)S(1)} %pad_maximum_fusion.3), channel_id=1, source_target_pairs={{0,16},{1,17},{2,18},{3,19},{4,12},{5,13},{6,14},{7,15},{8,24},{9,... | collective-permute-start | bytes 2654216 | tf_op jit(solution)/shard_map/ppermute | solution.py:605
  41.4 10.7 %collective-permute-start.7 = (bf16[3,96,768]{2,1,0:T(8,128)(2,1)S(1)}, bf16[3,96,768]{2,1,0:T(8,128)(2,1)S(1)}, u32[]{:S(2)}, u32[]{:S(2)}) collective-permute-start(bf16[3,96,768]{2,1,0:T(8,128)(2,1)S(1)} %fusion.17.refs_0_), channel_id=1, source_target_pairs={{0,8},{1,9},{2,10},{3,11},{4,20},{5,21},{6,22},{7,23},{8,0},{9,1},... | collective-permute-start | bytes 1327112 | tf_op jit(solution)/shard_map/ppermute | solution.py:605
  42.0 10.1 %collective-permute-start.8 = (bf16[2,96,768]{2,1,0:T(8,128)(2,1)S(1)}, bf16[2,96,768]{2,1,0:T(8,128)(2,1)S(1)}, u32[]{:S(2)}, u32[]{:S(2)}) collective-permute-start(bf16[2,96,768]{2,1,0:T(8,128)(2,1)S(1)} %pad_maximum_fusion.12), channel_id=1, source_target_pairs={{0,2},{1,3},{2,0},{3,1},{4,5},{5,4},{6,7},{7,6},{8,10},{9,11},{10,... | collective-permute-start | bytes 884744 | tf_op jit(solution)/shard_map/ppermute | solution.py:605
  53.5 3.7 %collective-permute-start.11 = (bf16[2,3,96,768]{3,2,1,0:T(8,128)(2,1)S(1)}, bf16[2,3,96,768]{3,2,1,0:T(8,128)(2,1)S(1)}, u32[]{:S(2)}, u32[]{:S(2)}) collective-permute-start(bf16[2,3,96,768]{3,2,1,0:T(8,128)(2,1)S(1)} %collective-permute-done.5.refs_2_), channel_id=1, source_target_pairs={{0,4},{1,5},{2,6},{3,7},{4,0},{5,1},{6,2},{7,3},{8,12},{9,13},{10,... | collective-permute-start | bytes 2654216 | tf_op jit(solution)/shard_map/ppermute | solution.py:605
  53.5 3.1 %collective-permute-start.9 = (bf16[3,96,768]{2,1,0:T(8,128)(2,1)S(1)}, bf16[3,96,768]{2,1,0:T(8,128)(2,1)S(1)}, u32[]{:S(2)}, u32[]{:S(2)}) collective-permute-start(bf16[3,96,768]{2,1,0:T(8,128)(2,1)S(1)} %get-tuple-element.247.refs_0_), channel_id=1, source_target_pairs={{0,4},{1,5},{2,6},{3,7},{4,0},{5,1},{6,2},{7,3},{8,12},{9,13},{10,... | collective-permute-start | bytes 1327112 | tf_op jit(solution)/shard_map/ppermute | solution.py:605
  54.0 3.2 %collective-permute-start.10 = (bf16[3,96,768]{2,1,0:T(8,128)(2,1)S(1)}, bf16[3,96,768]{2,1,0:T(8,128)(2,1)S(1)}, u32[]{:S(2)}, u32[]{:S(2)}) collective-permute-start(bf16[3,96,768]{2,1,0:T(8,128)(2,1)S(1)} %collective-permute-done.4.refs_1_), channel_id=1, source_target_pairs={{0,4},{1,5},{2,6},{3,7},{4,0},{5,1},{6,2},{7,3},{8,12},{9,13},{10,... | collective-permute-start | bytes 1327112 | tf_op jit(solution)/shard_map/ppermute | solution.py:605
  54.1 17.6 %collective-permute-start.12 = (bf16[2,3,96,768]{3,2,1,0:T(8,128)(2,1)S(1)}, bf16[2,3,96,768]{3,2,1,0:T(8,128)(2,1)S(1)}, u32[]{:S(2)}, u32[]{:S(2)}) collective-permute-start(bf16[2,3,96,768]{3,2,1,0:T(8,128)(2,1)S(1)} %pad_maximum_fusion.4), channel_id=1, source_target_pairs={{0,16},{1,17},{2,18},{3,19},{4,12},{5,13},{6,14},{7,15},{8,24},{9,... | collective-permute-start | bytes 2654216 | tf_op jit(solution)/shard_map/ppermute | solution.py:605
  55.2 11.2 %copy-start.1 = (bf16[192,768]{1,0:T(8,128)(2,1)S(1)}, bf16[192,768]{1,0:T(8,128)(2,1)}, u32[]{:S(2)}) copy-start(bf16[192,768]{1,0:T(8,128)(2,1)} %refs_0_.1) | copy-start | bytes 884740
  55.2 13.2 %collective-permute-start.13 = (bf16[3,96,768]{2,1,0:T(8,128)(2,1)S(1)}, bf16[3,96,768]{2,1,0:T(8,128)(2,1)S(1)}, u32[]{:S(2)}, u32[]{:S(2)}) collective-permute-start(bf16[3,96,768]{2,1,0:T(8,128)(2,1)S(1)} %get-tuple-element.245.refs_0_), channel_id=1, source_target_pairs={{0,8},{1,9},{2,10},{3,11},{4,20},{5,21},{6,22},{7,23},{8,0},{9,1},... | collective-permute-start | bytes 1327112 | tf_op jit(solution)/shard_map/ppermute | solution.py:605
  71.7 3.7 %collective-permute-start.16 = (bf16[2,3,96,768]{3,2,1,0:T(8,128)(2,1)S(1)}, bf16[2,3,96,768]{3,2,1,0:T(8,128)(2,1)S(1)}, u32[]{:S(2)}, u32[]{:S(2)}) collective-permute-start(bf16[2,3,96,768]{3,2,1,0:T(8,128)(2,1)S(1)} %collective-permute-done.12.refs_2_), channel_id=1, source_target_pairs={{0,4},{1,5},{2,6},{3,7},{4,0},{5,1},{6,2},{7,3},{8,12},{9,13},{10,... | collective-permute-start | bytes 2654216 | tf_op jit(solution)/shard_map/ppermute | solution.py:605
  71.7 3.1 %collective-permute-start.14 = (bf16[3,96,768]{2,1,0:T(8,128)(2,1)S(1)}, bf16[3,96,768]{2,1,0:T(8,128)(2,1)S(1)}, u32[]{:S(2)}, u32[]{:S(2)}) collective-permute-start(bf16[3,96,768]{2,1,0:T(8,128)(2,1)S(1)} %fusion.17.refs_0_), channel_id=1, source_target_pairs={{0,4},{1,5},{2,6},{3,7},{4,0},{5,1},{6,2},{7,3},{8,12},{9,13},{10,... | collective-permute-start | bytes 1327112 | tf_op jit(solution)/shard_map/ppermute | solution.py:605
  72.2 3.2 %collective-permute-start.15 = (bf16[3,96,768]{2,1,0:T(8,128)(2,1)S(1)}, bf16[3,96,768]{2,1,0:T(8,128)(2,1)S(1)}, u32[]{:S(2)}, u32[]{:S(2)}) collective-permute-start(bf16[3,96,768]{2,1,0:T(8,128)(2,1)S(1)} %collective-permute-done.7.refs_1_), channel_id=1, source_target_pairs={{0,4},{1,5},{2,6},{3,7},{4,0},{5,1},{6,2},{7,3},{8,12},{9,13},{10,... | collective-permute-start | bytes 1327112 | tf_op jit(solution)/shard_map/ppermute | solution.py:605
  72.3 13.1 %collective-permute-start.17 = (bf16[2,3,96,768]{3,2,1,0:T(8,128)(2,1)S(1)}, bf16[2,3,96,768]{3,2,1,0:T(8,128)(2,1)S(1)}, u32[]{:S(2)}, u32[]{:S(2)}) collective-permute-start(bf16[2,3,96,768]{3,2,1,0:T(8,128)(2,1)S(1)} %pad_maximum_fusion.5), channel_id=1, source_target_pairs={{0,16},{1,17},{2,18},{3,19},{4,12},{5,13},{6,14},{7,15},{8,24},{9,... | collective-permute-start | bytes 2654216 | tf_op jit(solution)/shard_map/ppermute | solution.py:605
  75.4 13.7 %copy-start.6 = (bf16[512,768]{1,0:T(8,128)(2,1)S(1)}, bf16[512,768]{1,0:T(8,128)(2,1)}, u32[]{:S(2)}) copy-start(bf16[512,768]{1,0:T(8,128)(2,1)} %cot.1) | copy-start | bytes 2359300
  85.4 3.7 %collective-permute-start.20 = (bf16[2,3,96,768]{3,2,1,0:T(8,128)(2,1)S(1)}, bf16[2,3,96,768]{3,2,1,0:T(8,128)(2,1)S(1)}, u32[]{:S(2)}, u32[]{:S(2)}) collective-permute-start(bf16[2,3,96,768]{3,2,1,0:T(8,128)(2,1)S(1)} %collective-permute-done.17.refs_2_), channel_id=1, source_target_pairs={{0,4},{1,5},{2,6},{3,7},{4,0},{5,1},{6,2},{7,3},{8,12},{9,13},{10,... | collective-permute-start | bytes 2654216 | tf_op jit(solution)/shard_map/ppermute | solution.py:605
  85.4 3.1 %collective-permute-start.18 = (bf16[3,96,768]{2,1,0:T(8,128)(2,1)S(1)}, bf16[3,96,768]{2,1,0:T(8,128)(2,1)S(1)}, u32[]{:S(2)}, u32[]{:S(2)}) collective-permute-start(bf16[3,96,768]{2,1,0:T(8,128)(2,1)S(1)} %get-tuple-element.245.refs_0_), channel_id=1, source_target_pairs={{0,4},{1,5},{2,6},{3,7},{4,0},{5,1},{6,2},{7,3},{8,12},{9,13},{10,... | collective-permute-start | bytes 1327112 | tf_op jit(solution)/shard_map/ppermute | solution.py:605
  85.9 3.2 %collective-permute-start.19 = (bf16[3,96,768]{2,1,0:T(8,128)(2,1)S(1)}, bf16[3,96,768]{2,1,0:T(8,128)(2,1)S(1)}, u32[]{:S(2)}, u32[]{:S(2)}) collective-permute-start(bf16[3,96,768]{2,1,0:T(8,128)(2,1)S(1)} %collective-permute-done.13.refs_1_), channel_id=1, source_target_pairs={{0,4},{1,5},{2,6},{3,7},{4,0},{5,1},{6,2},{7,3},{8,12},{9,13},{10,... | collective-permute-start | bytes 1327112 | tf_op jit(solution)/shard_map/ppermute | solution.py:605
  98.9 4.5 %collective-permute-start.21 = (bf16[2,2,4,96,768]{4,3,2,1,0:T(8,128)(2,1)S(1)}, bf16[2,2,4,96,768]{4,3,2,1,0:T(8,128)(2,1)S(1)}, u32[]{:S(2)}, u32[]{:S(2)}) collective-permute-start(bf16[2,2,4,96,768]{4,3,2,1,0:T(8,128)(2,1)S(1)} %get-tuple-element.154), channel_id=1, source_target_pairs={{0,4},{1,5},{2,6},{3,7},{4,0},{5,1},{6,2},{7,3},{8,12},{9,13},{10,... | collective-permute-start | bytes 7077896 | tf_op jit(solution)/shard_map/ppermute | solution.py:605
  104.2 16.3 %collective-permute-start.22 = (bf16[2,4,96,768]{3,2,1,0:T(8,128)(2,1)S(1)}, bf16[2,4,96,768]{3,2,1,0:T(8,128)(2,1)S(1)}, u32[]{:S(2)}, u32[]{:S(2)}) collective-permute-start(bf16[2,4,96,768]{3,2,1,0:T(8,128)(2,1)S(1)} %get-tuple-element.238), channel_id=1, source_target_pairs={{0,8},{1,9},{2,10},{3,11},{4,20},{5,21},{6,22},{7,23},{8,0},{9,1},... | collective-permute-start | bytes 3538952 | tf_op jit(solution)/shard_map/ppermute | solution.py:605
  120.5 10.1 %collective-permute-start.23 = (bf16[2,2,4,96,768]{4,3,2,1,0:T(8,128)(2,1)S(1)}, bf16[2,2,4,96,768]{4,3,2,1,0:T(8,128)(2,1)S(1)}, u32[]{:S(2)}, u32[]{:S(2)}) collective-permute-start(bf16[2,2,4,96,768]{4,3,2,1,0:T(8,128)(2,1)S(1)} %get-tuple-element.165), channel_id=1, source_target_pairs={{0,4},{1,5},{2,6},{3,7},{4,0},{5,1},{6,2},{7,3},{8,12},{9,13},{10,... | collective-permute-start | bytes 7077896 | tf_op jit(solution)/shard_map/ppermute | solution.py:605
  120.6 9.9 %collective-permute-start.24 = (bf16[4,96,768]{2,1,0:T(8,128)(2,1)S(1)}, bf16[4,96,768]{2,1,0:T(8,128)(2,1)S(1)}, u32[]{:S(2)}, u32[]{:S(2)}) collective-permute-start(bf16[4,96,768]{2,1,0:T(8,128)(2,1)S(1)} %fusion.13), channel_id=1, source_target_pairs={{0,16},{1,17},{2,18},{3,19},{4,12},{5,13},{6,14},{7,15},{8,24},{9,... | collective-permute-start | bytes 1769480 | tf_op jit(solution)/shard_map/ppermute | solution.py:605
  131.3 16.3 %collective-permute-start.25 = (bf16[2,4,96,768]{3,2,1,0:T(8,128)(2,1)S(1)}, bf16[2,4,96,768]{3,2,1,0:T(8,128)(2,1)S(1)}, u32[]{:S(2)}, u32[]{:S(2)}) collective-permute-start(bf16[2,4,96,768]{3,2,1,0:T(8,128)(2,1)S(1)} %get-tuple-element.236), channel_id=1, source_target_pairs={{0,8},{1,9},{2,10},{3,11},{4,20},{5,21},{6,22},{7,23},{8,0},{9,1},... | collective-permute-start | bytes 3538952 | tf_op jit(solution)/shard_map/ppermute | solution.py:605
  132.0 15.6 %collective-permute-start.26 = (bf16[2,2,2,96,768]{4,3,2,1,0:T(8,128)(2,1)S(1)}, bf16[2,2,2,96,768]{4,3,2,1,0:T(8,128)(2,1)S(1)}, u32[]{:S(2)}, u32[]{:S(2)}) collective-permute-start(bf16[2,2,2,96,768]{4,3,2,1,0:T(8,128)(2,1)S(1)} %get-tuple-element.176), channel_id=1, source_target_pairs={{0,4},{1,5},{2,6},{3,7},{4,0},{5,1},{6,2},{7,3},{8,12},{9,13},{10,... | collective-permute-start | bytes 3538952 | tf_op jit(solution)/shard_map/ppermute | solution.py:605
  132.2 10.4 %collective-permute-start.27 = (bf16[1,2,96,768]{3,2,1,0:T(8,128)(2,1)S(1)}, bf16[1,2,96,768]{3,2,1,0:T(8,128)(2,1)S(1)}, u32[]{:S(2)}, u32[]{:S(2)}) collective-permute-start(bf16[1,2,96,768]{3,2,1,0:T(8,128)(2,1)S(1)} %fusion.21), channel_id=1, source_target_pairs={{0,2},{1,3},{2,0},{3,1},{4,5},{5,4},{6,7},{7,6},{8,10},{9,11},{10,... | collective-permute-start | bytes 884744 | tf_op jit(solution)/shard_map/ppermute | solution.py:605
  147.6 10.1 %collective-permute-start.28 = (bf16[2,2,2,96,768]{4,3,2,1,0:T(8,128)(2,1)S(1)}, bf16[2,2,2,96,768]{4,3,2,1,0:T(8,128)(2,1)S(1)}, u32[]{:S(2)}, u32[]{:S(2)}) collective-permute-start(bf16[2,2,2,96,768]{4,3,2,1,0:T(8,128)(2,1)S(1)} %get-tuple-element.182), channel_id=1, source_target_pairs={{0,4},{1,5},{2,6},{3,7},{4,0},{5,1},{6,2},{7,3},{8,12},{9,13},{10,... | collective-permute-start | bytes 3538952 | tf_op jit(solution)/shard_map/ppermute | solution.py:605
  147.7 9.9 %collective-permute-start.29 = (bf16[4,96,768]{2,1,0:T(8,128)(2,1)S(1)}, bf16[4,96,768]{2,1,0:T(8,128)(2,1)S(1)}, u32[]{:S(2)}, u32[]{:S(2)}) collective-permute-start(bf16[4,96,768]{2,1,0:T(8,128)(2,1)S(1)} %fusion.15), channel_id=1, source_target_pairs={{0,16},{1,17},{2,18},{3,19},{4,12},{5,13},{6,14},{7,15},{8,24},{9,... | collective-permute-start | bytes 1769480 | tf_op jit(solution)/shard_map/ppermute | solution.py:605
  149.1 6.8 %collective-permute-start.30 = (bf16[1,96,768]{2,1,0:T(8,128)(2,1)S(1)}, bf16[1,96,768]{2,1,0:T(8,128)(2,1)S(1)}, u32[]{:S(2)}, u32[]{:S(2)}) collective-permute-start(bf16[1,96,768]{2,1,0:T(8,128)(2,1)S(1)} %slice_bitcast_fusion.19), channel_id=1, source_target_pairs={{0,1},{1,0},{2,3},{3,2},{4,6},{5,7},{6,4},{7,5},{8,9},{9,8},{10,11... | collective-permute-start | bytes 442376 | tf_op jit(solution)/shard_map/ppermute | solution.py:605
  149.1 4.7 %collective-permute-start.31 = (f32[16,768]{1,0:T(8,128)S(1)}, f32[16,768]{1,0:T(8,128)S(1)}, u32[]{:S(2)}, u32[]{:S(2)}) collective-permute-start(f32[16,768]{1,0:T(8,128)S(1)} %get-tuple-element.189), channel_id=1, source_target_pairs={{0,4},{1,5},{2,6},{3,7},{4,0},{5,1},{6,2},{7,3},{8,12},{9,13},{10,... | collective-permute-start | bytes 147464 | tf_op jit(solution)/shard_map/ppermute | solution.py:605
  158.5 16.5 %collective-permute-start.32 = (bf16[784,768]{1,0:T(8,128)(2,1)S(1)}, bf16[784,768]{1,0:T(8,128)(2,1)S(1)}, u32[]{:S(2)}, u32[]{:S(2)}) collective-permute-start(bf16[784,768]{1,0:T(8,128)(2,1)S(1)} %pad_maximum_fusion), channel_id=1, source_target_pairs={{0,8},{1,9},{2,10},{3,11},{4,20},{5,21},{6,22},{7,23},{8,0},{9,1},... | collective-permute-start | bytes 3612680 | tf_op jit(solution)/shard_map/ppermute | solution.py:605
  159.4 10.6 %collective-permute-start.33 = (bf16[1,2,96,768]{3,2,1,0:T(8,128)(2,1)S(1)}, bf16[1,2,96,768]{3,2,1,0:T(8,128)(2,1)S(1)}, u32[]{:S(2)}, u32[]{:S(2)}) collective-permute-start(bf16[1,2,96,768]{3,2,1,0:T(8,128)(2,1)S(1)} %fusion.19), channel_id=1, source_target_pairs={{0,2},{1,3},{2,0},{3,1},{4,5},{5,4},{6,7},{7,6},{8,10},{9,11},{10,... | collective-permute-start | bytes 884744 | tf_op jit(solution)/shard_map/ppermute | solution.py:605
  175.1 12.5 %copy-start.16 = (bf16[784,768]{1,0:T(8,128)(2,1)}, bf16[784,768]{1,0:T(8,128)(2,1)S(1)}, u32[]{:S(2)}) copy-start(bf16[784,768]{1,0:T(8,128)(2,1)S(1)} %collective-permute-done.32) | copy-start | bytes 3612676
  175.3 10.2 %collective-permute-start.34 = (bf16[400,768]{1,0:T(8,128)(2,1)S(1)}, bf16[400,768]{1,0:T(8,128)(2,1)S(1)}, u32[]{:S(2)}, u32[]{:S(2)}) collective-permute-start(bf16[400,768]{1,0:T(8,128)(2,1)S(1)} %pad_maximum_fusion.7), channel_id=1, source_target_pairs={{0,16},{1,17},{2,18},{3,19},{4,12},{5,13},{6,14},{7,15},{8,24},{9,... | collective-permute-start | bytes 1843208 | tf_op jit(solution)/shard_map/ppermute | solution.py:605
  176.6 5.8 %collective-permute-start.35 = (bf16[1,96,768]{2,1,0:T(8,128)(2,1)S(1)}, bf16[1,96,768]{2,1,0:T(8,128)(2,1)S(1)}, u32[]{:S(2)}, u32[]{:S(2)}) collective-permute-start(bf16[1,96,768]{2,1,0:T(8,128)(2,1)S(1)} %slice_bitcast_fusion.18), channel_id=1, source_target_pairs={{0,1},{1,0},{2,3},{3,2},{4,6},{5,7},{6,4},{7,5},{8,9},{9,8},{10,11... | collective-permute-start | bytes 442376 | tf_op jit(solution)/shard_map/ppermute | solution.py:605
  185.7 17.0 %collective-permute-start.39 = (bf16[2,96,768]{2,1,0:T(8,128)(2,1)S(1)}, bf16[2,96,768]{2,1,0:T(8,128)(2,1)S(1)}, u32[]{:S(2)}, u32[]{:S(2)}) collective-permute-start(bf16[2,96,768]{2,1,0:T(8,128)(2,1)S(1)} %get-tuple-element.249), channel_id=1, source_target_pairs={{0,8},{1,9},{2,10},{3,11},{4,12},{5,13},{6,14},{7,15},{8,0},{9,1},... | collective-permute-start | bytes 884744 | tf_op jit(solution)/shard_map/ppermute | solution.py:605
  186.3 16.3 %collective-permute-start.40 = (bf16[2,96,768]{2,1,0:T(8,128)(2,1)S(1)}, bf16[2,96,768]{2,1,0:T(8,128)(2,1)S(1)}, u32[]{:S(2)}, u32[]{:S(2)}) collective-permute-start(bf16[2,96,768]{2,1,0:T(8,128)(2,1)S(1)} %get-tuple-element.249), channel_id=1, source_target_pairs={{0,16},{1,17},{2,18},{3,19},{4,20},{5,21},{6,22},{7,23},{8,24},{9,... | collective-permute-start | bytes 884744 | tf_op jit(solution)/shard_map/ppermute | solution.py:605
  187.9 9.2 %collective-permute-start.36 = (bf16[112,768]{1,0:T(8,128)(2,1)S(1)}, bf16[112,768]{1,0:T(8,128)(2,1)S(1)}, u32[]{:S(2)}, u32[]{:S(2)}) collective-permute-start(bf16[112,768]{1,0:T(8,128)(2,1)S(1)} %get-tuple-element.255), channel_id=1, source_target_pairs={{0,3},{1,2},{2,1},{3,0},{4,7},{5,6},{6,5},{7,4},{8,11},{9,10},{10,... | collective-permute-start | bytes 516104 | tf_op jit(solution)/shard_map/ppermute | solution.py:605
  190.1 12.5 %collective-permute-start.37 = (bf16[112,768]{1,0:T(8,128)(2,1)S(1)}, bf16[112,768]{1,0:T(8,128)(2,1)S(1)}, u32[]{:S(2)}, u32[]{:S(2)}) collective-permute-start(bf16[112,768]{1,0:T(8,128)(2,1)S(1)} %get-tuple-element.254), channel_id=1, source_target_pairs={{0,2},{1,3},{2,0},{3,1},{4,6},{5,7},{6,4},{7,5},{8,10},{9,11},{10,... | collective-permute-start | bytes 516104 | tf_op jit(solution)/shard_map/ppermute | solution.py:605
  190.1 12.5 %collective-permute-start.38 = (bf16[112,768]{1,0:T(8,128)(2,1)S(1)}, bf16[112,768]{1,0:T(8,128)(2,1)S(1)}, u32[]{:S(2)}, u32[]{:S(2)}) collective-permute-start(bf16[112,768]{1,0:T(8,128)(2,1)S(1)} %get-tuple-element.253), channel_id=1, source_target_pairs={{0,1},{1,0},{2,3},{3,2},{4,5},{5,4},{6,7},{7,6},{8,9},{9,8},{10,11... | collective-permute-start | bytes 516104 | tf_op jit(solution)/shard_map/ppermute | solution.py:605
  202.8 9.8 %collective-permute-start.44 = (bf16[3,2,96,768]{3,2,1,0:T(8,128)(2,1)S(1)}, bf16[3,2,96,768]{3,2,1,0:T(8,128)(2,1)S(1)}, u32[]{:S(2)}, u32[]{:S(2)}) collective-permute-start(bf16[3,2,96,768]{3,2,1,0:T(8,128)(2,1)S(1)} %pad_maximum_fusion.6.held), channel_id=1, source_target_pairs={{0,4},{1,5},{2,6},{3,7},{4,0},{5,1},{6,2},{7,3},{8,12},{9,13},{10,... | collective-permute-start | bytes 2654216 | tf_op jit(solution)/shard_map/ppermute | solution.py:605
  202.9 9.7 %collective-permute-start.49 = (bf16[2,96,768]{2,1,0:T(8,128)(2,1)S(1)}, bf16[2,96,768]{2,1,0:T(8,128)(2,1)S(1)}, u32[]{:S(2)}, u32[]{:S(2)}) collective-permute-start(bf16[2,96,768]{2,1,0:T(8,128)(2,1)S(1)} %broadcast_select_fusion), channel_id=1, source_target_pairs={{0,8},{1,9},{2,10},{3,11},{4,20},{5,21},{6,22},{7,23},{8,0},{9,1},... | collective-permute-start | bytes 884744 | tf_op jit(solution)/shard_map/ppermute | solution.py:605
  204.5 11.6 %collective-permute-start.41 = (bf16[96,768]{1,0:T(8,128)(2,1)S(1)}, bf16[96,768]{1,0:T(8,128)(2,1)S(1)}, u32[]{:S(2)}, u32[]{:S(2)}) collective-permute-start(bf16[96,768]{1,0:T(8,128)(2,1)S(1)} %fusion.26.refs_0_), channel_id=1, source_target_pairs={{0,8},{1,9},{2,10},{3,11},{4,12},{5,13},{6,14},{7,15},{8,0},{9,1},... | collective-permute-start | bytes 442376 | tf_op jit(solution)/shard_map/ppermute | solution.py:605
  205.1 11.0 %collective-permute-start.42 = (bf16[96,768]{1,0:T(8,128)(2,1)S(1)}, bf16[96,768]{1,0:T(8,128)(2,1)S(1)}, u32[]{:S(2)}, u32[]{:S(2)}) collective-permute-start(bf16[96,768]{1,0:T(8,128)(2,1)S(1)} %fusion.26.refs_0_), channel_id=1, source_target_pairs={{0,16},{1,17},{2,18},{3,19},{4,20},{5,21},{6,22},{7,23},{8,24},{9,... | collective-permute-start | bytes 442376 | tf_op jit(solution)/shard_map/ppermute | solution.py:605
  206.0 10.3 %collective-permute-start.43 = (bf16[96,768]{1,0:T(8,128)(2,1)S(1)}, bf16[96,768]{1,0:T(8,128)(2,1)S(1)}, u32[]{:S(2)}, u32[]{:S(2)}) collective-permute-start(bf16[96,768]{1,0:T(8,128)(2,1)S(1)} %fusion.26.refs_0_), channel_id=1, source_target_pairs={{0,24},{1,25},{2,26},{3,27},{4,28},{5,29},{6,30},{7,31},{8,16},{9,... | collective-permute-start | bytes 442376 | tf_op jit(solution)/shard_map/ppermute | solution.py:605
  212.6 7.1 %collective-permute-start.45 = (bf16[96,768]{1,0:T(8,128)(2,1)S(1)}, bf16[96,768]{1,0:T(8,128)(2,1)S(1)}, u32[]{:S(2)}, u32[]{:S(2)}) collective-permute-start(bf16[96,768]{1,0:T(8,128)(2,1)S(1)} %fusion.26.refs_0_), channel_id=1, source_target_pairs={{0,4},{1,5},{2,6},{3,7},{4,0},{5,1},{6,2},{7,3},{8,12},{9,13},{10,... | collective-permute-start | bytes 442376 | tf_op jit(solution)/shard_map/ppermute | solution.py:605
  212.6 4.8 %collective-permute-start.50 = (bf16[2,96,768]{2,1,0:T(8,128)(2,1)S(1)}, bf16[2,96,768]{2,1,0:T(8,128)(2,1)S(1)}, u32[]{:S(2)}, u32[]{:S(2)}) collective-permute-start(bf16[2,96,768]{2,1,0:T(8,128)(2,1)S(1)} %collective-permute-done.49.corner), channel_id=1, source_target_pairs={{0,4},{1,5},{2,6},{3,7},{4,0},{5,1},{6,2},{7,3},{8,12},{9,13},{10,... | collective-permute-start | bytes 884744 | tf_op jit(solution)/shard_map/ppermute | solution.py:605
  216.3 3.3 %collective-permute-start.46 = (bf16[96,768]{1,0:T(8,128)(2,1)S(1)}, bf16[96,768]{1,0:T(8,128)(2,1)S(1)}, u32[]{:S(2)}, u32[]{:S(2)}) collective-permute-start(bf16[96,768]{1,0:T(8,128)(2,1)S(1)} %collective-permute-done.41.refs_1_), channel_id=1, source_target_pairs={{0,4},{1,5},{2,6},{3,7},{4,0},{5,1},{6,2},{7,3},{8,12},{9,13},{10,... | collective-permute-start | bytes 442376 | tf_op jit(solution)/shard_map/ppermute | solution.py:605
  216.3 3.3 %collective-permute-start.47 = (bf16[96,768]{1,0:T(8,128)(2,1)S(1)}, bf16[96,768]{1,0:T(8,128)(2,1)S(1)}, u32[]{:S(2)}, u32[]{:S(2)}) collective-permute-start(bf16[96,768]{1,0:T(8,128)(2,1)S(1)} %collective-permute-done.42.refs_2_), channel_id=1, source_target_pairs={{0,4},{1,5},{2,6},{3,7},{4,0},{5,1},{6,2},{7,3},{8,12},{9,13},{10,... | collective-permute-start | bytes 442376 | tf_op jit(solution)/shard_map/ppermute | solution.py:605
  216.8 2.8 %collective-permute-start.48 = (bf16[96,768]{1,0:T(8,128)(2,1)S(1)}, bf16[96,768]{1,0:T(8,128)(2,1)S(1)}, u32[]{:S(2)}, u32[]{:S(2)}) collective-permute-start(bf16[96,768]{1,0:T(8,128)(2,1)S(1)} %collective-permute-done.43.refs_3_), channel_id=1, source_target_pairs={{0,4},{1,5},{2,6},{3,7},{4,0},{5,1},{6,2},{7,3},{8,12},{9,13},{10,... | collective-permute-start | bytes 442376 | tf_op jit(solution)/shard_map/ppermute | solution.py:605
  (17 other events, 94.0 us)

commit v2 on v1

--- a/solution.py
+++ b/solution.py
@@ -129,10 +129,9 @@
         target[0] = own[...]
     skip = 1 if own is None else 0
     for s in range(2):
-        first, second, third = refs[3 * s : 3 * s + 3]
+        views = refs[4 * s : 4 * s + 4]
         holder = info[1] ^ s
         order = (1 + holder, 2 - holder, 3)
-        views = (first, second, third.at[0], third.at[1])
         for view, move in zip(views, (0,) + order):
             rows = view.shape[1]
             start = pl.multiple_of((holder * 4 + (info[2] ^ move)) * rows, rows)
@@ -175,9 +174,9 @@
 
 
 def attn_rest_kernel(info, tokens, bias, *refs):
-    qkv_out, whole, ctx, lse, out_w, weights, qkv, sems = refs[6:]
+    qkv_out, whole, ctx, lse, out_w, weights, qkv, sems = refs[8:]
     others, local = ctx.shape[:2]
-    assemble(info, refs[:6], weights)
+    assemble(info, refs[:8], weights)
     sent = [pltpu.make_async_copy(weights, whole, sems.at[others])]
     sent[0].start()
     out_w[...] = weights[:, 3 * local :]
@@ -203,7 +202,7 @@
     joint, whole = (others, 3 * local, seq), (others, size, cols)
     return pl.pallas_call(
         attn_rest_kernel,
-        in_specs=[smem()] + [vmem()] * 8,
+        in_specs=[smem()] + [vmem()] * 10,
         out_specs=[pl.BlockSpec(memory_space=pltpu.HBM)] * 2 + [vmem()] * 3,
         out_shape=[
             shaped(joint, low),
@@ -258,11 +257,11 @@
 
 
 def ffn_up_kernel(info, normed, bias, up_own, *refs):
-    _, act, slope, up, mark = refs[6:]
+    _, act, slope, up, mark = refs[8:]
     size = up.shape[2]
     first = bias.shape[2] - size
     mark[...] = jnp.zeros(mark.shape, wide)
-    assemble(info, refs[:6], up, up_own)
+    assemble(info, refs[:8], up, up_own)
 
     def forward(k, _):
         preact = mm(normed[...], up[k], 1, 0) + bias[k][:, first:].astype(wide)
@@ -279,7 +278,7 @@
     others, size = pieces[0].shape[0], up_own.shape[1]
     return pl.pallas_call(
         ffn_up_kernel,
-        in_specs=[smem()] + [vmem()] * (3 + 6) + [hbm()],
+        in_specs=[smem()] + [vmem()] * (3 + 8) + [hbm()],
         out_specs=[vmem()] * 4,
         out_shape=[
             shaped((others + 1, seq, size), low),
@@ -294,9 +293,9 @@
 
 
 def ffn_down_kernel(info, skip, vec, cot, act, down_own, *refs):
-    _, out, grad_ref, branch_ref, small, keep, send, down, scratch = refs[6:]
+    _, out, grad_ref, branch_ref, small, down = refs[8:]
     parts = act.shape[0]
-    assemble(info, refs[:6], down, down_own)
+    assemble(info, refs[:8], down, down_own)
     grad_ref[...] = skip[...]
 
     def branch(k, _):
@@ -318,12 +317,35 @@
     small[4:5] = jnp.sum(grad * hat_two, axis=0, keepdims=True)
     small[5:6] = jnp.sum(grad, axis=0, keepdims=True)
 
-    def weight(k, _):
-        scratch[...] = mm(act[k], branch_ref[...], 0, 0).astype(low)
-        place_pieces(info, scratch, keep, send, k)
+
+def down_grad_kernel(first, info, act, branch_low, keep, send, mark, scratch):
+    mark[...] = jnp.zeros(mark.shape, wide)
+
+    def weight(i, _):
+        scratch[...] = mm(act[first + i], branch_low[...], 0, 0).astype(low)
+        place_pieces(info, scratch, keep, send, i)
         return 0
 
-    lax.fori_loop(0, parts, weight, 0)
+    lax.fori_loop(0, 2, weight, 0)
+
+
+def down_grad(first, info, act, branch_low, mark):
+    size, width = act.shape[2], branch_low.shape[1]
+    half = halves_shape(2, size, width)
+    return pl.pallas_call(
+        partial(down_grad_ordered, first),
+        in_specs=[smem()] + [vmem()] * 2 + [hbm()],
+        out_specs=[vmem()] * 3,
+        out_shape=[shaped(half, low), shaped(half, low), shaped((8, 128), wide)],
+        scratch_shapes=[pltpu.VMEM((size, width), low)],
+        compiler_params=params(),
+        cost_estimate=cost(2),
+        name="down_grad",
+    )(info, act, branch_low, mark)
+
+
+def down_grad_ordered(first, info, act, branch_low, _, *refs):
+    down_grad_kernel(first, info, act, branch_low, *refs)
 
 
 def halves_shape(entries, rows, cols):
@@ -333,21 +355,17 @@
 def ffn_down(info, act, skip, vec, cot, down_own, pieces, mark):
     parts, seq, size = act.shape
     width = skip.shape[1]
-    half = halves_shape(parts, size, width)
     return pl.pallas_call(
         ffn_down_kernel,
-        in_specs=[smem()] + [vmem()] * (5 + 6) + [hbm()],
-        out_specs=[vmem()] * 7,
+        in_specs=[smem()] + [vmem()] * (5 + 8) + [hbm()],
+        out_specs=[vmem()] * 5,
         out_shape=[
             shaped((seq, width), low),
             shaped((seq, width), wide),
             shaped((seq, width), low),
             shaped((16, width), wide),
-            shaped(half, low),
-            shaped(half, low),
             shaped((parts, size, width), low),
         ],
-        scratch_shapes=[pltpu.VMEM((size, width), low)],
         compiler_params=params(),
         cost_estimate=cost(12),
         name="ffn_down",
@@ -421,10 +439,8 @@
     small[...] = small_in[...]
     key_pad, query_pad = masked_pad(info[0], seq)
     ones = jnp.ones((8, seq), low)
-    for i, (out_w, qkv_ref, ctx_ref, lse_ref) in enumerate(groups):
-        k = first + i
-        out_rows = out_w[...] if k == 0 else out_w[k - 1]
-        qkv, ctx, lse = (ref.at[max(k - 1, 0)] for ref in (qkv_ref, ctx_ref, lse_ref))
+
+    def group(i, out_rows, qkv, ctx, lse):
         grad_ctx = mm(out_rows, residual_low[...], 1, 1).astype(low)
         for h in range(local // HD):
             lo, hi = h * HD, (h + 1) * HD
@@ -453,6 +469,19 @@
         scratch[: 3 * local] = mm(grads, tokens[...], 1, 0).astype(low)
         scratch[3 * local :] = mm(ctx[...], residual_low[...], 1, 0).astype(low)
         place_pieces(info, scratch, keep, send, i)
+
+    if first == 0:
+        for i, (out_w, qkv_ref, ctx_ref, lse_ref) in enumerate(groups):
+            group(i, out_w[...] if i == 0 else out_w[0], qkv_ref.at[0], ctx_ref.at[0], lse_ref.at[0])
+        return
+    out_w, qkv_ref, ctx_ref, lse_ref = groups[0]
+
+    def step(i, _):
+        k = first - 1 + i
+        group(i, out_w[k], qkv_ref.at[k], ctx_ref.at[k], lse_ref.at[k])
+        return 0
+
+    lax.fori_loop(0, 2, step, 0)
 
 
 def attn_back(first, info, tokens, residual_low, small, out_own, own, out_rest, rest):
@@ -669,6 +698,9 @@
     def cut(array, index):
         return lax.dynamic_slice_in_dim(array, index * rows, rows, 0)
 
+    def mates(held):
+        return held + [links.core(array) for array in held]
+
     a0 = lax.select_n(piece >> 1, *(cut(array, piece & 1) for array in attn_w))
     bias_own = jnp.concatenate([b_query, b_value, b_up])
     bias_rows = jnp.pad(bias_own, (0, 8 * width - bias_own.size)).reshape(8, width)
@@ -677,17 +709,19 @@
     u0 = jnp.concatenate([cut(w_up, piece), bias_rows], axis=0)
     vec = jnp.stack([b_out, ln1_gain, ln1_bias, b_down, ln2_gain, ln2_bias, b_down, b_down])
     vec = vec.astype(wide)
-    a1, d1 = links.line(a0, 0), links.line(d0, 0)
+    a1, ax = links.line(a0, 0), links.line(a0, 1)
+    d1 = links.line(d0, 0)
     a1, u0, vec, tokens_in = after(a1, u0, vec, tokens)
-    a2 = links.line(jnp.stack([a0, a1]), 1)
-    u1 = links.line(u0, 0)
+    ay = links.line(a1, 1)
+    u1, ux = links.line(u0, 0), links.line(u0, 1)
     own = list(attn_own(info, tokens_in, attn_w[:3], bias_own.astype(wide)[None, None]))
-    a2, u1, d1, own[2] = after(a2, u1, d1, own[2])
-    a3 = jnp.concatenate([a1[None], a2])
-    a4 = links.plane(a3, 0)
-    u2 = links.line(jnp.stack([u0, u1]), 1)
-    a4, d1 = after(a4, d1)
-    u3 = jnp.concatenate([u1[None], u2])
+    ax, ay, u1, d1, own[2] = after(ax, ay, u1, d1, own[2])
+    a3 = jnp.stack([a1, ax, ay])
+    a4, a5 = links.plane(a3, 0), links.plane(a3, 1)
+    uy = links.line(u1, 1)
+    dx = links.line(d0, 1)
+    a4, ux, uy, d1 = after(a4, ux, uy, d1)
+    u3 = jnp.stack([u1, ux, uy])
     bias_rest = u3[:, rows:].reshape(parts - 1, 8 * width)[:, : bias_own.size]
     near, far = bias_rest[0], bias_rest[1]
     bias = jnp.stack(
@@ -695,23 +729,23 @@
     )
     bias = bias.astype(wide)[:, None]
     u3 = u3[:, :rows]
-    a5 = links.plane(jnp.stack([a3, a4]), 1)
-    u4 = links.plane(u3, 0)
-    d2 = links.line(jnp.stack([d0, d1]), 1)
-    a5, u4, d2, bias = after(a5, u4, d2, bias)
-    d3 = jnp.concatenate([d1[None], d2])
-    pieces_a = [a3, a4, a5] + [links.core(array) for array in (a3, a4, a5)]
-    u5 = links.plane(jnp.stack([u3, u4]), 1)
-    d4 = links.plane(d3, 0)
+    a6 = links.plane(a4, 1)
+    u4, u5 = links.plane(u3, 0), links.plane(u3, 1)
+    dy = links.line(d1, 1)
+    a5, a6, u4, dx, dy, bias = after(a5, a6, u4, dx, dy, bias)
+    d3 = jnp.stack([d1, dx, dy])
+    pieces_a = mates([a3, a4, a5, a6])
+    u6 = links.plane(u4, 1)
+    d4, d5 = links.plane(d3, 0), links.plane(d3, 1)
     qkv, attn_rest_w, ctx, lse, out_rest = attn_rest(info, tokens, bias, pieces_a)
     skip, normed_low, hat, inv = ffn_in(tokens, own[1], ctx, vec, w_out, out_rest)
-    u5, d4, lse, inv = after(u5, d4, lse, inv)
-    pieces_u = [u3, u4, u5] + [links.core(array) for array in (u3, u4, u5)]
-    d5 = links.plane(jnp.stack([d3, d4]), 1)
+    u5, u6, d4, lse, inv = after(u5, u6, d4, lse, inv)
+    pieces_u = mates([u3, u4, u5, u6])
+    d6 = links.plane(d4, 1)
     act, slope, up, mark = ffn_up(info, normed_low, bias, w_up, pieces_u, inv)
-    d5, mark = after(d5, mark)
-    pieces_d = [d3, d4, d5] + [links.core(array) for array in (d3, d4, d5)]
-    output, grad_branch, branch_low, small, keep_d, send_d, down = ffn_down(
+    d5, d6, mark = after(d5, d6, mark)
+    pieces_d = mates([d3, d4, d5, d6])
+    output, grad_branch, branch_low, small, down = ffn_down(
         info, act, skip, vec, cotangent, w_down, pieces_d, mark
     )
     rest = (qkv, ctx, lse)
@@ -739,18 +773,21 @@
             bit *= 2
         return total.astype(low)
 
-    def mates(held):
-        return held + [links.core(array) for array in held]
-
+    keep_c, send_c, mark = down_grad(0, info, act, branch_low, mark)
+    got_c = links.core(send_c)
+    keep_d, send_d, mark = down_grad(2, info, act, branch_low, mark)
+    got_c, send_d, mark = after(got_c, send_d, mark)
+    near_c, kept_c = plane_a(keep_c, got_c)
     got_d = links.core(send_d)
     got_d, small = after(got_d, small)
     near_d, kept_d = plane_a(keep_d, got_d)
     grad_residual, residual_low, small, keep_u, send_u = ffn_back(
         info, branch_low, grad_branch, slope, normed_low, hat, inv, vec, small, up, down
     )
-    near_d, send_u, small = after(near_d, send_u, small)
+    near_c, near_d, send_u, small = after(near_c, near_d, send_u, small)
     got_u = links.core(send_u)
-    far_d, kept_d = plane_b(kept_d, near_d)
+    far_d = links.plane(jnp.concatenate([add(kept_c[1], near_c[1]), add(kept_d[1], near_d[1])]), 1)
+    kept_d = jnp.concatenate([add(kept_c[0], near_c[0]), add(kept_d[0], near_d[0])])
     small, joint_a, keep_a, send_a = attn_back(
         0, info, tokens, residual_low, small, w_out, own, out_rest, rest
     )

time: 226 us -> 222 us (0.982)
  waiting for transfers between devices: 95.3 us -> 77.3 us
  starting transfers between devices: 40.3 us -> 48.3 us
  other arithmetic: 9.65 us -> 12.2 us
    ppermute x51 -> x62, waiting for transfers between devices: 95.3 us -> 77.3 us  [move(): return lax.ppermute(array, ('dp', 'tensor'), pairs)]
    ppermute x51 -> x62, starting transfers between devices: 40.3 us -> 48.3 us  [move(): return lax.ppermute(array, ('dp', 'tensor'), pairs)]
    pallas_call x3 -> x5, Pallas kernels: 27.7 us -> 29.2 us  [the longest x1 9.23 us: attn_rest(): pl.pallas_call(attn_rest_kernel, in_specs=[smem()] + [vmem()] * 10, out_s...]
  transfers between devices with their start and end apart: 51 -> 62, of which waited for: 30 -> 25; matrix products, arithmetic and copies ran while one was open for 4% -> 6% of each run, Pallas kernels for 26% -> 28%
where the time goes in v2:
time: 222 us; the launch traced here: 218 us
  waiting for transfers between devices  77.3 us (35%)
  Pallas kernels  70.9 us (32%)
  starting transfers between devices  48.3 us (22%)
  other arithmetic  12.2 us (5%)
  local copies, waits for them, and re-layouts  6.99 us (3%)
    ppermute x62, waiting for transfers between devices, move(): return lax.ppermute(array, ('dp', 'tensor'), pairs)  77.3 us
    ppermute x62, starting transfers between devices, move(): return lax.ppermute(array, ('dp', 'tensor'), pairs)  48.3 us
    pallas_call x2, Pallas kernels, attn_back(): pl.pallas_call(partial(attn_back_kernel, first), in_specs=[smem()] + [vme...  16.3 us
    pallas_call x1, Pallas kernels, ffn_back(): pl.pallas_call(ffn_back_kernel, in_specs=[smem()] + [vmem()] * 10, out_sp...  10.5 us
    pallas_call x1, Pallas kernels, attn_rest(): pl.pallas_call(attn_rest_kernel, in_specs=[smem()] + [vmem()] * 10, out_s...  9.23 us
    pallas_call x1, Pallas kernels, ffn_up(): pl.pallas_call(ffn_up_kernel, in_specs=[smem()] + [vmem()] * (3 + 8) + [h...  8.67 us
    pallas_call x1, Pallas kernels, ffn_down(): pl.pallas_call(ffn_down_kernel, in_specs=[smem()] + [vmem()] * (5 + 8) +...  6.03 us
    pallas_call x2, Pallas kernels, down_grad(): pl.pallas_call(partial(down_grad_ordered, first), in_specs=[smem()] + [vm...  5.25 us
  transfers between devices with their start and end apart: 62, of which 25 were waited for; matrix products, arithmetic and copies ran while one was open for 6% of the time, Pallas kernels for 28%

profile of v2, /device:TPU:0, one launch (start us, length us, event | category | flops | bytes accessed | tf_op | source)
XLA Modules:
  0.0 217.7 jit_solution(40160936901335800)
XLA Ops:
  0.8 2.0 fusion.30
  2.8 3.0 %collective-permute-start = (bf16[96,768]{1,0:T(8,128)(2,1)}, bf16[96,768]{1,0:T(8,128)(2,1)S(1)}, u32[]{:S(2)}, u32[]{:S(2)}) collective-permute-start(bf16[96,768]{1,0:T(8,128)(2,1)} %fusion.30), channel_id=1, source_target_pairs={{0,1},{1,0},{2,3},{3,2},{4,6},{5,7},{6,4},{7,5},{8,9},{9,8},{10,11... | collective-permute-start | bytes 442376 | tf_op jit(solution)/shard_map/ppermute | solution.py:634
  5.9 2.6 %collective-permute-start.1 = (bf16[96,768]{1,0:T(8,128)(2,1)}, bf16[96,768]{1,0:T(8,128)(2,1)S(1)}, u32[]{:S(2)}, u32[]{:S(2)}) collective-permute-start(bf16[96,768]{1,0:T(8,128)(2,1)} %fusion.30), channel_id=1, source_target_pairs={{0,2},{1,3},{2,0},{3,1},{4,5},{5,4},{6,7},{7,6},{8,10},{9,11},{10,... | collective-permute-start | bytes 442376 | tf_op jit(solution)/shard_map/ppermute | solution.py:634
  8.5 0.9 constant_dynamic-slice_fusion
  9.9 1.2 dynamic_slice.28
  11.1 0.9 constant_dynamic-slice_fusion.1
  14.5 2.4 %collective-permute-start.3 = (bf16[104,768]{1,0:T(8,128)(2,1)}, bf16[104,768]{1,0:T(8,128)(2,1)S(1)}, u32[]{:S(2)}, u32[]{:S(2)}) collective-permute-start(bf16[104,768]{1,0:T(8,128)(2,1)} %pad_maximum_fusion.13), channel_id=1, source_target_pairs={{0,1},{1,0},{2,3},{3,2},{4,6},{5,7},{6,4},{7,5},{8,9},{9,8},{10,11... | collective-permute-start | bytes 479240 | tf_op jit(solution)/shard_map/ppermute | solution.py:634
  16.9 3.0 %attn_own.1 = (bf16[1,576,512]{2,1,0:T(8,128)(2,1)S(1)}, bf16[1,192,512]{2,1,0:T(8,128)(2,1)S(1)}, f32[1,8,512]{2,1,0:T(8,128)S(1)}) custom-call(s32[4]{0:T(128)S(1)} %pad_add_fusion.info, bf16[512,768]{1,0:T(8,128)(2,1)S(1)} %copy-done.7, bf16[192,768]{1,0:T(8,128)(2,1)S(1)} %bitcast.170, bf16[192,768]{1,0:T(8,128)(2,1)S(1)} %bitcast.172, ...), custom_call_target="tpu_custom_call" | custom-call | flops 4400000000 | bytes 1048576 | tf_op jit(solution)/shard_map/attn_own/pallas_call | solution.py:161
  19.9 0.9 collective-permute-done.4
  20.8 3.2 %collective-permute-done.2 = bf16[96,768]{1,0:T(8,128)(2,1)S(1)} collective-permute-done((bf16[96,768]{1,0:T(8,128)(2,1)S(1)}, bf16[96,768]{1,0:T(8,128)(2,1)S(1)}, u32[]{:S(2)}, u32[]{:S(2)}) %collective-permute-start.2) | collective-permute-done | bytes 147488 | tf_op jit(solution)/shard_map/ppermute | solution.py:634
  24.0 1.9 collective-permute-start.6
  25.9 1.3 collective-permute-start.7
  27.2 1.6 collective-permute-start.8
  28.8 1.3 collective-permute-start.11
  30.2 1.5 collective-permute-start.5
  31.7 1.7 collective-permute-done.7
  33.3 3.4 %collective-permute-done.8 = bf16[104,768]{1,0:T(8,128)(2,1)} collective-permute-done((bf16[104,768]{1,0:T(8,128)(2,1)S(1)}, bf16[104,768]{1,0:T(8,128)(2,1)}, u32[]{:S(2)}, u32[]{:S(2)}) %collective-permute-start.8) | collective-permute-done | bytes 159776 | tf_op jit(solution)/shard_map/ppermute | solution.py:634
  36.8 1.1 pad_maximum_fusion.6
  38.6 3.9 %collective-permute-start.9 = (bf16[3,96,768]{2,1,0:T(8,128)(2,1)S(1)}, bf16[3,96,768]{2,1,0:T(8,128)(2,1)S(1)}, u32[]{:S(2)}, u32[]{:S(2)}) collective-permute-start(bf16[3,96,768]{2,1,0:T(8,128)(2,1)S(1)} %collective-permute-done.6.refs_1_), channel_id=1, source_target_pairs={{0,16},{1,17},{2,18},{3,19},{4,12},{5,13},{6,14},{7,15},{8,24},{9,... | collective-permute-start | bytes 1327112 | tf_op jit(solution)/shard_map/ppermute | solution.py:634
  43.4 6.9 %collective-permute-done.12 = bf16[96,768]{1,0:T(8,128)(2,1)S(1)} collective-permute-done((bf16[96,768]{1,0:T(8,128)(2,1)S(1)}, bf16[96,768]{1,0:T(8,128)(2,1)S(1)}, u32[]{:S(2)}, u32[]{:S(2)}) %collective-permute-start.12) | collective-permute-done | bytes 147488 | tf_op jit(solution)/shard_map/ppermute | solution.py:634
  51.4 1.0 pad_maximum_fusion.8.refs_0_
  53.3 1.3 collective-permute-start.18
  54.6 1.1 collective-permute-start.19
  55.7 9.2 %attn_rest.1 = (bf16[3,576,512]{2,1,0:T(8,128)(2,1)S(1)}, bf16[3,768,768]{2,1,0:T(8,128)(2,1)S(1)}, bf16[3,192,512]{2,1,0:T(8,128)(2,1)S(1)}, f32[3,8,512]{2,1,0:T(8,128)S(1)}, bf16[3,192,768]{2,1,0:T(8,128)(2,1)S(1)}) custom-call(s32[4]{0:T(128)S(1)} %pad_add_fusion.info, bf16[512,768]{1,0:T(8,128)(2,1)S(1)} %copy-done.7, ...), custom_call_target="tpu_custom_call" | custom-call | flops 8800000000 | bytes 1048576 | tf_op jit(solution)/shard_map/attn_rest/pallas_call | solution.py:203
  64.9 1.6 ffn_in.1
  66.6 2.6 %collective-permute-done.18.refs_3_ = bf16[3,96,768]{2,1,0:T(8,128)(2,1)S(1)} collective-permute-done((bf16[3,96,768]{2,1,0:T(8,128)(2,1)S(1)}, bf16[3,96,768]{2,1,0:T(8,128)(2,1)S(1)}, u32[]{:S(2)}, u32[]{:S(2)}) %collective-permute-start.18) | collective-permute-done | bytes 442400 | tf_op jit(solution)/shard_map/ppermute | solution.py:634
  70.5 1.3 collective-permute-start.25
  71.8 8.7 %ffn_up.1 = (bf16[4,512,768]{2,1,0:T(8,128)(2,1)S(1)}, bf16[4,512,768]{2,1,0:T(8,128)(2,1)S(1)}, bf16[4,768,768]{2,1,0:T(8,128)(2,1)S(1)}, f32[8,128]{1,0:T(8,128)S(1)}) custom-call(s32[4]{0:T(128)S(1)} %pad_add_fusion.info, bf16[512,768]{1,0:T(8,128)(2,1)S(1)} %get-tuple-element.155.normed.normed_low, f32[4,1,1152]{2,1,0:T(1,128)S(1)} %maximum_convert_fusion.bias, ...), custom_call_target="tpu_custom_call" | custom-call | flops 12099999744 | bytes 1048576 | tf_op jit(solution)/shard_map/ffn_up/pallas_call | solution.py:279
  80.5 2.2 %collective-permute-done.25.refs_3_ = bf16[3,96,768]{2,1,0:T(8,128)(2,1)S(1)} collective-permute-done((bf16[3,96,768]{2,1,0:T(8,128)(2,1)S(1)}, bf16[3,96,768]{2,1,0:T(8,128)(2,1)S(1)}, u32[]{:S(2)}, u32[]{:S(2)}) %collective-permute-start.25) | collective-permute-done | bytes 442400 | tf_op jit(solution)/shard_map/ppermute | solution.py:634
  83.2 1.3 collective-permute-done.28.refs_6_
  85.2 6.0 %ffn_down.1 = (bf16[512,768]{1,0:T(8,128)(2,1)}, f32[512,768]{1,0:T(8,128)S(1)}, bf16[512,768]{1,0:T(8,128)(2,1)S(1)}, f32[16,768]{1,0:T(8,128)S(1)}, bf16[4,768,768]{2,1,0:T(8,128)(2,1)S(1)}) custom-call(s32[4]{0:T(128)S(1)} %pad_add_fusion.info, f32[512,768]{1,0:T(8,128)S(1)} %get-tuple-element.154.skip, f32[8,768]{1,0:T(8,128)S(1)} %convert_element_type.421.vec, ...), custom_call_target="tpu_custom_call" | custom-call | flops 13200000000 | bytes 1048576 | tf_op jit(solution)/shard_map/ffn_down/pallas_call | solution.py:358
  91.2 2.3 %down_grad.2 = (bf16[2,2,2,96,768]{4,3,2,1,0:T(8,128)(2,1)S(1)}, bf16[2,2,2,96,768]{4,3,2,1,0:T(8,128)(2,1)S(1)}, f32[8,128]{1,0:T(8,128)S(1)}) custom-call(s32[4]{0:T(128)S(1)} %pad_add_fusion.info, bf16[4,512,768]{2,1,0:T(8,128)(2,1)S(1)} %get-tuple-element.164.act, bf16[512,768]{1,0:T(8,128)(2,1)S(1)} %get-tuple-element.171.branch_low, ...), custom_call_target="tpu_custom_call" | custom-call | flops 2200000000 | bytes 1048576 | tf_op jit(solution)/shard_map/down_grad/pallas_call | solution.py:335
  93.7 2.9 %down_grad.3 = (bf16[2,2,2,96,768]{4,3,2,1,0:T(8,128)(2,1)S(1)}, bf16[2,2,2,96,768]{4,3,2,1,0:T(8,128)(2,1)S(1)}, f32[8,128]{1,0:T(8,128)}) custom-call(s32[4]{0:T(128)S(1)} %pad_add_fusion.info, bf16[4,512,768]{2,1,0:T(8,128)(2,1)S(1)} %get-tuple-element.164.act, bf16[512,768]{1,0:T(8,128)(2,1)S(1)} %get-tuple-element.171.branch_low, ...), custom_call_target="tpu_custom_call" | custom-call | flops 2200000000 | bytes 1048576 | tf_op jit(solution)/shard_map/down_grad/pallas_call | solution.py:335
  97.3 1.1 collective-permute-start.32
  98.4 1.0 collective-permute-done.31
  99.8 1.1 collective-permute-start.33
  100.9 10.5 %ffn_back.1 = (f32[512,768]{1,0:T(8,128)S(1)}, bf16[512,768]{1,0:T(8,128)(2,1)S(1)}, f32[16,768]{1,0:T(8,128)S(1)}, bf16[2,2,4,96,768]{4,3,2,1,0:T(8,128)(2,1)S(1)}, bf16[2,2,4,96,768]{4,3,2,1,0:T(8,128)(2,1)S(1)}) custom-call(s32[4]{0:T(128)S(1)} %pad_add_fusion.info, bf16[512,768]{1,0:T(8,128)(2,1)S(1)} %get-tuple-element.171.branch_low, ...), custom_call_target="tpu_custom_call" | custom-call | flops 12099999744 | bytes 1048576 | tf_op jit(solution)/shard_map/ffn_back/pallas_call | solution.py:410
  111.4 2.2 collective-permute-done.33
  114.0 7.9 %attn_back.2 = (f32[16,768]{1,0:T(8,128)S(1)}, bf16[2,576,512]{2,1,0:T(8,128)(2,1)S(1)}, bf16[2,2,2,96,768]{4,3,2,1,0:T(8,128)(2,1)S(1)}, bf16[2,2,2,96,768]{4,3,2,1,0:T(8,128)(2,1)S(1)}) custom-call(s32[4]{0:T(128)S(1)} %pad_add_fusion.info, bf16[512,768]{1,0:T(8,128)(2,1)S(1)} %copy-done.7, bf16[512,768]{1,0:T(8,128)(2,1)S(1)} %get-tuple-element.193.residual_low, ...), custom_call_target="tpu_custom_call" | custom-call | flops 9900000256 | bytes 1048576 | tf_op jit(solution)/shard_map/attn_back/pallas_call | solution.py:494
  122.0 1.9 collective-permute-done.35
  124.7 1.1 collective-permute-start.36
  126.6 8.4 %attn_back.3 = (f32[16,768]{1,0:T(8,128)S(1)}, bf16[2,576,512]{2,1,0:T(8,128)(2,1)S(1)}, bf16[2,2,2,96,768]{4,3,2,1,0:T(8,128)(2,1)S(1)}, bf16[2,2,2,96,768]{4,3,2,1,0:T(8,128)(2,1)S(1)}) custom-call(s32[4]{0:T(128)S(1)} %pad_add_fusion.info, bf16[512,768]{1,0:T(8,128)(2,1)S(1)} %copy-done.7, bf16[512,768]{1,0:T(8,128)(2,1)S(1)} %get-tuple-element.193.residual_low, ...), custom_call_target="tpu_custom_call" | custom-call | flops 9900000256 | bytes 1048576 | tf_op jit(solution)/shard_map/attn_back/pallas_call | solution.py:494
  135.0 1.5 collective-permute-done.38
  136.5 4.5 %collective-permute-done.36 = bf16[2,4,96,768]{3,2,1,0:T(8,128)(2,1)S(1)} collective-permute-done((bf16[2,4,96,768]{3,2,1,0:T(8,128)(2,1)S(1)}, bf16[2,4,96,768]{3,2,1,0:T(8,128)(2,1)S(1)}, u32[]{:S(2)}, u32[]{:S(2)}) %collective-permute-start.36) | collective-permute-done | bytes 1179680 | tf_op jit(solution)/shard_map/ppermute | solution.py:634
  142.9 3.6 %grad_tokens.1 = bf16[512,768]{1,0:T(8,128)(2,1)} custom-call(f32[512,768]{1,0:T(8,128)S(1)} %get-tuple-element.211.grad, bf16[2,576,512]{2,1,0:T(8,128)(2,1)S(1)} %get-tuple-element.212.joint_a, bf16[2,576,512]{2,1,0:T(8,128)(2,1)S(1)} %get-tuple-element.213.joint_b, bf16[192,768]{1,0:T(8,128)(2,1)S(1)} %bitcast.171, bf16[192,768]{1,0:T(8,128)(2,1)S(1)} %bitcast.173, ...), custom_call_target="tpu_custom_call" | custom-call | flops 4400000000 | bytes 1048576 | tf_op jit(solution)/shard_map/grad_tokens/pallas_call | solution.py:523
  147.0 4.0 %collective-permute-done.40 = bf16[4,96,768]{2,1,0:T(8,128)(2,1)S(1)} collective-permute-done((bf16[4,96,768]{2,1,0:T(8,128)(2,1)S(1)}, bf16[4,96,768]{2,1,0:T(8,128)(2,1)S(1)}, u32[]{:S(2)}, u32[]{:S(2)}) %collective-permute-start.40) | collective-permute-done | bytes 589856 | tf_op jit(solution)/shard_map/ppermute | solution.py:634
  151.9 1.1 collective-permute-start.43
  154.0 9.9 %collective-permute-done.44 = bf16[1,2,96,768]{3,2,1,0:T(8,128)(2,1)S(1)} collective-permute-done((bf16[1,2,96,768]{3,2,1,0:T(8,128)(2,1)S(1)}, bf16[1,2,96,768]{3,2,1,0:T(8,128)(2,1)S(1)}, u32[]{:S(2)}, u32[]{:S(2)}) %collective-permute-start.44) | collective-permute-done | bytes 294944 | tf_op jit(solution)/shard_map/ppermute | solution.py:634
  163.9 4.6 %collective-permute-done.43 = bf16[784,768]{1,0:T(8,128)(2,1)S(1)} collective-permute-done((bf16[784,768]{1,0:T(8,128)(2,1)S(1)}, bf16[784,768]{1,0:T(8,128)(2,1)S(1)}, u32[]{:S(2)}, u32[]{:S(2)}) %collective-permute-start.43) | collective-permute-done | bytes 1204256 | tf_op jit(solution)/shard_map/ppermute | solution.py:634
  169.8 5.9 %collective-permute-done.46 = bf16[1,96,768]{2,1,0:T(8,128)(2,1)S(1)} collective-permute-done((bf16[1,96,768]{2,1,0:T(8,128)(2,1)S(1)}, bf16[1,96,768]{2,1,0:T(8,128)(2,1)S(1)}, u32[]{:S(2)}, u32[]{:S(2)}) %collective-permute-start.46) | collective-permute-done | bytes 147488 | tf_op jit(solution)/shard_map/ppermute | solution.py:634
  175.7 3.2 %collective-permute-done.45 = bf16[400,768]{1,0:T(8,128)(2,1)S(1)} collective-permute-done((bf16[400,768]{1,0:T(8,128)(2,1)S(1)}, bf16[400,768]{1,0:T(8,128)(2,1)S(1)}, u32[]{:S(2)}, u32[]{:S(2)}) %collective-permute-start.45) | collective-permute-done | bytes 614432 | tf_op jit(solution)/shard_map/ppermute | solution.py:634
  179.7 1.1 collective-permute-start.50
  181.4 1.9 collective-permute-start.47
  183.4 2.5 %collective-permute-start.49 = (bf16[112,768]{1,0:T(8,128)(2,1)S(1)}, bf16[112,768]{1,0:T(8,128)(2,1)S(1)}, u32[]{:S(2)}, u32[]{:S(2)}) collective-permute-start(bf16[112,768]{1,0:T(8,128)(2,1)S(1)} %get-tuple-element.281), channel_id=1, source_target_pairs={{0,1},{1,0},{2,3},{3,2},{4,5},{5,4},{6,7},{7,6},{8,9},{9,8},{10,11... | collective-permute-start | bytes 516104 | tf_op jit(solution)/shard_map/ppermute | solution.py:634
  185.9 4.7 %collective-permute-done.47 = bf16[112,768]{1,0:T(8,128)(2,1)S(1)} collective-permute-done((bf16[112,768]{1,0:T(8,128)(2,1)S(1)}, bf16[112,768]{1,0:T(8,128)(2,1)S(1)}, u32[]{:S(2)}, u32[]{:S(2)}) %collective-permute-start.47) | collective-permute-done | bytes 172064 | tf_op jit(solution)/shard_map/ppermute | solution.py:634
  190.6 5.6 %collective-permute-done.48 = bf16[112,768]{1,0:T(8,128)(2,1)S(1)} collective-permute-done((bf16[112,768]{1,0:T(8,128)(2,1)S(1)}, bf16[112,768]{1,0:T(8,128)(2,1)S(1)}, u32[]{:S(2)}, u32[]{:S(2)}) %collective-permute-start.48) | collective-permute-done | bytes 172064 | tf_op jit(solution)/shard_map/ppermute | solution.py:634
  197.1 1.1 broadcast_select_fusion
  198.2 1.0 collective-permute-start.60
  199.3 1.1 collective-permute-start.52
  200.4 1.7 collective-permute-start.53
  204.3 3.8 %collective-permute-done.60.corner = bf16[2,96,768]{2,1,0:T(8,128)(2,1)S(1)} collective-permute-done((bf16[2,96,768]{2,1,0:T(8,128)(2,1)S(1)}, bf16[2,96,768]{2,1,0:T(8,128)(2,1)S(1)}, u32[]{:S(2)}, u32[]{:S(2)}) %collective-permute-start.60) | collective-permute-done | bytes 294944 | tf_op jit(solution)/shard_map/ppermute | solution.py:634
  208.6 3.0 %finish_ffn.1 = (f32[768,768]{1,0:T(8,128)}, f32[768,768]{1,0:T(8,128)}, f32[8,128]{1,0:T(8,128)S(1)}) custom-call(s32[4]{0:T(128)S(1)} %pad_add_fusion.info, bf16[3,2,96,768]{3,2,1,0:T(8,128)(2,1)S(1)} %pad_maximum_fusion.3.held, bf16[3,2,96,768]{3,2,1,0:T(8,128)(2,1)S(1)} %collective-permute-done.55.held_mates), custom_call_target="tpu_custom_call" | custom-call | flops 3300000000 | bytes 1048576 | tf_op jit(solution)/shard_map/finish_ffn/pallas_call | solution.py:550
  212.9 1.6 finish_ffn_corner.1
  215.1 2.1 finish_attn.1
  (192 shorter events, 24.6 us)
Async XLA Ops:
  0.7 16.2 %copy-start.3 = (bf16[768,192]{0,1:T(8,128)(2,1)S(1)}, bf16[768,192]{0,1:T(8,128)(2,1)}, u32[]{:S(2)}) copy-start(bf16[768,192]{0,1:T(8,128)(2,1)} %param.23) | copy-start | bytes 884740
  0.7 16.2 %copy-start.2 = (bf16[768,192]{0,1:T(8,128)(2,1)S(1)}, bf16[768,192]{0,1:T(8,128)(2,1)}, u32[]{:S(2)}) copy-start(bf16[768,192]{0,1:T(8,128)(2,1)} %param.22) | copy-start | bytes 884740
  2.8 11.7 %collective-permute-start = (bf16[96,768]{1,0:T(8,128)(2,1)}, bf16[96,768]{1,0:T(8,128)(2,1)S(1)}, u32[]{:S(2)}, u32[]{:S(2)}) collective-permute-start(bf16[96,768]{1,0:T(8,128)(2,1)} %fusion.30), channel_id=1, source_target_pairs={{0,1},{1,0},{2,3},{3,2},{4,6},{5,7},{6,4},{7,5},{8,9},{9,8},{10,11... | collective-permute-start | bytes 442376 | tf_op jit(solution)/shard_map/ppermute | solution.py:634
  5.9 14.0 %collective-permute-start.1 = (bf16[96,768]{1,0:T(8,128)(2,1)}, bf16[96,768]{1,0:T(8,128)(2,1)S(1)}, u32[]{:S(2)}, u32[]{:S(2)}) collective-permute-start(bf16[96,768]{1,0:T(8,128)(2,1)} %fusion.30), channel_id=1, source_target_pairs={{0,2},{1,3},{2,0},{3,1},{4,5},{5,4},{6,7},{7,6},{8,10},{9,11},{10,... | collective-permute-start | bytes 442376 | tf_op jit(solution)/shard_map/ppermute | solution.py:634
  9.4 11.4 %collective-permute-start.4 = (bf16[96,768]{1,0:T(8,128)(2,1)S(1)}, bf16[96,768]{1,0:T(8,128)(2,1)S(1)}, u32[]{:S(2)}, u32[]{:S(2)}) collective-permute-start(bf16[96,768]{1,0:T(8,128)(2,1)S(1)} %constant_dynamic-slice_fusion), channel_id=1, source_target_pairs={{0,1},{1,0},{2,3},{3,2},{4,6},{5,7},{6,4},{7,5},{8,9},{9,8},{10,11... | collective-permute-start | bytes 442376 | tf_op jit(solution)/shard_map/ppermute | solution.py:634
  14.5 9.5 %collective-permute-start.2 = (bf16[96,768]{1,0:T(8,128)(2,1)S(1)}, bf16[96,768]{1,0:T(8,128)(2,1)S(1)}, u32[]{:S(2)}, u32[]{:S(2)}) collective-permute-start(bf16[96,768]{1,0:T(8,128)(2,1)S(1)} %collective-permute-done), channel_id=1, source_target_pairs={{0,2},{1,3},{2,0},{3,1},{4,5},{5,4},{6,7},{7,6},{8,10},{9,11},{10,... | collective-permute-start | bytes 442376 | tf_op jit(solution)/shard_map/ppermute | solution.py:634
  14.5 9.5 %collective-permute-start.3 = (bf16[104,768]{1,0:T(8,128)(2,1)}, bf16[104,768]{1,0:T(8,128)(2,1)S(1)}, u32[]{:S(2)}, u32[]{:S(2)}) collective-permute-start(bf16[104,768]{1,0:T(8,128)(2,1)} %pad_maximum_fusion.13), channel_id=1, source_target_pairs={{0,1},{1,0},{2,3},{3,2},{4,6},{5,7},{6,4},{7,5},{8,9},{9,8},{10,11... | collective-permute-start | bytes 479240 | tf_op jit(solution)/shard_map/ppermute | solution.py:634
  24.0 12.7 %collective-permute-start.6 = (bf16[3,96,768]{2,1,0:T(8,128)(2,1)S(1)}, bf16[3,96,768]{2,1,0:T(8,128)(2,1)S(1)}, u32[]{:S(2)}, u32[]{:S(2)}) collective-permute-start(bf16[3,96,768]{2,1,0:T(8,128)(2,1)S(1)} %pad_maximum_fusion.7.refs_0_), channel_id=1, source_target_pairs={{0,8},{1,9},{2,10},{3,11},{4,20},{5,21},{6,22},{7,23},{8,0},{9,1},... | collective-permute-start | bytes 1327112 | tf_op jit(solution)/shard_map/ppermute | solution.py:634
  25.9 7.4 %collective-permute-start.7 = (bf16[104,768]{1,0:T(8,128)(2,1)}, bf16[104,768]{1,0:T(8,128)(2,1)}, u32[]{:S(2)}, u32[]{:S(2)}) collective-permute-start(bf16[104,768]{1,0:T(8,128)(2,1)} %pad_maximum_fusion.13), channel_id=1, source_target_pairs={{0,2},{1,3},{2,0},{3,1},{4,5},{5,4},{6,7},{7,6},{8,10},{9,11},{10,... | collective-permute-start | bytes 479240 | tf_op jit(solution)/shard_map/ppermute | solution.py:634
  27.2 9.5 %collective-permute-start.8 = (bf16[104,768]{1,0:T(8,128)(2,1)S(1)}, bf16[104,768]{1,0:T(8,128)(2,1)}, u32[]{:S(2)}, u32[]{:S(2)}) collective-permute-start(bf16[104,768]{1,0:T(8,128)(2,1)S(1)} %collective-permute-done.3), channel_id=1, source_target_pairs={{0,2},{1,3},{2,0},{3,1},{4,5},{5,4},{6,7},{7,6},{8,10},{9,11},{10,... | collective-permute-start | bytes 479240 | tf_op jit(solution)/shard_map/ppermute | solution.py:634
  28.8 13.9 %collective-permute-start.11 = (bf16[96,768]{1,0:T(8,128)(2,1)}, bf16[96,768]{1,0:T(8,128)(2,1)}, u32[]{:S(2)}, u32[]{:S(2)}) collective-permute-start(bf16[96,768]{1,0:T(8,128)(2,1)} %copy-done.14), channel_id=1, source_target_pairs={{0,2},{1,3},{2,0},{3,1},{4,5},{5,4},{6,7},{7,6},{8,10},{9,11},{10,... | collective-permute-start | bytes 442376 | tf_op jit(solution)/shard_map/ppermute | solution.py:634
  30.2 12.7 %collective-permute-start.5 = (bf16[3,96,768]{2,1,0:T(8,128)(2,1)S(1)}, bf16[3,96,768]{2,1,0:T(8,128)(2,1)S(1)}, u32[]{:S(2)}, u32[]{:S(2)}) collective-permute-start(bf16[3,96,768]{2,1,0:T(8,128)(2,1)S(1)} %pad_maximum_fusion.7.refs_0_), channel_id=1, source_target_pairs={{0,16},{1,17},{2,18},{3,19},{4,12},{5,13},{6,14},{7,15},{8,24},{9,... | collective-permute-start | bytes 1327112 | tf_op jit(solution)/shard_map/ppermute | solution.py:634
  38.6 11.7 %collective-permute-start.9 = (bf16[3,96,768]{2,1,0:T(8,128)(2,1)S(1)}, bf16[3,96,768]{2,1,0:T(8,128)(2,1)S(1)}, u32[]{:S(2)}, u32[]{:S(2)}) collective-permute-start(bf16[3,96,768]{2,1,0:T(8,128)(2,1)S(1)} %collective-permute-done.6.refs_1_), channel_id=1, source_target_pairs={{0,16},{1,17},{2,18},{3,19},{4,12},{5,13},{6,14},{7,15},{8,24},{9,... | collective-permute-start | bytes 1327112 | tf_op jit(solution)/shard_map/ppermute | solution.py:634
  42.5 8.4 %collective-permute-start.10 = (bf16[3,96,768]{2,1,0:T(8,128)(2,1)S(1)}, bf16[3,96,768]{2,1,0:T(8,128)(2,1)S(1)}, u32[]{:S(2)}, u32[]{:S(2)}) collective-permute-start(bf16[3,96,768]{2,1,0:T(8,128)(2,1)S(1)} %slice.297.refs_0_), channel_id=1, source_target_pairs={{0,8},{1,9},{2,10},{3,11},{4,20},{5,21},{6,22},{7,23},{8,0},{9,1},... | collective-permute-start | bytes 1327112 | tf_op jit(solution)/shard_map/ppermute | solution.py:634
  42.6 7.7 %collective-permute-start.12 = (bf16[96,768]{1,0:T(8,128)(2,1)S(1)}, bf16[96,768]{1,0:T(8,128)(2,1)S(1)}, u32[]{:S(2)}, u32[]{:S(2)}) collective-permute-start(bf16[96,768]{1,0:T(8,128)(2,1)S(1)} %copy-done.13), channel_id=1, source_target_pairs={{0,2},{1,3},{2,0},{3,1},{4,5},{5,4},{6,7},{7,6},{8,10},{9,11},{10,... | collective-permute-start | bytes 442376 | tf_op jit(solution)/shard_map/ppermute | solution.py:634
  42.8 9.6 %collective-permute-start.13 = (bf16[3,96,768]{2,1,0:T(8,128)(2,1)S(1)}, bf16[3,96,768]{2,1,0:T(8,128)(2,1)S(1)}, u32[]{:S(2)}, u32[]{:S(2)}) collective-permute-start(bf16[3,96,768]{2,1,0:T(8,128)(2,1)S(1)} %pad_maximum_fusion.7.refs_0_), channel_id=1, source_target_pairs={{0,4},{1,5},{2,6},{3,7},{4,0},{5,1},{6,2},{7,3},{8,12},{9,13},{10,... | collective-permute-start | bytes 1327112 | tf_op jit(solution)/shard_map/ppermute | solution.py:634
  42.9 10.4 %collective-permute-start.14 = (bf16[3,96,768]{2,1,0:T(8,128)(2,1)S(1)}, bf16[3,96,768]{2,1,0:T(8,128)(2,1)S(1)}, u32[]{:S(2)}, u32[]{:S(2)}) collective-permute-start(bf16[3,96,768]{2,1,0:T(8,128)(2,1)S(1)} %collective-permute-done.6.refs_1_), channel_id=1, source_target_pairs={{0,4},{1,5},{2,6},{3,7},{4,0},{5,1},{6,2},{7,3},{8,12},{9,13},{10,... | collective-permute-start | bytes 1327112 | tf_op jit(solution)/shard_map/ppermute | solution.py:634
  50.9 3.7 %collective-permute-start.15 = (bf16[3,96,768]{2,1,0:T(8,128)(2,1)S(1)}, bf16[3,96,768]{2,1,0:T(8,128)(2,1)S(1)}, u32[]{:S(2)}, u32[]{:S(2)}) collective-permute-start(bf16[3,96,768]{2,1,0:T(8,128)(2,1)S(1)} %collective-permute-done.5.refs_2_), channel_id=1, source_target_pairs={{0,4},{1,5},{2,6},{3,7},{4,0},{5,1},{6,2},{7,3},{8,12},{9,13},{10,... | collective-permute-start | bytes 1327112 | tf_op jit(solution)/shard_map/ppermute | solution.py:634
  50.9 3.7 %collective-permute-start.16 = (bf16[3,96,768]{2,1,0:T(8,128)(2,1)S(1)}, bf16[3,96,768]{2,1,0:T(8,128)(2,1)S(1)}, u32[]{:S(2)}, u32[]{:S(2)}) collective-permute-start(bf16[3,96,768]{2,1,0:T(8,128)(2,1)S(1)} %collective-permute-done.9.refs_3_), channel_id=1, source_target_pairs={{0,4},{1,5},{2,6},{3,7},{4,0},{5,1},{6,2},{7,3},{8,12},{9,13},{10,... | collective-permute-start | bytes 1327112 | tf_op jit(solution)/shard_map/ppermute | solution.py:634
  51.4 15.2 %collective-permute-start.17 = (bf16[3,96,768]{2,1,0:T(8,128)(2,1)S(1)}, bf16[3,96,768]{2,1,0:T(8,128)(2,1)S(1)}, u32[]{:S(2)}, u32[]{:S(2)}) collective-permute-start(bf16[3,96,768]{2,1,0:T(8,128)(2,1)S(1)} %slice.297.refs_0_), channel_id=1, source_target_pairs={{0,16},{1,17},{2,18},{3,19},{4,12},{5,13},{6,14},{7,15},{8,24},{9,... | collective-permute-start | bytes 1327112 | tf_op jit(solution)/shard_map/ppermute | solution.py:634
  52.4 17.3 %collective-permute-start.20 = (bf16[3,96,768]{2,1,0:T(8,128)(2,1)S(1)}, bf16[3,96,768]{2,1,0:T(8,128)(2,1)S(1)}, u32[]{:S(2)}, u32[]{:S(2)}) collective-permute-start(bf16[3,96,768]{2,1,0:T(8,128)(2,1)S(1)} %slice.297.refs_0_), channel_id=1, source_target_pairs={{0,4},{1,5},{2,6},{3,7},{4,0},{5,1},{6,2},{7,3},{8,12},{9,13},{10,... | collective-permute-start | bytes 1327112 | tf_op jit(solution)/shard_map/ppermute | solution.py:634
  53.3 15.9 %collective-permute-start.18 = (bf16[3,96,768]{2,1,0:T(8,128)(2,1)S(1)}, bf16[3,96,768]{2,1,0:T(8,128)(2,1)S(1)}, u32[]{:S(2)}, u32[]{:S(2)}) collective-permute-start(bf16[3,96,768]{2,1,0:T(8,128)(2,1)S(1)} %collective-permute-done.10.refs_1_), channel_id=1, source_target_pairs={{0,16},{1,17},{2,18},{3,19},{4,12},{5,13},{6,14},{7,15},{8,24},{9,... | collective-permute-start | bytes 1327112 | tf_op jit(solution)/shard_map/ppermute | solution.py:634
  54.5 15.9 %collective-permute-start.21 = (bf16[3,96,768]{2,1,0:T(8,128)(2,1)S(1)}, bf16[3,96,768]{2,1,0:T(8,128)(2,1)S(1)}, u32[]{:S(2)}, u32[]{:S(2)}) collective-permute-start(bf16[3,96,768]{2,1,0:T(8,128)(2,1)S(1)} %collective-permute-done.10.refs_1_), channel_id=1, source_target_pairs={{0,4},{1,5},{2,6},{3,7},{4,0},{5,1},{6,2},{7,3},{8,12},{9,13},{10,... | collective-permute-start | bytes 1327112 | tf_op jit(solution)/shard_map/ppermute | solution.py:634
  54.6 14.6 %collective-permute-start.19 = (bf16[3,96,768]{2,1,0:T(8,128)(2,1)S(1)}, bf16[3,96,768]{2,1,0:T(8,128)(2,1)S(1)}, u32[]{:S(2)}, u32[]{:S(2)}) collective-permute-start(bf16[3,96,768]{2,1,0:T(8,128)(2,1)S(1)} %pad_maximum_fusion.8.refs_0_), channel_id=1, source_target_pairs={{0,8},{1,9},{2,10},{3,11},{4,20},{5,21},{6,22},{7,23},{8,0},{9,1},... | collective-permute-start | bytes 1327112 | tf_op jit(solution)/shard_map/ppermute | solution.py:634
  69.2 2.6 %collective-permute-start.22 = (bf16[3,96,768]{2,1,0:T(8,128)(2,1)S(1)}, bf16[3,96,768]{2,1,0:T(8,128)(2,1)S(1)}, u32[]{:S(2)}, u32[]{:S(2)}) collective-permute-start(bf16[3,96,768]{2,1,0:T(8,128)(2,1)S(1)} %collective-permute-done.17.refs_2_), channel_id=1, source_target_pairs={{0,4},{1,5},{2,6},{3,7},{4,0},{5,1},{6,2},{7,3},{8,12},{9,13},{10,... | collective-permute-start | bytes 1327112 | tf_op jit(solution)/shard_map/ppermute | solution.py:634
  69.2 2.6 %collective-permute-start.23 = (bf16[3,96,768]{2,1,0:T(8,128)(2,1)S(1)}, bf16[3,96,768]{2,1,0:T(8,128)(2,1)S(1)}, u32[]{:S(2)}, u32[]{:S(2)}) collective-permute-start(bf16[3,96,768]{2,1,0:T(8,128)(2,1)S(1)} %collective-permute-done.18.refs_3_), channel_id=1, source_target_pairs={{0,4},{1,5},{2,6},{3,7},{4,0},{5,1},{6,2},{7,3},{8,12},{9,13},{10,... | collective-permute-start | bytes 1327112 | tf_op jit(solution)/shard_map/ppermute | solution.py:634
  69.7 10.8 %collective-permute-start.24 = (bf16[3,96,768]{2,1,0:T(8,128)(2,1)S(1)}, bf16[3,96,768]{2,1,0:T(8,128)(2,1)S(1)}, u32[]{:S(2)}, u32[]{:S(2)}) collective-permute-start(bf16[3,96,768]{2,1,0:T(8,128)(2,1)S(1)} %pad_maximum_fusion.8.refs_0_), channel_id=1, source_target_pairs={{0,16},{1,17},{2,18},{3,19},{4,12},{5,13},{6,14},{7,15},{8,24},{9,... | collective-permute-start | bytes 1327112 | tf_op jit(solution)/shard_map/ppermute | solution.py:634
  69.7 13.6 %collective-permute-start.26 = (bf16[3,96,768]{2,1,0:T(8,128)(2,1)S(1)}, bf16[3,96,768]{2,1,0:T(8,128)(2,1)S(1)}, u32[]{:S(2)}, u32[]{:S(2)}) collective-permute-start(bf16[3,96,768]{2,1,0:T(8,128)(2,1)S(1)} %pad_maximum_fusion.8.refs_0_), channel_id=1, source_target_pairs={{0,4},{1,5},{2,6},{3,7},{4,0},{5,1},{6,2},{7,3},{8,12},{9,13},{10,... | collective-permute-start | bytes 1327112 | tf_op jit(solution)/shard_map/ppermute | solution.py:634
  70.5 12.3 %collective-permute-start.25 = (bf16[3,96,768]{2,1,0:T(8,128)(2,1)S(1)}, bf16[3,96,768]{2,1,0:T(8,128)(2,1)S(1)}, u32[]{:S(2)}, u32[]{:S(2)}) collective-permute-start(bf16[3,96,768]{2,1,0:T(8,128)(2,1)S(1)} %collective-permute-done.19.refs_1_), channel_id=1, source_target_pairs={{0,16},{1,17},{2,18},{3,19},{4,12},{5,13},{6,14},{7,15},{8,24},{9,... | collective-permute-start | bytes 1327112 | tf_op jit(solution)/shard_map/ppermute | solution.py:634
  71.8 11.5 %collective-permute-start.27 = (bf16[3,96,768]{2,1,0:T(8,128)(2,1)S(1)}, bf16[3,96,768]{2,1,0:T(8,128)(2,1)S(1)}, u32[]{:S(2)}, u32[]{:S(2)}) collective-permute-start(bf16[3,96,768]{2,1,0:T(8,128)(2,1)S(1)} %collective-permute-done.19.refs_1_), channel_id=1, source_target_pairs={{0,4},{1,5},{2,6},{3,7},{4,0},{5,1},{6,2},{7,3},{8,12},{9,13},{10,... | collective-permute-start | bytes 1327112 | tf_op jit(solution)/shard_map/ppermute | solution.py:634
  82.7 1.8 collective-permute-start.28
  82.7 2.4 %collective-permute-start.29 = (bf16[3,96,768]{2,1,0:T(8,128)(2,1)S(1)}, bf16[3,96,768]{2,1,0:T(8,128)(2,1)S(1)}, u32[]{:S(2)}, u32[]{:S(2)}) collective-permute-start(bf16[3,96,768]{2,1,0:T(8,128)(2,1)S(1)} %collective-permute-done.25.refs_3_), channel_id=1, source_target_pairs={{0,4},{1,5},{2,6},{3,7},{4,0},{5,1},{6,2},{7,3},{8,12},{9,13},{10,... | collective-permute-start | bytes 1327112 | tf_op jit(solution)/shard_map/ppermute | solution.py:634
  93.5 3.1 %collective-permute-start.30 = (bf16[2,2,2,96,768]{4,3,2,1,0:T(8,128)(2,1)S(1)}, bf16[2,2,2,96,768]{4,3,2,1,0:T(8,128)(2,1)S(1)}, u32[]{:S(2)}, u32[]{:S(2)}) collective-permute-start(bf16[2,2,2,96,768]{4,3,2,1,0:T(8,128)(2,1)S(1)} %get-tuple-element.174), channel_id=1, source_target_pairs={{0,4},{1,5},{2,6},{3,7},{4,0},{5,1},{6,2},{7,3},{8,12},{9,13},{10,... | collective-permute-start | bytes 3538952 | tf_op jit(solution)/shard_map/ppermute | solution.py:634
  96.6 2.8 %collective-permute-start.31 = (bf16[2,2,2,96,768]{4,3,2,1,0:T(8,128)(2,1)S(1)}, bf16[2,2,2,96,768]{4,3,2,1,0:T(8,128)(2,1)S(1)}, u32[]{:S(2)}, u32[]{:S(2)}) collective-permute-start(bf16[2,2,2,96,768]{4,3,2,1,0:T(8,128)(2,1)S(1)} %get-tuple-element.177), channel_id=1, source_target_pairs={{0,4},{1,5},{2,6},{3,7},{4,0},{5,1},{6,2},{7,3},{8,12},{9,13},{10,... | collective-permute-start | bytes 3538952 | tf_op jit(solution)/shard_map/ppermute | solution.py:634
  97.3 14.1 %collective-permute-start.32 = (bf16[2,2,96,768]{3,2,1,0:T(8,128)(2,1)S(1)}, bf16[2,2,96,768]{3,2,1,0:T(8,128)(2,1)S(1)}, u32[]{:S(2)}, u32[]{:S(2)}) collective-permute-start(bf16[2,2,96,768]{3,2,1,0:T(8,128)(2,1)S(1)} %get-tuple-element.264), channel_id=1, source_target_pairs={{0,8},{1,9},{2,10},{3,11},{4,20},{5,21},{6,22},{7,23},{8,0},{9,1},... | collective-permute-start | bytes 1769480 | tf_op jit(solution)/shard_map/ppermute | solution.py:634
  99.8 13.8 %collective-permute-start.33 = (bf16[2,2,96,768]{3,2,1,0:T(8,128)(2,1)S(1)}, bf16[2,2,96,768]{3,2,1,0:T(8,128)(2,1)S(1)}, u32[]{:S(2)}, u32[]{:S(2)}) collective-permute-start(bf16[2,2,96,768]{3,2,1,0:T(8,128)(2,1)S(1)} %get-tuple-element.266), channel_id=1, source_target_pairs={{0,8},{1,9},{2,10},{3,11},{4,20},{5,21},{6,22},{7,23},{8,0},{9,1},... | collective-permute-start | bytes 1769480 | tf_op jit(solution)/shard_map/ppermute | solution.py:634
  113.6 10.3 %collective-permute-start.34 = (bf16[2,2,4,96,768]{4,3,2,1,0:T(8,128)(2,1)S(1)}, bf16[2,2,4,96,768]{4,3,2,1,0:T(8,128)(2,1)S(1)}, u32[]{:S(2)}, u32[]{:S(2)}) collective-permute-start(bf16[2,2,4,96,768]{4,3,2,1,0:T(8,128)(2,1)S(1)} %get-tuple-element.190), channel_id=1, source_target_pairs={{0,4},{1,5},{2,6},{3,7},{4,0},{5,1},{6,2},{7,3},{8,12},{9,13},{10,... | collective-permute-start | bytes 7077896 | tf_op jit(solution)/shard_map/ppermute | solution.py:634
  114.0 9.9 %collective-permute-start.35 = (bf16[4,96,768]{2,1,0:T(8,128)(2,1)S(1)}, bf16[4,96,768]{2,1,0:T(8,128)(2,1)S(1)}, u32[]{:S(2)}, u32[]{:S(2)}) collective-permute-start(bf16[4,96,768]{2,1,0:T(8,128)(2,1)S(1)} %pad_maximum_fusion.5), channel_id=1, source_target_pairs={{0,16},{1,17},{2,18},{3,19},{4,12},{5,13},{6,14},{7,15},{8,24},{9,... | collective-permute-start | bytes 1769480 | tf_op jit(solution)/shard_map/ppermute | solution.py:634
  124.7 16.3 %collective-permute-start.36 = (bf16[2,4,96,768]{3,2,1,0:T(8,128)(2,1)S(1)}, bf16[2,4,96,768]{3,2,1,0:T(8,128)(2,1)S(1)}, u32[]{:S(2)}, u32[]{:S(2)}) collective-permute-start(bf16[2,4,96,768]{3,2,1,0:T(8,128)(2,1)S(1)} %get-tuple-element.262), channel_id=1, source_target_pairs={{0,8},{1,9},{2,10},{3,11},{4,20},{5,21},{6,22},{7,23},{8,0},{9,1},... | collective-permute-start | bytes 3538952 | tf_op jit(solution)/shard_map/ppermute | solution.py:634
  125.8 15.1 %collective-permute-start.37 = (bf16[2,2,2,96,768]{4,3,2,1,0:T(8,128)(2,1)S(1)}, bf16[2,2,2,96,768]{4,3,2,1,0:T(8,128)(2,1)S(1)}, u32[]{:S(2)}, u32[]{:S(2)}) collective-permute-start(bf16[2,2,2,96,768]{4,3,2,1,0:T(8,128)(2,1)S(1)} %get-tuple-element.202), channel_id=1, source_target_pairs={{0,4},{1,5},{2,6},{3,7},{4,0},{5,1},{6,2},{7,3},{8,12},{9,13},{10,... | collective-permute-start | bytes 3538952 | tf_op jit(solution)/shard_map/ppermute | solution.py:634
  126.0 10.5 %collective-permute-start.38 = (bf16[1,2,96,768]{3,2,1,0:T(8,128)(2,1)S(1)}, bf16[1,2,96,768]{3,2,1,0:T(8,128)(2,1)S(1)}, u32[]{:S(2)}, u32[]{:S(2)}) collective-permute-start(bf16[1,2,96,768]{3,2,1,0:T(8,128)(2,1)S(1)} %fusion.24), channel_id=1, source_target_pairs={{0,2},{1,3},{2,0},{3,1},{4,5},{5,4},{6,7},{7,6},{8,10},{9,11},{10,... | collective-permute-start | bytes 884744 | tf_op jit(solution)/shard_map/ppermute | solution.py:634
  140.9 10.1 %collective-permute-start.39 = (bf16[2,2,2,96,768]{4,3,2,1,0:T(8,128)(2,1)S(1)}, bf16[2,2,2,96,768]{4,3,2,1,0:T(8,128)(2,1)S(1)}, u32[]{:S(2)}, u32[]{:S(2)}) collective-permute-start(bf16[2,2,2,96,768]{4,3,2,1,0:T(8,128)(2,1)S(1)} %get-tuple-element.208), channel_id=1, source_target_pairs={{0,4},{1,5},{2,6},{3,7},{4,0},{5,1},{6,2},{7,3},{8,12},{9,13},{10,... | collective-permute-start | bytes 3538952 | tf_op jit(solution)/shard_map/ppermute | solution.py:634
  141.1 9.9 %collective-permute-start.40 = (bf16[4,96,768]{2,1,0:T(8,128)(2,1)S(1)}, bf16[4,96,768]{2,1,0:T(8,128)(2,1)S(1)}, u32[]{:S(2)}, u32[]{:S(2)}) collective-permute-start(bf16[4,96,768]{2,1,0:T(8,128)(2,1)S(1)} %fusion.11), channel_id=1, source_target_pairs={{0,16},{1,17},{2,18},{3,19},{4,12},{5,13},{6,14},{7,15},{8,24},{9,... | collective-permute-start | bytes 1769480 | tf_op jit(solution)/shard_map/ppermute | solution.py:634
  141.4 5.7 %collective-permute-start.41 = (bf16[1,96,768]{2,1,0:T(8,128)(2,1)S(1)}, bf16[1,96,768]{2,1,0:T(8,128)(2,1)S(1)}, u32[]{:S(2)}, u32[]{:S(2)}) collective-permute-start(bf16[1,96,768]{2,1,0:T(8,128)(2,1)S(1)} %slice_bitcast_fusion.21), channel_id=1, source_target_pairs={{0,1},{1,0},{2,3},{3,2},{4,6},{5,7},{6,4},{7,5},{8,9},{9,8},{10,11... | collective-permute-start | bytes 442376 | tf_op jit(solution)/shard_map/ppermute | solution.py:634
  142.2 4.4 %collective-permute-start.42 = (f32[16,768]{1,0:T(8,128)S(1)}, f32[16,768]{1,0:T(8,128)S(1)}, u32[]{:S(2)}, u32[]{:S(2)}) collective-permute-start(f32[16,768]{1,0:T(8,128)S(1)} %get-tuple-element.215), channel_id=1, source_target_pairs={{0,4},{1,5},{2,6},{3,7},{4,0},{5,1},{6,2},{7,3},{8,12},{9,13},{10,... | collective-permute-start | bytes 147464 | tf_op jit(solution)/shard_map/ppermute | solution.py:634
  151.9 16.5 %collective-permute-start.43 = (bf16[784,768]{1,0:T(8,128)(2,1)S(1)}, bf16[784,768]{1,0:T(8,128)(2,1)S(1)}, u32[]{:S(2)}, u32[]{:S(2)}) collective-permute-start(bf16[784,768]{1,0:T(8,128)(2,1)S(1)} %pad_maximum_fusion), channel_id=1, source_target_pairs={{0,8},{1,9},{2,10},{3,11},{4,20},{5,21},{6,22},{7,23},{8,0},{9,1},... | collective-permute-start | bytes 3612680 | tf_op jit(solution)/shard_map/ppermute | solution.py:634
  153.3 10.6 %collective-permute-start.44 = (bf16[1,2,96,768]{3,2,1,0:T(8,128)(2,1)S(1)}, bf16[1,2,96,768]{3,2,1,0:T(8,128)(2,1)S(1)}, u32[]{:S(2)}, u32[]{:S(2)}) collective-permute-start(bf16[1,2,96,768]{3,2,1,0:T(8,128)(2,1)S(1)} %fusion.22), channel_id=1, source_target_pairs={{0,2},{1,3},{2,0},{3,1},{4,5},{5,4},{6,7},{7,6},{8,10},{9,11},{10,... | collective-permute-start | bytes 884744 | tf_op jit(solution)/shard_map/ppermute | solution.py:634
  168.7 10.2 %collective-permute-start.45 = (bf16[400,768]{1,0:T(8,128)(2,1)S(1)}, bf16[400,768]{1,0:T(8,128)(2,1)S(1)}, u32[]{:S(2)}, u32[]{:S(2)}) collective-permute-start(bf16[400,768]{1,0:T(8,128)(2,1)S(1)} %pad_maximum_fusion.4), channel_id=1, source_target_pairs={{0,16},{1,17},{2,18},{3,19},{4,12},{5,13},{6,14},{7,15},{8,24},{9,... | collective-permute-start | bytes 1843208 | tf_op jit(solution)/shard_map/ppermute | solution.py:634
  168.9 6.7 %collective-permute-start.46 = (bf16[1,96,768]{2,1,0:T(8,128)(2,1)S(1)}, bf16[1,96,768]{2,1,0:T(8,128)(2,1)S(1)}, u32[]{:S(2)}, u32[]{:S(2)}) collective-permute-start(bf16[1,96,768]{2,1,0:T(8,128)(2,1)S(1)} %slice_bitcast_fusion.20), channel_id=1, source_target_pairs={{0,1},{1,0},{2,3},{3,2},{4,6},{5,7},{6,4},{7,5},{8,9},{9,8},{10,11... | collective-permute-start | bytes 442376 | tf_op jit(solution)/shard_map/ppermute | solution.py:634
  179.7 16.5 %collective-permute-start.50 = (bf16[2,96,768]{2,1,0:T(8,128)(2,1)S(1)}, bf16[2,96,768]{2,1,0:T(8,128)(2,1)S(1)}, u32[]{:S(2)}, u32[]{:S(2)}) collective-permute-start(bf16[2,96,768]{2,1,0:T(8,128)(2,1)S(1)} %get-tuple-element.277), channel_id=1, source_target_pairs={{0,8},{1,9},{2,10},{3,11},{4,12},{5,13},{6,14},{7,15},{8,0},{9,1},... | collective-permute-start | bytes 884744 | tf_op jit(solution)/shard_map/ppermute | solution.py:634
  180.8 15.4 %collective-permute-start.51 = (bf16[2,96,768]{2,1,0:T(8,128)(2,1)S(1)}, bf16[2,96,768]{2,1,0:T(8,128)(2,1)S(1)}, u32[]{:S(2)}, u32[]{:S(2)}) collective-permute-start(bf16[2,96,768]{2,1,0:T(8,128)(2,1)S(1)} %get-tuple-element.277), channel_id=1, source_target_pairs={{0,16},{1,17},{2,18},{3,19},{4,20},{5,21},{6,22},{7,23},{8,24},{9,... | collective-permute-start | bytes 884744 | tf_op jit(solution)/shard_map/ppermute | solution.py:634
  181.4 9.2 %collective-permute-start.47 = (bf16[112,768]{1,0:T(8,128)(2,1)S(1)}, bf16[112,768]{1,0:T(8,128)(2,1)S(1)}, u32[]{:S(2)}, u32[]{:S(2)}) collective-permute-start(bf16[112,768]{1,0:T(8,128)(2,1)S(1)} %get-tuple-element.283), channel_id=1, source_target_pairs={{0,3},{1,2},{2,1},{3,0},{4,7},{5,6},{6,5},{7,4},{8,11},{9,10},{10,... | collective-permute-start | bytes 516104 | tf_op jit(solution)/shard_map/ppermute | solution.py:634
  183.4 12.8 %collective-permute-start.48 = (bf16[112,768]{1,0:T(8,128)(2,1)S(1)}, bf16[112,768]{1,0:T(8,128)(2,1)S(1)}, u32[]{:S(2)}, u32[]{:S(2)}) collective-permute-start(bf16[112,768]{1,0:T(8,128)(2,1)S(1)} %get-tuple-element.282), channel_id=1, source_target_pairs={{0,2},{1,3},{2,0},{3,1},{4,6},{5,7},{6,4},{7,5},{8,10},{9,11},{10,... | collective-permute-start | bytes 516104 | tf_op jit(solution)/shard_map/ppermute | solution.py:634
  183.4 12.8 %collective-permute-start.49 = (bf16[112,768]{1,0:T(8,128)(2,1)S(1)}, bf16[112,768]{1,0:T(8,128)(2,1)S(1)}, u32[]{:S(2)}, u32[]{:S(2)}) collective-permute-start(bf16[112,768]{1,0:T(8,128)(2,1)S(1)} %get-tuple-element.281), channel_id=1, source_target_pairs={{0,1},{1,0},{2,3},{3,2},{4,5},{5,4},{6,7},{7,6},{8,9},{9,8},{10,11... | collective-permute-start | bytes 516104 | tf_op jit(solution)/shard_map/ppermute | solution.py:634
  197.0 11.1 %collective-permute-start.55 = (bf16[3,2,96,768]{3,2,1,0:T(8,128)(2,1)S(1)}, bf16[3,2,96,768]{3,2,1,0:T(8,128)(2,1)S(1)}, u32[]{:S(2)}, u32[]{:S(2)}) collective-permute-start(bf16[3,2,96,768]{3,2,1,0:T(8,128)(2,1)S(1)} %pad_maximum_fusion.3.held), channel_id=1, source_target_pairs={{0,4},{1,5},{2,6},{3,7},{4,0},{5,1},{6,2},{7,3},{8,12},{9,13},{10,... | collective-permute-start | bytes 2654216 | tf_op jit(solution)/shard_map/ppermute | solution.py:634
  198.2 9.9 %collective-permute-start.60 = (bf16[2,96,768]{2,1,0:T(8,128)(2,1)S(1)}, bf16[2,96,768]{2,1,0:T(8,128)(2,1)S(1)}, u32[]{:S(2)}, u32[]{:S(2)}) collective-permute-start(bf16[2,96,768]{2,1,0:T(8,128)(2,1)S(1)} %broadcast_select_fusion), channel_id=1, source_target_pairs={{0,8},{1,9},{2,10},{3,11},{4,20},{5,21},{6,22},{7,23},{8,0},{9,1},... | collective-permute-start | bytes 884744 | tf_op jit(solution)/shard_map/ppermute | solution.py:634
  199.3 12.3 %collective-permute-start.52 = (bf16[96,768]{1,0:T(8,128)(2,1)S(1)}, bf16[96,768]{1,0:T(8,128)(2,1)S(1)}, u32[]{:S(2)}, u32[]{:S(2)}) collective-permute-start(bf16[96,768]{1,0:T(8,128)(2,1)S(1)} %fusion.29.refs_0_), channel_id=1, source_target_pairs={{0,8},{1,9},{2,10},{3,11},{4,12},{5,13},{6,14},{7,15},{8,0},{9,1},... | collective-permute-start | bytes 442376 | tf_op jit(solution)/shard_map/ppermute | solution.py:634
  200.4 11.2 %collective-permute-start.53 = (bf16[96,768]{1,0:T(8,128)(2,1)S(1)}, bf16[96,768]{1,0:T(8,128)(2,1)S(1)}, u32[]{:S(2)}, u32[]{:S(2)}) collective-permute-start(bf16[96,768]{1,0:T(8,128)(2,1)S(1)} %fusion.29.refs_0_), channel_id=1, source_target_pairs={{0,16},{1,17},{2,18},{3,19},{4,20},{5,21},{6,22},{7,23},{8,24},{9,... | collective-permute-start | bytes 442376 | tf_op jit(solution)/shard_map/ppermute | solution.py:634
  202.2 9.5 %collective-permute-start.54 = (bf16[96,768]{1,0:T(8,128)(2,1)S(1)}, bf16[96,768]{1,0:T(8,128)(2,1)S(1)}, u32[]{:S(2)}, u32[]{:S(2)}) collective-permute-start(bf16[96,768]{1,0:T(8,128)(2,1)S(1)} %fusion.29.refs_0_), channel_id=1, source_target_pairs={{0,24},{1,25},{2,26},{3,27},{4,28},{5,29},{6,30},{7,31},{8,16},{9,... | collective-permute-start | bytes 442376 | tf_op jit(solution)/shard_map/ppermute | solution.py:634
  208.1 7.0 %collective-permute-start.56 = (bf16[96,768]{1,0:T(8,128)(2,1)S(1)}, bf16[96,768]{1,0:T(8,128)(2,1)S(1)}, u32[]{:S(2)}, u32[]{:S(2)}) collective-permute-start(bf16[96,768]{1,0:T(8,128)(2,1)S(1)} %fusion.29.refs_0_), channel_id=1, source_target_pairs={{0,4},{1,5},{2,6},{3,7},{4,0},{5,1},{6,2},{7,3},{8,12},{9,13},{10,... | collective-permute-start | bytes 442376 | tf_op jit(solution)/shard_map/ppermute | solution.py:634
  208.1 4.7 %collective-permute-start.61 = (bf16[2,96,768]{2,1,0:T(8,128)(2,1)S(1)}, bf16[2,96,768]{2,1,0:T(8,128)(2,1)S(1)}, u32[]{:S(2)}, u32[]{:S(2)}) collective-permute-start(bf16[2,96,768]{2,1,0:T(8,128)(2,1)S(1)} %collective-permute-done.60.corner), channel_id=1, source_target_pairs={{0,4},{1,5},{2,6},{3,7},{4,0},{5,1},{6,2},{7,3},{8,12},{9,13},{10,... | collective-permute-start | bytes 884744 | tf_op jit(solution)/shard_map/ppermute | solution.py:634
  211.6 3.5 %collective-permute-start.57 = (bf16[96,768]{1,0:T(8,128)(2,1)S(1)}, bf16[96,768]{1,0:T(8,128)(2,1)S(1)}, u32[]{:S(2)}, u32[]{:S(2)}) collective-permute-start(bf16[96,768]{1,0:T(8,128)(2,1)S(1)} %collective-permute-done.52.refs_1_), channel_id=1, source_target_pairs={{0,4},{1,5},{2,6},{3,7},{4,0},{5,1},{6,2},{7,3},{8,12},{9,13},{10,... | collective-permute-start | bytes 442376 | tf_op jit(solution)/shard_map/ppermute | solution.py:634
  211.7 3.4 %collective-permute-start.58 = (bf16[96,768]{1,0:T(8,128)(2,1)S(1)}, bf16[96,768]{1,0:T(8,128)(2,1)S(1)}, u32[]{:S(2)}, u32[]{:S(2)}) collective-permute-start(bf16[96,768]{1,0:T(8,128)(2,1)S(1)} %collective-permute-done.53.refs_2_), channel_id=1, source_target_pairs={{0,4},{1,5},{2,6},{3,7},{4,0},{5,1},{6,2},{7,3},{8,12},{9,13},{10,... | collective-permute-start | bytes 442376 | tf_op jit(solution)/shard_map/ppermute | solution.py:634
  212.2 2.9 %collective-permute-start.59 = (bf16[96,768]{1,0:T(8,128)(2,1)S(1)}, bf16[96,768]{1,0:T(8,128)(2,1)S(1)}, u32[]{:S(2)}, u32[]{:S(2)}) collective-permute-start(bf16[96,768]{1,0:T(8,128)(2,1)S(1)} %collective-permute-done.54.refs_3_), channel_id=1, source_target_pairs={{0,4},{1,5},{2,6},{3,7},{4,0},{5,1},{6,2},{7,3},{8,12},{9,13},{10,... | collective-permute-start | bytes 442376 | tf_op jit(solution)/shard_map/ppermute | solution.py:634
  (23 other events, 227.9 us)

commit v3 on v2

--- a/solution.py
+++ b/solution.py
@@ -806,27 +806,30 @@
     last_d, kept_d = line_b(kept_d, line_d)
     grad_tokens = grad_tokens_of(grad_residual, joint_a, joint_b, attn_w[:3], attn_rest_w)
     small_got = links.core(small)
-    got_b, far_u, last_d, grad_tokens, small_got = after(got_b, far_u, last_d, grad_tokens, small_got)
+    got_a, got_b, far_u, last_d, grad_tokens, small_got = after(
+        got_a, got_b, far_u, last_d, grad_tokens, small_got
+    )
     small = small + small_got
-    size = parts * 2 * rows
 
     def joined(share, small):
         return jnp.concatenate([share.reshape(-1, width), small.astype(low)], axis=0)
 
-    keep_ab, got_ab = jnp.stack([keep_a, keep_b], axis=2), jnp.stack([got_a, got_b], axis=2)
-    near_a = links.plane(joined(add(keep_ab[1], got_ab[1]), small), 0)
-    kept_a = add(keep_ab[0], got_ab[0])
+    near_a, kept_a = plane_a(keep_a, got_a)
+    near_b = links.plane(joined(add(keep_b[1], got_b[1]), small), 0)
+    kept_b = add(keep_b[0], got_b[0])
     line_u, kept_u = line_a(add(kept_u, far_u))
-    near_a, line_u = after(near_a, line_u)
-    small = small + near_a[size:].astype(wide)
-    near_a = near_a[:size].reshape(kept_a.shape)
-    far_a = links.plane(joined(add(kept_a[1], near_a[1]), small), 1)
-    kept_a = add(kept_a[0], near_a[0])
+    near_a, near_b, line_u = after(near_a, near_b, line_u)
+    size = 4 * rows
+    far_a, kept_a = plane_b(kept_a, near_a)
+    small = small + near_b[size:].astype(wide)
+    near_b = near_b[:size].reshape(kept_b.shape)
+    size = 2 * rows
+    far_b = links.plane(joined(add(kept_b[1], near_b[1]), small), 1)
+    kept_b = add(kept_b[0], near_b[0])
     last_u, kept_u = line_b(kept_u, line_u)
-    far_a, last_u = after(far_a, last_u)
-    size = parts * rows
-    small = small + far_a[size:].astype(wide)
-    share = add(kept_a, far_a[:size].reshape(kept_a.shape)).reshape(parts, rows, width)
+    far_a, far_b = after(far_a, far_b)
+    small = small + far_b[size:].astype(wide)
+    share = jnp.concatenate([add(kept_a, far_a), add(kept_b, far_b[:size].reshape(kept_b.shape))])
     across = [links.across(joined(share[k], small), k) for k in range(parts - 1, 0, -1)]
     sum_f = jnp.stack([settle(kept_d, last_d)[0], settle(kept_u, last_u)[0]])
     f_x, f_y = links.everywhere(sum_f, (2, 4))

time: 222 us -> 220 us (level)
  waiting for transfers between devices: 77.3 us -> 70.4 us
  starting transfers between devices: 48.3 us -> 52.7 us
    ppermute x62 -> x64, waiting for transfers between devices: 77.3 us -> 70.4 us  [move(): return lax.ppermute(array, ('dp', 'tensor'), pairs)]
    ppermute x62 -> x64, starting transfers between devices: 48.3 us -> 52.7 us  [move(): return lax.ppermute(array, ('dp', 'tensor'), pairs)]
  transfers between devices with their start and end apart: 62 -> 64, of which waited for: 25 -> 27; matrix products, arithmetic and copies ran while one was open for 6% -> 7% of each run, Pallas kernels for 28% -> 28%
where the time goes in v3:
time: 220 us; the launch traced here: 215 us
  Pallas kernels  71 us (32%)
  waiting for transfers between devices  70.4 us (32%)
  starting transfers between devices  52.7 us (24%)
  other arithmetic  12 us (5%)
  local copies, waits for them, and re-layouts  7.19 us (3%)
    ppermute x64, waiting for transfers between devices, move(): return lax.ppermute(array, ('dp', 'tensor'), pairs)  70.4 us
    ppermute x64, starting transfers between devices, move(): return lax.ppermute(array, ('dp', 'tensor'), pairs)  52.7 us
    pallas_call x2, Pallas kernels, attn_back(): pl.pallas_call(partial(attn_back_kernel, first), in_specs=[smem()] + [vme...  16.3 us
    pallas_call x1, Pallas kernels, ffn_back(): pl.pallas_call(ffn_back_kernel, in_specs=[smem()] + [vmem()] * 10, out_sp...  10.5 us
    pallas_call x1, Pallas kernels, attn_rest(): pl.pallas_call(attn_rest_kernel, in_specs=[smem()] + [vmem()] * 10, out_s...  9.23 us
    pallas_call x1, Pallas kernels, ffn_up(): pl.pallas_call(ffn_up_kernel, in_specs=[smem()] + [vmem()] * (3 + 8) + [h...  8.68 us
    pallas_call x1, Pallas kernels, ffn_down(): pl.pallas_call(ffn_down_kernel, in_specs=[smem()] + [vmem()] * (5 + 8) +...  6.03 us
    pallas_call x2, Pallas kernels, down_grad(): pl.pallas_call(partial(down_grad_ordered, first), in_specs=[smem()] + [vm...  5.26 us
  transfers between devices with their start and end apart: 64, of which 27 were waited for; matrix products, arithmetic and copies ran while one was open for 7% of the time, Pallas kernels for 28%

profile of v3, /device:TPU:0, one launch (start us, length us, event | category | flops | bytes accessed | tf_op | source)
XLA Modules:
  0.0 215.2 jit_solution(7210638695959004062)
XLA Ops:
  0.8 2.0 fusion.34
  2.8 3.0 %collective-permute-start = (bf16[96,768]{1,0:T(8,128)(2,1)}, bf16[96,768]{1,0:T(8,128)(2,1)S(1)}, u32[]{:S(2)}, u32[]{:S(2)}) collective-permute-start(bf16[96,768]{1,0:T(8,128)(2,1)} %fusion.34), channel_id=1, source_target_pairs={{0,1},{1,0},{2,3},{3,2},{4,6},{5,7},{6,4},{7,5},{8,9},{9,8},{10,11... | collective-permute-start | bytes 442376 | tf_op jit(solution)/shard_map/ppermute | solution.py:634
  5.9 2.6 %collective-permute-start.1 = (bf16[96,768]{1,0:T(8,128)(2,1)}, bf16[96,768]{1,0:T(8,128)(2,1)S(1)}, u32[]{:S(2)}, u32[]{:S(2)}) collective-permute-start(bf16[96,768]{1,0:T(8,128)(2,1)} %fusion.34), channel_id=1, source_target_pairs={{0,2},{1,3},{2,0},{3,1},{4,5},{5,4},{6,7},{7,6},{8,10},{9,11},{10,... | collective-permute-start | bytes 442376 | tf_op jit(solution)/shard_map/ppermute | solution.py:634
  9.9 1.2 dynamic_slice.28
  14.5 2.4 %collective-permute-start.3 = (bf16[104,768]{1,0:T(8,128)(2,1)}, bf16[104,768]{1,0:T(8,128)(2,1)S(1)}, u32[]{:S(2)}, u32[]{:S(2)}) collective-permute-start(bf16[104,768]{1,0:T(8,128)(2,1)} %pad_maximum_fusion.11), channel_id=1, source_target_pairs={{0,1},{1,0},{2,3},{3,2},{4,6},{5,7},{6,4},{7,5},{8,9},{9,8},{10,11... | collective-permute-start | bytes 479240 | tf_op jit(solution)/shard_map/ppermute | solution.py:634
  16.9 3.0 %attn_own.1 = (bf16[1,576,512]{2,1,0:T(8,128)(2,1)S(1)}, bf16[1,192,512]{2,1,0:T(8,128)(2,1)S(1)}, f32[1,8,512]{2,1,0:T(8,128)S(1)}) custom-call(s32[4]{0:T(128)S(1)} %pad_add_fusion.info, bf16[512,768]{1,0:T(8,128)(2,1)S(1)} %copy-done.7, bf16[192,768]{1,0:T(8,128)(2,1)S(1)} %bitcast.185, bf16[192,768]{1,0:T(8,128)(2,1)S(1)} %bitcast.187, ...), custom_call_target="tpu_custom_call" | custom-call | flops 4400000000 | bytes 1048576 | tf_op jit(solution)/shard_map/attn_own/pallas_call | solution.py:161
  20.8 3.2 %collective-permute-done.2 = bf16[96,768]{1,0:T(8,128)(2,1)S(1)} collective-permute-done((bf16[96,768]{1,0:T(8,128)(2,1)S(1)}, bf16[96,768]{1,0:T(8,128)(2,1)S(1)}, u32[]{:S(2)}, u32[]{:S(2)}) %collective-permute-start.2) | collective-permute-done | bytes 147488 | tf_op jit(solution)/shard_map/ppermute | solution.py:634
  24.0 1.9 collective-permute-start.6
  25.9 1.3 collective-permute-start.7
  27.2 1.6 collective-permute-start.8
  28.8 1.3 collective-permute-start.11
  30.2 1.5 collective-permute-start.5
  31.7 1.7 collective-permute-done.7
  33.3 3.4 %collective-permute-done.8 = bf16[104,768]{1,0:T(8,128)(2,1)} collective-permute-done((bf16[104,768]{1,0:T(8,128)(2,1)S(1)}, bf16[104,768]{1,0:T(8,128)(2,1)}, u32[]{:S(2)}, u32[]{:S(2)}) %collective-permute-start.8) | collective-permute-done | bytes 159776 | tf_op jit(solution)/shard_map/ppermute | solution.py:634
  36.8 1.1 pad_maximum_fusion.3
  38.6 3.9 %collective-permute-start.9 = (bf16[3,96,768]{2,1,0:T(8,128)(2,1)S(1)}, bf16[3,96,768]{2,1,0:T(8,128)(2,1)S(1)}, u32[]{:S(2)}, u32[]{:S(2)}) collective-permute-start(bf16[3,96,768]{2,1,0:T(8,128)(2,1)S(1)} %collective-permute-done.6.refs_1_), channel_id=1, source_target_pairs={{0,16},{1,17},{2,18},{3,19},{4,12},{5,13},{6,14},{7,15},{8,24},{9,... | collective-permute-start | bytes 1327112 | tf_op jit(solution)/shard_map/ppermute | solution.py:634
  43.4 6.9 %collective-permute-done.12 = bf16[96,768]{1,0:T(8,128)(2,1)S(1)} collective-permute-done((bf16[96,768]{1,0:T(8,128)(2,1)S(1)}, bf16[96,768]{1,0:T(8,128)(2,1)S(1)}, u32[]{:S(2)}, u32[]{:S(2)}) %collective-permute-start.12) | collective-permute-done | bytes 147488 | tf_op jit(solution)/shard_map/ppermute | solution.py:634
  51.4 1.0 pad_maximum_fusion.5.refs_0_
  53.3 1.3 collective-permute-start.18
  54.6 1.1 collective-permute-start.19
  55.7 9.2 %attn_rest.1 = (bf16[3,576,512]{2,1,0:T(8,128)(2,1)S(1)}, bf16[3,768,768]{2,1,0:T(8,128)(2,1)S(1)}, bf16[3,192,512]{2,1,0:T(8,128)(2,1)S(1)}, f32[3,8,512]{2,1,0:T(8,128)S(1)}, bf16[3,192,768]{2,1,0:T(8,128)(2,1)S(1)}) custom-call(s32[4]{0:T(128)S(1)} %pad_add_fusion.info, bf16[512,768]{1,0:T(8,128)(2,1)S(1)} %copy-done.7, ...), custom_call_target="tpu_custom_call" | custom-call | flops 8800000000 | bytes 1048576 | tf_op jit(solution)/shard_map/attn_rest/pallas_call | solution.py:203
  64.9 1.6 ffn_in.1
  66.6 2.6 %collective-permute-done.18.refs_3_ = bf16[3,96,768]{2,1,0:T(8,128)(2,1)S(1)} collective-permute-done((bf16[3,96,768]{2,1,0:T(8,128)(2,1)S(1)}, bf16[3,96,768]{2,1,0:T(8,128)(2,1)S(1)}, u32[]{:S(2)}, u32[]{:S(2)}) %collective-permute-start.18) | collective-permute-done | bytes 442400 | tf_op jit(solution)/shard_map/ppermute | solution.py:634
  70.5 1.3 collective-permute-start.25
  71.8 8.7 %ffn_up.1 = (bf16[4,512,768]{2,1,0:T(8,128)(2,1)S(1)}, bf16[4,512,768]{2,1,0:T(8,128)(2,1)S(1)}, bf16[4,768,768]{2,1,0:T(8,128)(2,1)S(1)}, f32[8,128]{1,0:T(8,128)S(1)}) custom-call(s32[4]{0:T(128)S(1)} %pad_add_fusion.info, bf16[512,768]{1,0:T(8,128)(2,1)S(1)} %get-tuple-element.157.normed.normed_low, f32[4,1,1152]{2,1,0:T(1,128)S(1)} %maximum_convert_fusion.bias, ...), custom_call_target="tpu_custom_call" | custom-call | flops 12099999744 | bytes 1048576 | tf_op jit(solution)/shard_map/ffn_up/pallas_call | solution.py:279
  80.5 2.2 %collective-permute-done.25.refs_3_ = bf16[3,96,768]{2,1,0:T(8,128)(2,1)S(1)} collective-permute-done((bf16[3,96,768]{2,1,0:T(8,128)(2,1)S(1)}, bf16[3,96,768]{2,1,0:T(8,128)(2,1)S(1)}, u32[]{:S(2)}, u32[]{:S(2)}) %collective-permute-start.25) | collective-permute-done | bytes 442400 | tf_op jit(solution)/shard_map/ppermute | solution.py:634
  83.2 1.3 collective-permute-done.28.refs_6_
  85.2 6.0 %ffn_down.1 = (bf16[512,768]{1,0:T(8,128)(2,1)}, f32[512,768]{1,0:T(8,128)S(1)}, bf16[512,768]{1,0:T(8,128)(2,1)S(1)}, f32[16,768]{1,0:T(8,128)S(1)}, bf16[4,768,768]{2,1,0:T(8,128)(2,1)S(1)}) custom-call(s32[4]{0:T(128)S(1)} %pad_add_fusion.info, f32[512,768]{1,0:T(8,128)S(1)} %get-tuple-element.156.skip, f32[8,768]{1,0:T(8,128)S(1)} %convert_element_type.485.vec, ...), custom_call_target="tpu_custom_call" | custom-call | flops 13200000000 | bytes 1048576 | tf_op jit(solution)/shard_map/ffn_down/pallas_call | solution.py:358
  91.2 2.3 %down_grad.2 = (bf16[2,2,2,96,768]{4,3,2,1,0:T(8,128)(2,1)S(1)}, bf16[2,2,2,96,768]{4,3,2,1,0:T(8,128)(2,1)S(1)}, f32[8,128]{1,0:T(8,128)S(1)}) custom-call(s32[4]{0:T(128)S(1)} %pad_add_fusion.info, bf16[4,512,768]{2,1,0:T(8,128)(2,1)S(1)} %get-tuple-element.166.act, bf16[512,768]{1,0:T(8,128)(2,1)S(1)} %get-tuple-element.173.branch_low, ...), custom_call_target="tpu_custom_call" | custom-call | flops 2200000000 | bytes 1048576 | tf_op jit(solution)/shard_map/down_grad/pallas_call | solution.py:335
  93.7 2.9 %down_grad.3 = (bf16[2,2,2,96,768]{4,3,2,1,0:T(8,128)(2,1)S(1)}, bf16[2,2,2,96,768]{4,3,2,1,0:T(8,128)(2,1)S(1)}, f32[8,128]{1,0:T(8,128)}) custom-call(s32[4]{0:T(128)S(1)} %pad_add_fusion.info, bf16[4,512,768]{2,1,0:T(8,128)(2,1)S(1)} %get-tuple-element.166.act, bf16[512,768]{1,0:T(8,128)(2,1)S(1)} %get-tuple-element.173.branch_low, ...), custom_call_target="tpu_custom_call" | custom-call | flops 2200000000 | bytes 1048576 | tf_op jit(solution)/shard_map/down_grad/pallas_call | solution.py:335
  97.3 1.1 collective-permute-start.32
  98.4 1.1 collective-permute-done.31
  99.8 1.1 collective-permute-start.33
  100.9 10.5 %ffn_back.1 = (f32[512,768]{1,0:T(8,128)S(1)}, bf16[512,768]{1,0:T(8,128)(2,1)S(1)}, f32[16,768]{1,0:T(8,128)S(1)}, bf16[2,2,4,96,768]{4,3,2,1,0:T(8,128)(2,1)S(1)}, bf16[2,2,4,96,768]{4,3,2,1,0:T(8,128)(2,1)S(1)}) custom-call(s32[4]{0:T(128)S(1)} %pad_add_fusion.info, bf16[512,768]{1,0:T(8,128)(2,1)S(1)} %get-tuple-element.173.branch_low, ...), custom_call_target="tpu_custom_call" | custom-call | flops 12099999744 | bytes 1048576 | tf_op jit(solution)/shard_map/ffn_back/pallas_call | solution.py:410
  111.4 2.2 %collective-permute-done.33 = bf16[2,2,96,768]{3,2,1,0:T(8,128)(2,1)S(1)} collective-permute-done((bf16[2,2,96,768]{3,2,1,0:T(8,128)(2,1)S(1)}, bf16[2,2,96,768]{3,2,1,0:T(8,128)(2,1)S(1)}, u32[]{:S(2)}, u32[]{:S(2)}) %collective-permute-start.33) | collective-permute-done | bytes 589856 | tf_op jit(solution)/shard_map/ppermute | solution.py:634
  114.1 7.9 %attn_back.2 = (f32[16,768]{1,0:T(8,128)S(1)}, bf16[2,576,512]{2,1,0:T(8,128)(2,1)S(1)}, bf16[2,2,2,96,768]{4,3,2,1,0:T(8,128)(2,1)S(1)}, bf16[2,2,2,96,768]{4,3,2,1,0:T(8,128)(2,1)S(1)}) custom-call(s32[4]{0:T(128)S(1)} %pad_add_fusion.info, bf16[512,768]{1,0:T(8,128)(2,1)S(1)} %copy-done.7, bf16[512,768]{1,0:T(8,128)(2,1)S(1)} %get-tuple-element.195.residual_low, ...), custom_call_target="tpu_custom_call" | custom-call | flops 9900000256 | bytes 1048576 | tf_op jit(solution)/shard_map/attn_back/pallas_call | solution.py:494
  122.0 1.9 collective-permute-done.35
  124.7 1.1 collective-permute-start.36
  126.6 8.4 %attn_back.3 = (f32[16,768]{1,0:T(8,128)S(1)}, bf16[2,576,512]{2,1,0:T(8,128)(2,1)S(1)}, bf16[2,2,2,96,768]{4,3,2,1,0:T(8,128)(2,1)S(1)}, bf16[2,2,2,96,768]{4,3,2,1,0:T(8,128)(2,1)S(1)}) custom-call(s32[4]{0:T(128)S(1)} %pad_add_fusion.info, bf16[512,768]{1,0:T(8,128)(2,1)S(1)} %copy-done.7, bf16[512,768]{1,0:T(8,128)(2,1)S(1)} %get-tuple-element.195.residual_low, ...), custom_call_target="tpu_custom_call" | custom-call | flops 9900000256 | bytes 1048576 | tf_op jit(solution)/shard_map/attn_back/pallas_call | solution.py:494
  135.0 1.5 collective-permute-done.38
  136.5 4.5 %collective-permute-done.36 = bf16[2,4,96,768]{3,2,1,0:T(8,128)(2,1)S(1)} collective-permute-done((bf16[2,4,96,768]{3,2,1,0:T(8,128)(2,1)S(1)}, bf16[2,4,96,768]{3,2,1,0:T(8,128)(2,1)S(1)}, u32[]{:S(2)}, u32[]{:S(2)}) %collective-permute-start.36) | collective-permute-done | bytes 1179680 | tf_op jit(solution)/shard_map/ppermute | solution.py:634
  142.9 3.6 %grad_tokens.1 = bf16[512,768]{1,0:T(8,128)(2,1)} custom-call(f32[512,768]{1,0:T(8,128)S(1)} %get-tuple-element.214.grad, bf16[2,576,512]{2,1,0:T(8,128)(2,1)S(1)} %get-tuple-element.215.joint_a, bf16[2,576,512]{2,1,0:T(8,128)(2,1)S(1)} %get-tuple-element.216.joint_b, bf16[192,768]{1,0:T(8,128)(2,1)S(1)} %bitcast.186, bf16[192,768]{1,0:T(8,128)(2,1)S(1)} %bitcast.188, ...), custom_call_target="tpu_custom_call" | custom-call | flops 4400000000 | bytes 1048576 | tf_op jit(solution)/shard_map/grad_tokens/pallas_call | solution.py:523
  147.0 4.0 %collective-permute-done.40 = bf16[4,96,768]{2,1,0:T(8,128)(2,1)S(1)} collective-permute-done((bf16[4,96,768]{2,1,0:T(8,128)(2,1)S(1)}, bf16[4,96,768]{2,1,0:T(8,128)(2,1)S(1)}, u32[]{:S(2)}, u32[]{:S(2)}) %collective-permute-start.40) | collective-permute-done | bytes 589856 | tf_op jit(solution)/shard_map/ppermute | solution.py:634
  151.4 1.1 collective-permute-start.43
  152.8 1.0 collective-permute-start.44
  154.1 1.4 collective-permute-start.45
  155.6 9.3 %collective-permute-done.45 = bf16[1,2,96,768]{3,2,1,0:T(8,128)(2,1)S(1)} collective-permute-done((bf16[1,2,96,768]{3,2,1,0:T(8,128)(2,1)S(1)}, bf16[1,2,96,768]{3,2,1,0:T(8,128)(2,1)S(1)}, u32[]{:S(2)}, u32[]{:S(2)}) %collective-permute-start.45) | collective-permute-done | bytes 294944 | tf_op jit(solution)/shard_map/ppermute | solution.py:634
  164.9 3.0 %collective-permute-done.44 = bf16[400,768]{1,0:T(8,128)(2,1)S(1)} collective-permute-done((bf16[400,768]{1,0:T(8,128)(2,1)S(1)}, bf16[400,768]{1,0:T(8,128)(2,1)S(1)}, u32[]{:S(2)}, u32[]{:S(2)}) %collective-permute-start.44) | collective-permute-done | bytes 614432 | tf_op jit(solution)/shard_map/ppermute | solution.py:634
  169.2 1.3 collective-permute-start.47
  170.5 4.6 %collective-permute-done.51 = bf16[1,96,768]{2,1,0:T(8,128)(2,1)S(1)} collective-permute-done((bf16[1,96,768]{2,1,0:T(8,128)(2,1)S(1)}, bf16[1,96,768]{2,1,0:T(8,128)(2,1)S(1)}, u32[]{:S(2)}, u32[]{:S(2)}) %collective-permute-start.51) | collective-permute-done | bytes 147488 | tf_op jit(solution)/shard_map/ppermute | solution.py:634
  175.2 1.3 collective-permute-start.52
  176.5 1.1 collective-permute-start.53
  179.8 3.1 %collective-permute-start.48 = (bf16[112,768]{1,0:T(8,128)(2,1)S(1)}, bf16[112,768]{1,0:T(8,128)(2,1)S(1)}, u32[]{:S(2)}, u32[]{:S(2)}) collective-permute-start(bf16[112,768]{1,0:T(8,128)(2,1)S(1)} %get-tuple-element.286), channel_id=1, source_target_pairs={{0,3},{1,2},{2,1},{3,0},{4,7},{5,6},{6,5},{7,4},{8,11},{9,10},{10,... | collective-permute-start | bytes 516104 | tf_op jit(solution)/shard_map/ppermute | solution.py:634
  182.8 1.4 collective-permute-start.50
  184.5 4.4 %collective-permute-done.48 = bf16[112,768]{1,0:T(8,128)(2,1)S(1)} collective-permute-done((bf16[112,768]{1,0:T(8,128)(2,1)S(1)}, bf16[112,768]{1,0:T(8,128)(2,1)S(1)}, u32[]{:S(2)}, u32[]{:S(2)}) %collective-permute-start.48) | collective-permute-done | bytes 172064 | tf_op jit(solution)/shard_map/ppermute | solution.py:634
  188.9 5.9 %collective-permute-done.49 = bf16[112,768]{1,0:T(8,128)(2,1)S(1)} collective-permute-done((bf16[112,768]{1,0:T(8,128)(2,1)S(1)}, bf16[112,768]{1,0:T(8,128)(2,1)S(1)}, u32[]{:S(2)}, u32[]{:S(2)}) %collective-permute-start.49) | collective-permute-done | bytes 172064 | tf_op jit(solution)/shard_map/ppermute | solution.py:634
  195.8 1.4 collective-permute-start.62
  197.2 1.1 fusion.33.refs_0_
  200.0 1.9 collective-permute-start.56
  203.3 1.1 collective-permute-done.62.corner
  204.9 3.0 %finish_ffn.1 = (f32[768,768]{1,0:T(8,128)}, f32[768,768]{1,0:T(8,128)}, f32[8,128]{1,0:T(8,128)S(1)}) custom-call(s32[4]{0:T(128)S(1)} %pad_add_fusion.info, bf16[3,2,96,768]{3,2,1,0:T(8,128)(2,1)S(1)} %pad_maximum_fusion.held, bf16[3,2,96,768]{3,2,1,0:T(8,128)(2,1)S(1)} %collective-permute-done.57.held_mates), custom_call_target="tpu_custom_call" | custom-call | flops 3300000000 | bytes 1048576 | tf_op jit(solution)/shard_map/finish_ffn/pallas_call | solution.py:550
  207.9 1.4 collective-permute-done.56.refs_3_
  210.4 1.6 finish_ffn_corner.1
  212.7 2.1 finish_attn.1
  (207 shorter events, 28.4 us)
Async XLA Ops:
  2.8 11.7 %collective-permute-start = (bf16[96,768]{1,0:T(8,128)(2,1)}, bf16[96,768]{1,0:T(8,128)(2,1)S(1)}, u32[]{:S(2)}, u32[]{:S(2)}) collective-permute-start(bf16[96,768]{1,0:T(8,128)(2,1)} %fusion.34), channel_id=1, source_target_pairs={{0,1},{1,0},{2,3},{3,2},{4,6},{5,7},{6,4},{7,5},{8,9},{9,8},{10,11... | collective-permute-start | bytes 442376 | tf_op jit(solution)/shard_map/ppermute | solution.py:634
  5.9 14.0 %collective-permute-start.1 = (bf16[96,768]{1,0:T(8,128)(2,1)}, bf16[96,768]{1,0:T(8,128)(2,1)S(1)}, u32[]{:S(2)}, u32[]{:S(2)}) collective-permute-start(bf16[96,768]{1,0:T(8,128)(2,1)} %fusion.34), channel_id=1, source_target_pairs={{0,2},{1,3},{2,0},{3,1},{4,5},{5,4},{6,7},{7,6},{8,10},{9,11},{10,... | collective-permute-start | bytes 442376 | tf_op jit(solution)/shard_map/ppermute | solution.py:634
  9.4 11.4 %collective-permute-start.4 = (bf16[96,768]{1,0:T(8,128)(2,1)S(1)}, bf16[96,768]{1,0:T(8,128)(2,1)S(1)}, u32[]{:S(2)}, u32[]{:S(2)}) collective-permute-start(bf16[96,768]{1,0:T(8,128)(2,1)S(1)} %constant_dynamic-slice_fusion), channel_id=1, source_target_pairs={{0,1},{1,0},{2,3},{3,2},{4,6},{5,7},{6,4},{7,5},{8,9},{9,8},{10,11... | collective-permute-start | bytes 442376 | tf_op jit(solution)/shard_map/ppermute | solution.py:634
  14.5 9.5 %collective-permute-start.2 = (bf16[96,768]{1,0:T(8,128)(2,1)S(1)}, bf16[96,768]{1,0:T(8,128)(2,1)S(1)}, u32[]{:S(2)}, u32[]{:S(2)}) collective-permute-start(bf16[96,768]{1,0:T(8,128)(2,1)S(1)} %collective-permute-done), channel_id=1, source_target_pairs={{0,2},{1,3},{2,0},{3,1},{4,5},{5,4},{6,7},{7,6},{8,10},{9,11},{10,... | collective-permute-start | bytes 442376 | tf_op jit(solution)/shard_map/ppermute | solution.py:634
  14.5 9.5 %collective-permute-start.3 = (bf16[104,768]{1,0:T(8,128)(2,1)}, bf16[104,768]{1,0:T(8,128)(2,1)S(1)}, u32[]{:S(2)}, u32[]{:S(2)}) collective-permute-start(bf16[104,768]{1,0:T(8,128)(2,1)} %pad_maximum_fusion.11), channel_id=1, source_target_pairs={{0,1},{1,0},{2,3},{3,2},{4,6},{5,7},{6,4},{7,5},{8,9},{9,8},{10,11... | collective-permute-start | bytes 479240 | tf_op jit(solution)/shard_map/ppermute | solution.py:634
  24.0 12.7 %collective-permute-start.6 = (bf16[3,96,768]{2,1,0:T(8,128)(2,1)S(1)}, bf16[3,96,768]{2,1,0:T(8,128)(2,1)S(1)}, u32[]{:S(2)}, u32[]{:S(2)}) collective-permute-start(bf16[3,96,768]{2,1,0:T(8,128)(2,1)S(1)} %pad_maximum_fusion.4.refs_0_), channel_id=1, source_target_pairs={{0,8},{1,9},{2,10},{3,11},{4,20},{5,21},{6,22},{7,23},{8,0},{9,1},... | collective-permute-start | bytes 1327112 | tf_op jit(solution)/shard_map/ppermute | solution.py:634
  25.9 7.4 %collective-permute-start.7 = (bf16[104,768]{1,0:T(8,128)(2,1)}, bf16[104,768]{1,0:T(8,128)(2,1)}, u32[]{:S(2)}, u32[]{:S(2)}) collective-permute-start(bf16[104,768]{1,0:T(8,128)(2,1)} %pad_maximum_fusion.11), channel_id=1, source_target_pairs={{0,2},{1,3},{2,0},{3,1},{4,5},{5,4},{6,7},{7,6},{8,10},{9,11},{10,... | collective-permute-start | bytes 479240 | tf_op jit(solution)/shard_map/ppermute | solution.py:634
  27.2 9.5 %collective-permute-start.8 = (bf16[104,768]{1,0:T(8,128)(2,1)S(1)}, bf16[104,768]{1,0:T(8,128)(2,1)}, u32[]{:S(2)}, u32[]{:S(2)}) collective-permute-start(bf16[104,768]{1,0:T(8,128)(2,1)S(1)} %collective-permute-done.3), channel_id=1, source_target_pairs={{0,2},{1,3},{2,0},{3,1},{4,5},{5,4},{6,7},{7,6},{8,10},{9,11},{10,... | collective-permute-start | bytes 479240 | tf_op jit(solution)/shard_map/ppermute | solution.py:634
  28.8 13.9 %collective-permute-start.11 = (bf16[96,768]{1,0:T(8,128)(2,1)}, bf16[96,768]{1,0:T(8,128)(2,1)}, u32[]{:S(2)}, u32[]{:S(2)}) collective-permute-start(bf16[96,768]{1,0:T(8,128)(2,1)} %copy-done.18), channel_id=1, source_target_pairs={{0,2},{1,3},{2,0},{3,1},{4,5},{5,4},{6,7},{7,6},{8,10},{9,11},{10,... | collective-permute-start | bytes 442376 | tf_op jit(solution)/shard_map/ppermute | solution.py:634
  30.2 12.7 %collective-permute-start.5 = (bf16[3,96,768]{2,1,0:T(8,128)(2,1)S(1)}, bf16[3,96,768]{2,1,0:T(8,128)(2,1)S(1)}, u32[]{:S(2)}, u32[]{:S(2)}) collective-permute-start(bf16[3,96,768]{2,1,0:T(8,128)(2,1)S(1)} %pad_maximum_fusion.4.refs_0_), channel_id=1, source_target_pairs={{0,16},{1,17},{2,18},{3,19},{4,12},{5,13},{6,14},{7,15},{8,24},{9,... | collective-permute-start | bytes 1327112 | tf_op jit(solution)/shard_map/ppermute | solution.py:634
  38.6 11.7 %collective-permute-start.9 = (bf16[3,96,768]{2,1,0:T(8,128)(2,1)S(1)}, bf16[3,96,768]{2,1,0:T(8,128)(2,1)S(1)}, u32[]{:S(2)}, u32[]{:S(2)}) collective-permute-start(bf16[3,96,768]{2,1,0:T(8,128)(2,1)S(1)} %collective-permute-done.6.refs_1_), channel_id=1, source_target_pairs={{0,16},{1,17},{2,18},{3,19},{4,12},{5,13},{6,14},{7,15},{8,24},{9,... | collective-permute-start | bytes 1327112 | tf_op jit(solution)/shard_map/ppermute | solution.py:634
  42.5 8.4 %collective-permute-start.10 = (bf16[3,96,768]{2,1,0:T(8,128)(2,1)S(1)}, bf16[3,96,768]{2,1,0:T(8,128)(2,1)S(1)}, u32[]{:S(2)}, u32[]{:S(2)}) collective-permute-start(bf16[3,96,768]{2,1,0:T(8,128)(2,1)S(1)} %slice.331.refs_0_), channel_id=1, source_target_pairs={{0,8},{1,9},{2,10},{3,11},{4,20},{5,21},{6,22},{7,23},{8,0},{9,1},... | collective-permute-start | bytes 1327112 | tf_op jit(solution)/shard_map/ppermute | solution.py:634
  42.6 7.7 %collective-permute-start.12 = (bf16[96,768]{1,0:T(8,128)(2,1)S(1)}, bf16[96,768]{1,0:T(8,128)(2,1)S(1)}, u32[]{:S(2)}, u32[]{:S(2)}) collective-permute-start(bf16[96,768]{1,0:T(8,128)(2,1)S(1)} %copy-done.17), channel_id=1, source_target_pairs={{0,2},{1,3},{2,0},{3,1},{4,5},{5,4},{6,7},{7,6},{8,10},{9,11},{10,... | collective-permute-start | bytes 442376 | tf_op jit(solution)/shard_map/ppermute | solution.py:634
  42.8 9.6 %collective-permute-start.13 = (bf16[3,96,768]{2,1,0:T(8,128)(2,1)S(1)}, bf16[3,96,768]{2,1,0:T(8,128)(2,1)S(1)}, u32[]{:S(2)}, u32[]{:S(2)}) collective-permute-start(bf16[3,96,768]{2,1,0:T(8,128)(2,1)S(1)} %pad_maximum_fusion.4.refs_0_), channel_id=1, source_target_pairs={{0,4},{1,5},{2,6},{3,7},{4,0},{5,1},{6,2},{7,3},{8,12},{9,13},{10,... | collective-permute-start | bytes 1327112 | tf_op jit(solution)/shard_map/ppermute | solution.py:634
  42.9 10.4 %collective-permute-start.14 = (bf16[3,96,768]{2,1,0:T(8,128)(2,1)S(1)}, bf16[3,96,768]{2,1,0:T(8,128)(2,1)S(1)}, u32[]{:S(2)}, u32[]{:S(2)}) collective-permute-start(bf16[3,96,768]{2,1,0:T(8,128)(2,1)S(1)} %collective-permute-done.6.refs_1_), channel_id=1, source_target_pairs={{0,4},{1,5},{2,6},{3,7},{4,0},{5,1},{6,2},{7,3},{8,12},{9,13},{10,... | collective-permute-start | bytes 1327112 | tf_op jit(solution)/shard_map/ppermute | solution.py:634
  50.9 3.7 %collective-permute-start.15 = (bf16[3,96,768]{2,1,0:T(8,128)(2,1)S(1)}, bf16[3,96,768]{2,1,0:T(8,128)(2,1)S(1)}, u32[]{:S(2)}, u32[]{:S(2)}) collective-permute-start(bf16[3,96,768]{2,1,0:T(8,128)(2,1)S(1)} %collective-permute-done.5.refs_2_), channel_id=1, source_target_pairs={{0,4},{1,5},{2,6},{3,7},{4,0},{5,1},{6,2},{7,3},{8,12},{9,13},{10,... | collective-permute-start | bytes 1327112 | tf_op jit(solution)/shard_map/ppermute | solution.py:634
  50.9 3.7 %collective-permute-start.16 = (bf16[3,96,768]{2,1,0:T(8,128)(2,1)S(1)}, bf16[3,96,768]{2,1,0:T(8,128)(2,1)S(1)}, u32[]{:S(2)}, u32[]{:S(2)}) collective-permute-start(bf16[3,96,768]{2,1,0:T(8,128)(2,1)S(1)} %collective-permute-done.9.refs_3_), channel_id=1, source_target_pairs={{0,4},{1,5},{2,6},{3,7},{4,0},{5,1},{6,2},{7,3},{8,12},{9,13},{10,... | collective-permute-start | bytes 1327112 | tf_op jit(solution)/shard_map/ppermute | solution.py:634
  51.4 15.2 %collective-permute-start.17 = (bf16[3,96,768]{2,1,0:T(8,128)(2,1)S(1)}, bf16[3,96,768]{2,1,0:T(8,128)(2,1)S(1)}, u32[]{:S(2)}, u32[]{:S(2)}) collective-permute-start(bf16[3,96,768]{2,1,0:T(8,128)(2,1)S(1)} %slice.331.refs_0_), channel_id=1, source_target_pairs={{0,16},{1,17},{2,18},{3,19},{4,12},{5,13},{6,14},{7,15},{8,24},{9,... | collective-permute-start | bytes 1327112 | tf_op jit(solution)/shard_map/ppermute | solution.py:634
  52.4 17.3 %collective-permute-start.20 = (bf16[3,96,768]{2,1,0:T(8,128)(2,1)S(1)}, bf16[3,96,768]{2,1,0:T(8,128)(2,1)S(1)}, u32[]{:S(2)}, u32[]{:S(2)}) collective-permute-start(bf16[3,96,768]{2,1,0:T(8,128)(2,1)S(1)} %slice.331.refs_0_), channel_id=1, source_target_pairs={{0,4},{1,5},{2,6},{3,7},{4,0},{5,1},{6,2},{7,3},{8,12},{9,13},{10,... | collective-permute-start | bytes 1327112 | tf_op jit(solution)/shard_map/ppermute | solution.py:634
  53.3 15.9 %collective-permute-start.18 = (bf16[3,96,768]{2,1,0:T(8,128)(2,1)S(1)}, bf16[3,96,768]{2,1,0:T(8,128)(2,1)S(1)}, u32[]{:S(2)}, u32[]{:S(2)}) collective-permute-start(bf16[3,96,768]{2,1,0:T(8,128)(2,1)S(1)} %collective-permute-done.10.refs_1_), channel_id=1, source_target_pairs={{0,16},{1,17},{2,18},{3,19},{4,12},{5,13},{6,14},{7,15},{8,24},{9,... | collective-permute-start | bytes 1327112 | tf_op jit(solution)/shard_map/ppermute | solution.py:634
  54.5 15.9 %collective-permute-start.21 = (bf16[3,96,768]{2,1,0:T(8,128)(2,1)S(1)}, bf16[3,96,768]{2,1,0:T(8,128)(2,1)S(1)}, u32[]{:S(2)}, u32[]{:S(2)}) collective-permute-start(bf16[3,96,768]{2,1,0:T(8,128)(2,1)S(1)} %collective-permute-done.10.refs_1_), channel_id=1, source_target_pairs={{0,4},{1,5},{2,6},{3,7},{4,0},{5,1},{6,2},{7,3},{8,12},{9,13},{10,... | collective-permute-start | bytes 1327112 | tf_op jit(solution)/shard_map/ppermute | solution.py:634
  54.6 14.6 %collective-permute-start.19 = (bf16[3,96,768]{2,1,0:T(8,128)(2,1)S(1)}, bf16[3,96,768]{2,1,0:T(8,128)(2,1)S(1)}, u32[]{:S(2)}, u32[]{:S(2)}) collective-permute-start(bf16[3,96,768]{2,1,0:T(8,128)(2,1)S(1)} %pad_maximum_fusion.5.refs_0_), channel_id=1, source_target_pairs={{0,8},{1,9},{2,10},{3,11},{4,20},{5,21},{6,22},{7,23},{8,0},{9,1},... | collective-permute-start | bytes 1327112 | tf_op jit(solution)/shard_map/ppermute | solution.py:634
  69.2 2.6 %collective-permute-start.22 = (bf16[3,96,768]{2,1,0:T(8,128)(2,1)S(1)}, bf16[3,96,768]{2,1,0:T(8,128)(2,1)S(1)}, u32[]{:S(2)}, u32[]{:S(2)}) collective-permute-start(bf16[3,96,768]{2,1,0:T(8,128)(2,1)S(1)} %collective-permute-done.17.refs_2_), channel_id=1, source_target_pairs={{0,4},{1,5},{2,6},{3,7},{4,0},{5,1},{6,2},{7,3},{8,12},{9,13},{10,... | collective-permute-start | bytes 1327112 | tf_op jit(solution)/shard_map/ppermute | solution.py:634
  69.2 2.6 %collective-permute-start.23 = (bf16[3,96,768]{2,1,0:T(8,128)(2,1)S(1)}, bf16[3,96,768]{2,1,0:T(8,128)(2,1)S(1)}, u32[]{:S(2)}, u32[]{:S(2)}) collective-permute-start(bf16[3,96,768]{2,1,0:T(8,128)(2,1)S(1)} %collective-permute-done.18.refs_3_), channel_id=1, source_target_pairs={{0,4},{1,5},{2,6},{3,7},{4,0},{5,1},{6,2},{7,3},{8,12},{9,13},{10,... | collective-permute-start | bytes 1327112 | tf_op jit(solution)/shard_map/ppermute | solution.py:634
  69.7 10.8 %collective-permute-start.24 = (bf16[3,96,768]{2,1,0:T(8,128)(2,1)S(1)}, bf16[3,96,768]{2,1,0:T(8,128)(2,1)S(1)}, u32[]{:S(2)}, u32[]{:S(2)}) collective-permute-start(bf16[3,96,768]{2,1,0:T(8,128)(2,1)S(1)} %pad_maximum_fusion.5.refs_0_), channel_id=1, source_target_pairs={{0,16},{1,17},{2,18},{3,19},{4,12},{5,13},{6,14},{7,15},{8,24},{9,... | collective-permute-start | bytes 1327112 | tf_op jit(solution)/shard_map/ppermute | solution.py:634
  69.7 13.6 %collective-permute-start.26 = (bf16[3,96,768]{2,1,0:T(8,128)(2,1)S(1)}, bf16[3,96,768]{2,1,0:T(8,128)(2,1)S(1)}, u32[]{:S(2)}, u32[]{:S(2)}) collective-permute-start(bf16[3,96,768]{2,1,0:T(8,128)(2,1)S(1)} %pad_maximum_fusion.5.refs_0_), channel_id=1, source_target_pairs={{0,4},{1,5},{2,6},{3,7},{4,0},{5,1},{6,2},{7,3},{8,12},{9,13},{10,... | collective-permute-start | bytes 1327112 | tf_op jit(solution)/shard_map/ppermute | solution.py:634
  70.5 12.3 %collective-permute-start.25 = (bf16[3,96,768]{2,1,0:T(8,128)(2,1)S(1)}, bf16[3,96,768]{2,1,0:T(8,128)(2,1)S(1)}, u32[]{:S(2)}, u32[]{:S(2)}) collective-permute-start(bf16[3,96,768]{2,1,0:T(8,128)(2,1)S(1)} %collective-permute-done.19.refs_1_), channel_id=1, source_target_pairs={{0,16},{1,17},{2,18},{3,19},{4,12},{5,13},{6,14},{7,15},{8,24},{9,... | collective-permute-start | bytes 1327112 | tf_op jit(solution)/shard_map/ppermute | solution.py:634
  71.8 11.5 %collective-permute-start.27 = (bf16[3,96,768]{2,1,0:T(8,128)(2,1)S(1)}, bf16[3,96,768]{2,1,0:T(8,128)(2,1)S(1)}, u32[]{:S(2)}, u32[]{:S(2)}) collective-permute-start(bf16[3,96,768]{2,1,0:T(8,128)(2,1)S(1)} %collective-permute-done.19.refs_1_), channel_id=1, source_target_pairs={{0,4},{1,5},{2,6},{3,7},{4,0},{5,1},{6,2},{7,3},{8,12},{9,13},{10,... | collective-permute-start | bytes 1327112 | tf_op jit(solution)/shard_map/ppermute | solution.py:634
  82.7 1.8 collective-permute-start.28
  82.7 2.4 %collective-permute-start.29 = (bf16[3,96,768]{2,1,0:T(8,128)(2,1)S(1)}, bf16[3,96,768]{2,1,0:T(8,128)(2,1)S(1)}, u32[]{:S(2)}, u32[]{:S(2)}) collective-permute-start(bf16[3,96,768]{2,1,0:T(8,128)(2,1)S(1)} %collective-permute-done.25.refs_3_), channel_id=1, source_target_pairs={{0,4},{1,5},{2,6},{3,7},{4,0},{5,1},{6,2},{7,3},{8,12},{9,13},{10,... | collective-permute-start | bytes 1327112 | tf_op jit(solution)/shard_map/ppermute | solution.py:634
  93.5 3.1 %collective-permute-start.30 = (bf16[2,2,2,96,768]{4,3,2,1,0:T(8,128)(2,1)S(1)}, bf16[2,2,2,96,768]{4,3,2,1,0:T(8,128)(2,1)S(1)}, u32[]{:S(2)}, u32[]{:S(2)}) collective-permute-start(bf16[2,2,2,96,768]{4,3,2,1,0:T(8,128)(2,1)S(1)} %get-tuple-element.176), channel_id=1, source_target_pairs={{0,4},{1,5},{2,6},{3,7},{4,0},{5,1},{6,2},{7,3},{8,12},{9,13},{10,... | collective-permute-start | bytes 3538952 | tf_op jit(solution)/shard_map/ppermute | solution.py:634
  96.7 2.8 %collective-permute-start.31 = (bf16[2,2,2,96,768]{4,3,2,1,0:T(8,128)(2,1)S(1)}, bf16[2,2,2,96,768]{4,3,2,1,0:T(8,128)(2,1)S(1)}, u32[]{:S(2)}, u32[]{:S(2)}) collective-permute-start(bf16[2,2,2,96,768]{4,3,2,1,0:T(8,128)(2,1)S(1)} %get-tuple-element.179), channel_id=1, source_target_pairs={{0,4},{1,5},{2,6},{3,7},{4,0},{5,1},{6,2},{7,3},{8,12},{9,13},{10,... | collective-permute-start | bytes 3538952 | tf_op jit(solution)/shard_map/ppermute | solution.py:634
  97.3 14.1 %collective-permute-start.32 = (bf16[2,2,96,768]{3,2,1,0:T(8,128)(2,1)S(1)}, bf16[2,2,96,768]{3,2,1,0:T(8,128)(2,1)S(1)}, u32[]{:S(2)}, u32[]{:S(2)}) collective-permute-start(bf16[2,2,96,768]{3,2,1,0:T(8,128)(2,1)S(1)} %get-tuple-element.270), channel_id=1, source_target_pairs={{0,8},{1,9},{2,10},{3,11},{4,20},{5,21},{6,22},{7,23},{8,0},{9,1},... | collective-permute-start | bytes 1769480 | tf_op jit(solution)/shard_map/ppermute | solution.py:634
  99.8 13.8 %collective-permute-start.33 = (bf16[2,2,96,768]{3,2,1,0:T(8,128)(2,1)S(1)}, bf16[2,2,96,768]{3,2,1,0:T(8,128)(2,1)S(1)}, u32[]{:S(2)}, u32[]{:S(2)}) collective-permute-start(bf16[2,2,96,768]{3,2,1,0:T(8,128)(2,1)S(1)} %get-tuple-element.272), channel_id=1, source_target_pairs={{0,8},{1,9},{2,10},{3,11},{4,20},{5,21},{6,22},{7,23},{8,0},{9,1},... | collective-permute-start | bytes 1769480 | tf_op jit(solution)/shard_map/ppermute | solution.py:634
  113.6 10.3 %collective-permute-start.34 = (bf16[2,2,4,96,768]{4,3,2,1,0:T(8,128)(2,1)S(1)}, bf16[2,2,4,96,768]{4,3,2,1,0:T(8,128)(2,1)S(1)}, u32[]{:S(2)}, u32[]{:S(2)}) collective-permute-start(bf16[2,2,4,96,768]{4,3,2,1,0:T(8,128)(2,1)S(1)} %get-tuple-element.192), channel_id=1, source_target_pairs={{0,4},{1,5},{2,6},{3,7},{4,0},{5,1},{6,2},{7,3},{8,12},{9,13},{10,... | collective-permute-start | bytes 7077896 | tf_op jit(solution)/shard_map/ppermute | solution.py:634
  114.0 9.9 %collective-permute-start.35 = (bf16[4,96,768]{2,1,0:T(8,128)(2,1)S(1)}, bf16[4,96,768]{2,1,0:T(8,128)(2,1)S(1)}, u32[]{:S(2)}, u32[]{:S(2)}) collective-permute-start(bf16[4,96,768]{2,1,0:T(8,128)(2,1)S(1)} %pad_maximum_fusion.2), channel_id=1, source_target_pairs={{0,16},{1,17},{2,18},{3,19},{4,12},{5,13},{6,14},{7,15},{8,24},{9,... | collective-permute-start | bytes 1769480 | tf_op jit(solution)/shard_map/ppermute | solution.py:634
  124.7 16.3 %collective-permute-start.36 = (bf16[2,4,96,768]{3,2,1,0:T(8,128)(2,1)S(1)}, bf16[2,4,96,768]{3,2,1,0:T(8,128)(2,1)S(1)}, u32[]{:S(2)}, u32[]{:S(2)}) collective-permute-start(bf16[2,4,96,768]{3,2,1,0:T(8,128)(2,1)S(1)} %get-tuple-element.264), channel_id=1, source_target_pairs={{0,8},{1,9},{2,10},{3,11},{4,20},{5,21},{6,22},{7,23},{8,0},{9,1},... | collective-permute-start | bytes 3538952 | tf_op jit(solution)/shard_map/ppermute | solution.py:634
  125.8 15.2 %collective-permute-start.37 = (bf16[2,2,2,96,768]{4,3,2,1,0:T(8,128)(2,1)S(1)}, bf16[2,2,2,96,768]{4,3,2,1,0:T(8,128)(2,1)S(1)}, u32[]{:S(2)}, u32[]{:S(2)}) collective-permute-start(bf16[2,2,2,96,768]{4,3,2,1,0:T(8,128)(2,1)S(1)} %get-tuple-element.204), channel_id=1, source_target_pairs={{0,4},{1,5},{2,6},{3,7},{4,0},{5,1},{6,2},{7,3},{8,12},{9,13},{10,... | collective-permute-start | bytes 3538952 | tf_op jit(solution)/shard_map/ppermute | solution.py:634
  126.0 10.5 %collective-permute-start.38 = (bf16[1,2,96,768]{3,2,1,0:T(8,128)(2,1)S(1)}, bf16[1,2,96,768]{3,2,1,0:T(8,128)(2,1)S(1)}, u32[]{:S(2)}, u32[]{:S(2)}) collective-permute-start(bf16[1,2,96,768]{3,2,1,0:T(8,128)(2,1)S(1)} %fusion.28), channel_id=1, source_target_pairs={{0,2},{1,3},{2,0},{3,1},{4,5},{5,4},{6,7},{7,6},{8,10},{9,11},{10,... | collective-permute-start | bytes 884744 | tf_op jit(solution)/shard_map/ppermute | solution.py:634
  140.9 10.1 %collective-permute-start.39 = (bf16[2,2,2,96,768]{4,3,2,1,0:T(8,128)(2,1)S(1)}, bf16[2,2,2,96,768]{4,3,2,1,0:T(8,128)(2,1)S(1)}, u32[]{:S(2)}, u32[]{:S(2)}) collective-permute-start(bf16[2,2,2,96,768]{4,3,2,1,0:T(8,128)(2,1)S(1)} %get-tuple-element.211), channel_id=1, source_target_pairs={{0,4},{1,5},{2,6},{3,7},{4,0},{5,1},{6,2},{7,3},{8,12},{9,13},{10,... | collective-permute-start | bytes 3538952 | tf_op jit(solution)/shard_map/ppermute | solution.py:634
  141.1 9.9 %collective-permute-start.40 = (bf16[4,96,768]{2,1,0:T(8,128)(2,1)S(1)}, bf16[4,96,768]{2,1,0:T(8,128)(2,1)S(1)}, u32[]{:S(2)}, u32[]{:S(2)}) collective-permute-start(bf16[4,96,768]{2,1,0:T(8,128)(2,1)S(1)} %fusion.7), channel_id=1, source_target_pairs={{0,16},{1,17},{2,18},{3,19},{4,12},{5,13},{6,14},{7,15},{8,24},{9,... | collective-permute-start | bytes 1769480 | tf_op jit(solution)/shard_map/ppermute | solution.py:634
  141.4 5.7 %collective-permute-start.41 = (bf16[1,96,768]{2,1,0:T(8,128)(2,1)S(1)}, bf16[1,96,768]{2,1,0:T(8,128)(2,1)S(1)}, u32[]{:S(2)}, u32[]{:S(2)}) collective-permute-start(bf16[1,96,768]{2,1,0:T(8,128)(2,1)S(1)} %slice_bitcast_fusion.24), channel_id=1, source_target_pairs={{0,1},{1,0},{2,3},{3,2},{4,6},{5,7},{6,4},{7,5},{8,9},{9,8},{10,11... | collective-permute-start | bytes 442376 | tf_op jit(solution)/shard_map/ppermute | solution.py:634
  142.2 4.4 %collective-permute-start.42 = (f32[16,768]{1,0:T(8,128)S(1)}, f32[16,768]{1,0:T(8,128)S(1)}, u32[]{:S(2)}, u32[]{:S(2)}) collective-permute-start(f32[16,768]{1,0:T(8,128)S(1)} %get-tuple-element.218), channel_id=1, source_target_pairs={{0,4},{1,5},{2,6},{3,7},{4,0},{5,1},{6,2},{7,3},{8,12},{9,13},{10,... | collective-permute-start | bytes 147464 | tf_op jit(solution)/shard_map/ppermute | solution.py:634
  151.4 13.5 %collective-permute-start.43 = (bf16[2,2,96,768]{3,2,1,0:T(8,128)(2,1)S(1)}, bf16[2,2,96,768]{3,2,1,0:T(8,128)(2,1)S(1)}, u32[]{:S(2)}, u32[]{:S(2)}) collective-permute-start(bf16[2,2,96,768]{3,2,1,0:T(8,128)(2,1)S(1)} %get-tuple-element.267), channel_id=1, source_target_pairs={{0,8},{1,9},{2,10},{3,11},{4,20},{5,21},{6,22},{7,23},{8,0},{9,1},... | collective-permute-start | bytes 1769480 | tf_op jit(solution)/shard_map/ppermute | solution.py:634
  152.8 15.0 %collective-permute-start.44 = (bf16[400,768]{1,0:T(8,128)(2,1)S(1)}, bf16[400,768]{1,0:T(8,128)(2,1)S(1)}, u32[]{:S(2)}, u32[]{:S(2)}) collective-permute-start(bf16[400,768]{1,0:T(8,128)(2,1)S(1)} %pad_maximum_fusion.1), channel_id=1, source_target_pairs={{0,8},{1,9},{2,10},{3,11},{4,20},{5,21},{6,22},{7,23},{8,0},{9,1},... | collective-permute-start | bytes 1843208 | tf_op jit(solution)/shard_map/ppermute | solution.py:634
  154.1 10.7 %collective-permute-start.45 = (bf16[1,2,96,768]{3,2,1,0:T(8,128)(2,1)S(1)}, bf16[1,2,96,768]{3,2,1,0:T(8,128)(2,1)S(1)}, u32[]{:S(2)}, u32[]{:S(2)}) collective-permute-start(bf16[1,2,96,768]{3,2,1,0:T(8,128)(2,1)S(1)} %fusion.26), channel_id=1, source_target_pairs={{0,2},{1,3},{2,0},{3,1},{4,5},{5,4},{6,7},{7,6},{8,10},{9,11},{10,... | collective-permute-start | bytes 884744 | tf_op jit(solution)/shard_map/ppermute | solution.py:634
  168.0 9.6 %collective-permute-start.46 = (bf16[2,96,768]{2,1,0:T(8,128)(2,1)S(1)}, bf16[2,96,768]{2,1,0:T(8,128)(2,1)S(1)}, u32[]{:S(2)}, u32[]{:S(2)}) collective-permute-start(bf16[2,96,768]{2,1,0:T(8,128)(2,1)S(1)} %fusion.24), channel_id=1, source_target_pairs={{0,16},{1,17},{2,18},{3,19},{4,12},{5,13},{6,14},{7,15},{8,24},{9,... | collective-permute-start | bytes 884744 | tf_op jit(solution)/shard_map/ppermute | solution.py:634
  168.3 6.7 %collective-permute-start.51 = (bf16[1,96,768]{2,1,0:T(8,128)(2,1)S(1)}, bf16[1,96,768]{2,1,0:T(8,128)(2,1)S(1)}, u32[]{:S(2)}, u32[]{:S(2)}) collective-permute-start(bf16[1,96,768]{2,1,0:T(8,128)(2,1)S(1)} %slice_bitcast_fusion.17), channel_id=1, source_target_pairs={{0,1},{1,0},{2,3},{3,2},{4,6},{5,7},{6,4},{7,5},{8,9},{9,8},{10,11... | collective-permute-start | bytes 442376 | tf_op jit(solution)/shard_map/ppermute | solution.py:634
  169.2 9.2 %collective-permute-start.47 = (bf16[208,768]{1,0:T(8,128)(2,1)S(1)}, bf16[208,768]{1,0:T(8,128)(2,1)S(1)}, u32[]{:S(2)}, u32[]{:S(2)}) collective-permute-start(bf16[208,768]{1,0:T(8,128)(2,1)S(1)} %pad_maximum_fusion.6), channel_id=1, source_target_pairs={{0,16},{1,17},{2,18},{3,19},{4,12},{5,13},{6,14},{7,15},{8,24},{9,... | collective-permute-start | bytes 958472 | tf_op jit(solution)/shard_map/ppermute | solution.py:634
  175.2 9.0 %collective-permute-start.52 = (bf16[2,96,768]{2,1,0:T(8,128)(2,1)S(1)}, bf16[2,96,768]{2,1,0:T(8,128)(2,1)S(1)}, u32[]{:S(2)}, u32[]{:S(2)}) collective-permute-start(bf16[2,96,768]{2,1,0:T(8,128)(2,1)S(1)} %get-tuple-element.278), channel_id=1, source_target_pairs={{0,8},{1,9},{2,10},{3,11},{4,12},{5,13},{6,14},{7,15},{8,0},{9,1},... | collective-permute-start | bytes 884744 | tf_op jit(solution)/shard_map/ppermute | solution.py:634
  176.5 8.0 %collective-permute-start.53 = (bf16[2,96,768]{2,1,0:T(8,128)(2,1)S(1)}, bf16[2,96,768]{2,1,0:T(8,128)(2,1)S(1)}, u32[]{:S(2)}, u32[]{:S(2)}) collective-permute-start(bf16[2,96,768]{2,1,0:T(8,128)(2,1)S(1)} %get-tuple-element.278), channel_id=1, source_target_pairs={{0,16},{1,17},{2,18},{3,19},{4,20},{5,21},{6,22},{7,23},{8,24},{9,... | collective-permute-start | bytes 884744 | tf_op jit(solution)/shard_map/ppermute | solution.py:634
  179.8 9.2 %collective-permute-start.48 = (bf16[112,768]{1,0:T(8,128)(2,1)S(1)}, bf16[112,768]{1,0:T(8,128)(2,1)S(1)}, u32[]{:S(2)}, u32[]{:S(2)}) collective-permute-start(bf16[112,768]{1,0:T(8,128)(2,1)S(1)} %get-tuple-element.286), channel_id=1, source_target_pairs={{0,3},{1,2},{2,1},{3,0},{4,7},{5,6},{6,5},{7,4},{8,11},{9,10},{10,... | collective-permute-start | bytes 516104 | tf_op jit(solution)/shard_map/ppermute | solution.py:634
  182.8 12.0 %collective-permute-start.49 = (bf16[112,768]{1,0:T(8,128)(2,1)S(1)}, bf16[112,768]{1,0:T(8,128)(2,1)S(1)}, u32[]{:S(2)}, u32[]{:S(2)}) collective-permute-start(bf16[112,768]{1,0:T(8,128)(2,1)S(1)} %get-tuple-element.285), channel_id=1, source_target_pairs={{0,2},{1,3},{2,0},{3,1},{4,6},{5,7},{6,4},{7,5},{8,10},{9,11},{10,... | collective-permute-start | bytes 516104 | tf_op jit(solution)/shard_map/ppermute | solution.py:634
  182.8 12.0 %collective-permute-start.50 = (bf16[112,768]{1,0:T(8,128)(2,1)S(1)}, bf16[112,768]{1,0:T(8,128)(2,1)S(1)}, u32[]{:S(2)}, u32[]{:S(2)}) collective-permute-start(bf16[112,768]{1,0:T(8,128)(2,1)S(1)} %get-tuple-element.284), channel_id=1, source_target_pairs={{0,1},{1,0},{2,3},{3,2},{4,5},{5,4},{6,7},{7,6},{8,9},{9,8},{10,11... | collective-permute-start | bytes 516104 | tf_op jit(solution)/shard_map/ppermute | solution.py:634
  195.7 8.7 %collective-permute-start.57 = (bf16[3,2,96,768]{3,2,1,0:T(8,128)(2,1)S(1)}, bf16[3,2,96,768]{3,2,1,0:T(8,128)(2,1)S(1)}, u32[]{:S(2)}, u32[]{:S(2)}) collective-permute-start(bf16[3,2,96,768]{3,2,1,0:T(8,128)(2,1)S(1)} %pad_maximum_fusion.held), channel_id=1, source_target_pairs={{0,4},{1,5},{2,6},{3,7},{4,0},{5,1},{6,2},{7,3},{8,12},{9,13},{10,... | collective-permute-start | bytes 2654216 | tf_op jit(solution)/shard_map/ppermute | solution.py:634
  195.8 8.6 %collective-permute-start.62 = (bf16[2,96,768]{2,1,0:T(8,128)(2,1)S(1)}, bf16[2,96,768]{2,1,0:T(8,128)(2,1)S(1)}, u32[]{:S(2)}, u32[]{:S(2)}) collective-permute-start(bf16[2,96,768]{2,1,0:T(8,128)(2,1)S(1)} %broadcast_select_fusion), channel_id=1, source_target_pairs={{0,8},{1,9},{2,10},{3,11},{4,20},{5,21},{6,22},{7,23},{8,0},{9,1},... | collective-permute-start | bytes 884744 | tf_op jit(solution)/shard_map/ppermute | solution.py:634
  198.3 9.6 %collective-permute-start.54 = (bf16[96,768]{1,0:T(8,128)(2,1)S(1)}, bf16[96,768]{1,0:T(8,128)(2,1)S(1)}, u32[]{:S(2)}, u32[]{:S(2)}) collective-permute-start(bf16[96,768]{1,0:T(8,128)(2,1)S(1)} %fusion.33.refs_0_), channel_id=1, source_target_pairs={{0,8},{1,9},{2,10},{3,11},{4,12},{5,13},{6,14},{7,15},{8,0},{9,1},... | collective-permute-start | bytes 442376 | tf_op jit(solution)/shard_map/ppermute | solution.py:634
  199.0 8.9 %collective-permute-start.55 = (bf16[96,768]{1,0:T(8,128)(2,1)S(1)}, bf16[96,768]{1,0:T(8,128)(2,1)S(1)}, u32[]{:S(2)}, u32[]{:S(2)}) collective-permute-start(bf16[96,768]{1,0:T(8,128)(2,1)S(1)} %fusion.33.refs_0_), channel_id=1, source_target_pairs={{0,16},{1,17},{2,18},{3,19},{4,20},{5,21},{6,22},{7,23},{8,24},{9,... | collective-permute-start | bytes 442376 | tf_op jit(solution)/shard_map/ppermute | solution.py:634
  200.0 9.3 %collective-permute-start.56 = (bf16[96,768]{1,0:T(8,128)(2,1)S(1)}, bf16[96,768]{1,0:T(8,128)(2,1)S(1)}, u32[]{:S(2)}, u32[]{:S(2)}) collective-permute-start(bf16[96,768]{1,0:T(8,128)(2,1)S(1)} %fusion.33.refs_0_), channel_id=1, source_target_pairs={{0,24},{1,25},{2,26},{3,27},{4,28},{5,29},{6,30},{7,31},{8,16},{9,... | collective-permute-start | bytes 442376 | tf_op jit(solution)/shard_map/ppermute | solution.py:634
  204.4 8.2 %collective-permute-start.58 = (bf16[96,768]{1,0:T(8,128)(2,1)S(1)}, bf16[96,768]{1,0:T(8,128)(2,1)S(1)}, u32[]{:S(2)}, u32[]{:S(2)}) collective-permute-start(bf16[96,768]{1,0:T(8,128)(2,1)S(1)} %fusion.33.refs_0_), channel_id=1, source_target_pairs={{0,4},{1,5},{2,6},{3,7},{4,0},{5,1},{6,2},{7,3},{8,12},{9,13},{10,... | collective-permute-start | bytes 442376 | tf_op jit(solution)/shard_map/ppermute | solution.py:634
  204.4 6.0 %collective-permute-start.63 = (bf16[2,96,768]{2,1,0:T(8,128)(2,1)S(1)}, bf16[2,96,768]{2,1,0:T(8,128)(2,1)S(1)}, u32[]{:S(2)}, u32[]{:S(2)}) collective-permute-start(bf16[2,96,768]{2,1,0:T(8,128)(2,1)S(1)} %collective-permute-done.62.corner), channel_id=1, source_target_pairs={{0,4},{1,5},{2,6},{3,7},{4,0},{5,1},{6,2},{7,3},{8,12},{9,13},{10,... | collective-permute-start | bytes 884744 | tf_op jit(solution)/shard_map/ppermute | solution.py:634
  209.3 3.3 %collective-permute-start.59 = (bf16[96,768]{1,0:T(8,128)(2,1)S(1)}, bf16[96,768]{1,0:T(8,128)(2,1)S(1)}, u32[]{:S(2)}, u32[]{:S(2)}) collective-permute-start(bf16[96,768]{1,0:T(8,128)(2,1)S(1)} %collective-permute-done.54.refs_1_), channel_id=1, source_target_pairs={{0,4},{1,5},{2,6},{3,7},{4,0},{5,1},{6,2},{7,3},{8,12},{9,13},{10,... | collective-permute-start | bytes 442376 | tf_op jit(solution)/shard_map/ppermute | solution.py:634
  209.3 3.3 %collective-permute-start.60 = (bf16[96,768]{1,0:T(8,128)(2,1)S(1)}, bf16[96,768]{1,0:T(8,128)(2,1)S(1)}, u32[]{:S(2)}, u32[]{:S(2)}) collective-permute-start(bf16[96,768]{1,0:T(8,128)(2,1)S(1)} %collective-permute-done.55.refs_2_), channel_id=1, source_target_pairs={{0,4},{1,5},{2,6},{3,7},{4,0},{5,1},{6,2},{7,3},{8,12},{9,13},{10,... | collective-permute-start | bytes 442376 | tf_op jit(solution)/shard_map/ppermute | solution.py:634
  209.8 2.8 %collective-permute-start.61 = (bf16[96,768]{1,0:T(8,128)(2,1)S(1)}, bf16[96,768]{1,0:T(8,128)(2,1)S(1)}, u32[]{:S(2)}, u32[]{:S(2)}) collective-permute-start(bf16[96,768]{1,0:T(8,128)(2,1)S(1)} %collective-permute-done.56.refs_3_), channel_id=1, source_target_pairs={{0,4},{1,5},{2,6},{3,7},{4,0},{5,1},{6,2},{7,3},{8,12},{9,13},{10,... | collective-permute-start | bytes 442376 | tf_op jit(solution)/shard_map/ppermute | solution.py:634
  (29 other events, 271.5 us)
